TPU v7x, 32 devices: a whole 2x2x4 slice. The times are simulated.
32 devices in a mesh: fields: 8 (over y, x, core), blk: 4 (over z).
Axes of the slice: x: 2, y: 2, z: 4, core: 2. Of those that a mesh axis runs over, the one named last changes fastest.
Arguments:
- tokens: bfloat16 [32, 1024, 768], P('fields', 'blk'), may hold values from -6 to 6
- keep_index: int32 [32, 1024], P('fields', 'blk'), may hold values from 0 to 2047, as said below
- counts: int32 [32], P('fields'), may hold values from 205 to 1024, as said below
- norm1_gain: bfloat16 [768], replicated, may hold values from 0.099609375 to 1.8984375
- norm1_bias: bfloat16 [768], replicated, may hold values from -1.75 to 1.75
- qkv_weight: bfloat16 [768, 2304], replicated, may hold values from -0.21875 to 0.21875
- query_bias: bfloat16 [768], replicated, may hold values from -1.75 to 1.75
- value_bias: bfloat16 [768], replicated, may hold values from -1.75 to 1.75
- out_weight: bfloat16 [768, 768], replicated, may hold values from -0.875 to 0.875
- out_bias: bfloat16 [768], replicated, may hold values from -1.75 to 1.75
- norm2_gain: bfloat16 [768], replicated, may hold values from 0.099609375 to 1.8984375
- norm2_bias: bfloat16 [768], replicated, may hold values from -1.75 to 1.75
- up_weight: bfloat16 [768, 3072], replicated, may hold values from -0.21875 to 0.21875
- up_bias: bfloat16 [3072], replicated, may hold values from -1.75 to 1.75
- down_weight: bfloat16 [3072, 768], replicated, may hold values from -0.109375 to 0.109375
- down_bias: bfloat16 [768], replicated, may hold values from -1.75 to 1.75
- cotangent: bfloat16 [32, 1024, 768], P('fields', 'blk'), may hold values from -6 to 6
Outputs:
- output: bfloat16 [32, 1024, 768], P('fields', 'blk')
- input_grad: bfloat16 [32, 1024, 768], P('fields', 'blk')
- norm1_gain_grad: float32 [768], replicated
- norm1_bias_grad: float32 [768], replicated
- qkv_weight_grad: float32 [768, 2304], replicated
- query_bias_grad: float32 [768], replicated
- value_bias_grad: float32 [768], replicated
- out_weight_grad: float32 [768, 768], replicated
- out_bias_grad: float32 [768], replicated
- norm2_gain_grad: float32 [768], replicated
- norm2_bias_grad: float32 [768], replicated
- up_weight_grad: float32 [768, 3072], replicated
- up_bias_grad: float32 [3072], replicated
- down_weight_grad: float32 [3072, 768], replicated
- down_bias_grad: float32 [768], replicated
Inputs may be any that keep to these rules, and one draw needn't show every extreme that they name: `keep_index`: within a field the slots carry distinct patch numbers below 2048. `counts`: each field keeps ceil(2048 (100 - m) / 100) patches for an integer mask percentage m of 50 to 90; key slots at or past it are padding.
All inputs are finite; a program needn't handle non-finite values.
Results may differ from a plain program's by a relative error of at most 0.025.
Values may be sent and summed in bfloat16 or wider, within the bound.
A program may use at most 320 MiB of HBM per device.

v0:
```python
from functools import partial

import jax
import jax.numpy as jnp
from jax import lax
from jax.sharding import PartitionSpec as P

HEAD_DIM = 64
GRID_W = 64


epsilon = 1e-06
negative = -1e30


def positional(keep, width):
    row_pos = (keep // GRID_W).astype(jnp.float32)
    col_pos = (keep % GRID_W).astype(jnp.float32)
    quarter = width // 4
    omega = 1.0 / 10000.0 ** (jnp.arange(quarter).astype(jnp.float32) / quarter)
    row_ang = row_pos[..., None] * omega
    col_ang = col_pos[..., None] * omega
    return jnp.concatenate(
        [jnp.sin(row_ang), jnp.cos(row_ang), jnp.sin(col_ang), jnp.cos(col_ang)], -1
    )


def layer_norm(values, gain, bias):
    centre = jnp.mean(values, -1, keepdims=True)
    centred = values - centre
    spread = jnp.mean(centred * centred, -1, keepdims=True)
    return centred * lax.rsqrt(spread + epsilon) * gain + bias


def outer_sum(left, right):
    return lax.dot_general(
        left, right, (((0,), (0,)), ((), ())), preferred_element_type=jnp.float32
    )


def back_mul(grad, weight):
    return lax.dot_general(
        grad, weight, (((1,), (1,)), ((), ())), preferred_element_type=jnp.float32
    )


def split_pair(kv_all, width):
    pair, slots = (kv_all.shape[0], kv_all.shape[1])
    keys = kv_all[..., :width].reshape(pair, slots, width // HEAD_DIM, HEAD_DIM)
    values = kv_all[..., width:].reshape(pair, slots, width // HEAD_DIM, HEAD_DIM)
    return (keys, values)


def pair_scores(query, keys, count):
    scores = jnp.einsum(
        "fqhd,fkhd->fhqk", query, keys, preferred_element_type=jnp.float32
    ) * HEAD_DIM ** (-0.5)
    visible = jnp.arange(keys.shape[1])[None, :] < count[:, None]
    return jnp.where(visible[:, None, None, :], scores, negative)


def attend_pair(query, kv_all, count):
    width = kv_all.shape[2] // 2
    keys, values = split_pair(kv_all, width)
    scores = pair_scores(query, keys, count)
    top = jnp.max(scores, -1, keepdims=True)
    expo = jnp.exp(scores - top)
    total = jnp.sum(expo, -1, keepdims=True)
    probs = (expo / total).astype(jnp.bfloat16)
    mixed = jnp.einsum("fhqk,fkhd->fqhd", probs, values, preferred_element_type=jnp.float32)
    mixed = mixed.reshape(query.shape[0], query.shape[1], width).astype(jnp.bfloat16)
    return (mixed, top + jnp.log(total))


def attend_back(query, kv_all, count, log_total, grad_mixed):
    width = kv_all.shape[2] // 2
    keys, values = split_pair(kv_all, width)
    scores = pair_scores(query, keys, count)
    probs = jnp.exp(scores - log_total)
    grad_heads = grad_mixed.reshape(query.shape)
    grad_probs = jnp.einsum(
        "fqhd,fkhd->fhqk", grad_heads, values, preferred_element_type=jnp.float32
    )
    centre = jnp.sum(probs * grad_probs, -1, keepdims=True)
    grad_scores = (probs * (grad_probs - centre)).astype(jnp.bfloat16)
    scale = HEAD_DIM ** (-0.5)
    grad_query = (
        jnp.einsum("fhqk,fkhd->fqhd", grad_scores, keys, preferred_element_type=jnp.float32) * scale
    )
    grad_keys = (
        jnp.einsum("fhqk,fqhd->fkhd", grad_scores, query, preferred_element_type=jnp.float32)
        * scale
    )
    grad_values = jnp.einsum(
        "fhqk,fqhd->fkhd",
        probs.astype(jnp.bfloat16),
        grad_heads,
        preferred_element_type=jnp.float32,
    )
    pair, slots = (kv_all.shape[0], kv_all.shape[1])
    grad_query = grad_query.reshape(query.shape[0], query.shape[1], width).astype(jnp.bfloat16)
    key_terms = jnp.concatenate(
        [grad_keys.reshape(pair, slots, width), grad_values.reshape(pair, slots, width)], -1
    )
    return (grad_query, key_terms, centre)


def per_device(
    tokens,
    keep_index,
    counts,
    norm1_gain,
    norm1_bias,
    qkv_weight,
    query_bias,
    value_bias,
    out_weight,
    out_bias,
    norm2_gain,
    norm2_bias,
    up_weight,
    up_bias,
    down_weight,
    down_bias,
    cotangent,
):
    fields_here, slots_here, width = tokens.shape
    rows = fields_here * slots_here
    heads = width // HEAD_DIM
    pairs = fields_here // 2
    gain_one = norm1_gain.astype(jnp.float32)
    bias_one = norm1_bias.astype(jnp.float32)
    gain_two = norm2_gain.astype(jnp.float32)
    bias_two = norm2_bias.astype(jnp.float32)
    x_zero = (tokens.astype(jnp.float32) + positional(keep_index, width)).reshape(rows, width)
    normed_one, norm_one_pull = jax.vjp(layer_norm, x_zero, gain_one, bias_one)
    a_one = normed_one.astype(jnp.bfloat16)
    qkv = jnp.dot(a_one, qkv_weight, preferred_element_type=jnp.float32)
    query = (qkv[:, :width] + query_bias.astype(jnp.float32)).astype(jnp.bfloat16)
    keys = qkv[:, width : 2 * width].astype(jnp.bfloat16)
    values = (qkv[:, 2 * width :] + value_bias.astype(jnp.float32)).astype(jnp.bfloat16)
    kv_local = jnp.concatenate([keys, values], -1).reshape(fields_here, slots_here, 2 * width)
    kv_all = lax.all_gather(kv_local, "blk", axis=1, tiled=True)
    slots = kv_all.shape[1]
    query_pairs = query.reshape(pairs, 2, slots_here, heads, HEAD_DIM)
    kv_pairs = kv_all.reshape(pairs, 2, slots, 2 * width)
    count_pairs = counts.reshape(pairs, 2)
    mixed, log_total = lax.map(
        lambda item: attend_pair(item[0], item[1], item[2]), (query_pairs, kv_pairs, count_pairs)
    )
    attn_out = mixed.reshape(rows, width)
    branch = jnp.dot(attn_out, out_weight, preferred_element_type=jnp.float32) + out_bias.astype(
        jnp.float32
    )
    x_one = x_zero + branch
    normed_two, norm_two_pull = jax.vjp(layer_norm, x_one, gain_two, bias_two)
    a_two = normed_two.astype(jnp.bfloat16)
    hidden = jnp.dot(a_two, up_weight, preferred_element_type=jnp.float32) + up_bias.astype(
        jnp.float32
    )
    gelu_val, gelu_pull = jax.vjp(partial(jax.nn.gelu, approximate=False), hidden)
    gelu_out = gelu_val.astype(jnp.bfloat16)
    result = (
        x_one
        + jnp.dot(gelu_out, down_weight, preferred_element_type=jnp.float32)
        + down_bias.astype(jnp.float32)
    )
    output = result.reshape(fields_here, slots_here, width).astype(jnp.bfloat16)
    grad_out = cotangent.reshape(rows, width)
    grad_float = grad_out.astype(jnp.float32)
    down_grad = outer_sum(gelu_out, grad_out)
    down_bias_grad = jnp.sum(grad_float, 0)
    grad_gelu = back_mul(grad_out, down_weight)
    grad_hidden = gelu_pull(grad_gelu)[0].astype(jnp.bfloat16)
    up_grad = outer_sum(a_two, grad_hidden)
    up_bias_grad = jnp.sum(grad_hidden.astype(jnp.float32), 0)
    grad_norm_two = back_mul(grad_hidden, up_weight)
    grad_x_two, gain_two_grad, bias_two_grad = norm_two_pull(grad_norm_two)
    grad_x_one = grad_float + grad_x_two
    grad_branch = grad_x_one.astype(jnp.bfloat16)
    out_grad = outer_sum(attn_out, grad_branch)
    out_bias_grad = jnp.sum(grad_branch.astype(jnp.float32), 0)
    grad_attn = back_mul(grad_branch, out_weight).astype(jnp.bfloat16)
    grad_pairs = grad_attn.reshape(pairs, 2, slots_here, width)
    grad_query, key_terms, centre = lax.map(
        lambda item: attend_back(item[0], item[1], item[2], item[3], item[4]),
        (query_pairs, kv_pairs, count_pairs, log_total, grad_pairs),
    )
    key_terms = key_terms.reshape(fields_here, slots, 2 * width)
    grad_kv = lax.psum_scatter(
        key_terms.astype(jnp.bfloat16), "blk", scatter_dimension=1, tiled=True
    )
    grad_kv = grad_kv.reshape(rows, 2 * width)
    grad_query = grad_query.reshape(rows, width)
    grad_qkv = jnp.concatenate([grad_query, grad_kv], -1)
    qkv_grad = outer_sum(a_one, grad_qkv)
    query_bias_grad = jnp.sum(grad_query.astype(jnp.float32), 0)
    value_bias_grad = jnp.sum(grad_kv[:, width:].astype(jnp.float32), 0)
    grad_norm_one = back_mul(grad_qkv, qkv_weight)
    grad_x_zero, gain_one_grad, bias_one_grad = norm_one_pull(grad_norm_one)
    input_grad = (
        (grad_x_one + grad_x_zero).reshape(fields_here, slots_here, width).astype(jnp.bfloat16)
    )
    summed = lax.psum(
        (
            gain_one_grad,
            bias_one_grad,
            qkv_grad,
            query_bias_grad,
            value_bias_grad,
            out_grad,
            out_bias_grad,
            gain_two_grad,
            bias_two_grad,
            up_grad,
            up_bias_grad,
            down_grad,
            down_bias_grad,
        ),
        ("fields", "blk"),
    )
    return (
        output,
        input_grad,
        summed[0],
        summed[1],
        summed[2],
        summed[3],
        summed[4],
        summed[5],
        summed[6],
        summed[7],
        summed[8],
        summed[9],
        summed[10],
        summed[11],
        summed[12],
    )


def solution(mesh):
    return jax.shard_map(
        per_device,
        mesh=mesh,
        in_specs=(
            P("fields", "blk", None),
            P("fields", "blk"),
            P("fields"),
            P(),
            P(),
            P(),
            P(),
            P(),
            P(),
            P(),
            P(),
            P(),
            P(),
            P(),
            P(),
            P(),
            P("fields", "blk", None),
        ),
        out_specs=(
            P("fields", "blk", None),
            P("fields", "blk", None),
            P(),
            P(),
            P(),
            P(),
            P(),
            P(),
            P(),
            P(),
            P(),
            P(),
            P(),
            P(),
            P(),
        ),
        check_vma=False,
    )
```

profile of v0, /device:TPU:0, one launch (start us, length us, event | category | flops | bytes accessed | tf_op | source)
XLA Modules:
  0.0 1328.0 jit_solution(18398175500937142640)
XLA Ops:
  9.7 7.3 multiply_sine_fusion.1
  20.2 4.1 fusion.54
  32.0 3.8 reshape.279
  40.5 208.6 %all-gather.2.cloned.1.call-done = bf16[4,1024,1536]{2,1,0:T(8,128)(2,1)} async-done(((bf16[4,256,1536]{2,1,0:T(8,128)(2,1)}), bf16[4,1024,1536]{2,1,0:T(8,128)(2,1)}) %all-gather.2.cloned.1.call-update) | async-done | bytes 12582928 | tf_op jit(solution)/shard_map/all_gather | solution.py:143
  249.1 16.7 %copy.36 = bf16[4,1024,1536]{1,2,0:T(8,128)(2,1)} copy(bf16[4,1024,1536]{2,1,0:T(8,128)(2,1)} %all-gather.2.cloned.1.call-done) | data formatting | bytes 25165824 | tf_op jit(solution)/shard_map/all_gather | solution.py:143
  265.8 88.3 %while.24 = (s32[]{:T(128)}, bf16[2,2,256,768]{3,2,1,0:T(8,128)(2,1)}, f32[2,2,12,256,1]{3,2,1,4,0:T(8,128)}, bf16[2,2,1024,1536]{2,3,1,0:T(8,128)(2,1)}, s32[2,...) while((s32[]{:T(128)}, bf16[2,2,256,768]{3,2,1,0:T(8,128)(2,1)}, ...), condition=%wide.region_5.6_spmd, body=%wide.region_2.5_spmd.sunk | while | flops 1686499328 | bytes 118393040 | solution.py:148
  265.8 3.5 dynamic-slice_bitcast_fusion.6
  270.7 10.2 fusion.112
  280.9 11.2 fusion.113
  292.1 12.1 fusion.114
  309.9 3.5 dynamic-slice_bitcast_fusion.6
  314.9 10.2 fusion.112
  325.0 11.2 fusion.113
  336.3 12.1 fusion.114
  354.1 4.4 fusion.53
  359.1 44.6 %multiply_convert_fusion.2 = (bf16[1024,3072]{1,0:T(8,128)(2,1)}, f32[1024,3072]{1,0:T(8,128)}, f32[1024,3072]{1,0:T(8,128)}) fusion(f32[3072]{0:T(1024)S(1)} %copy-done.45, bf16[768,3072]{1,0:T(8,128)(2,1)S(1)} %copy-done.54, f32[1024,768]{1,0:T(8,128)S(1)} %get-tuple-element.201, f32[768]{0:T(1024)S(1)} %copy-done.33, f32[768]{0:T(1024)S(1)} %copy-done.31, ...), kind=kOutput, calls=%fused_computation.49 | convolution fusion | flops 5043388416 | bytes 39348224 | tf_op jit(solution)/shard_map/dot_general | solution.py:158
  403.7 18.7 %convert_reduce_fusion = (f32[3072]{0:T(1024)}, bf16[1024,3072]{1,0:T(8,128)(2,1)}) fusion(f32[1024,3072]{1,0:T(8,128)} %get-tuple-element.177, bf16[1024,768]{1,0:T(8,128)(2,1)} %bitcast.176, bf16[3072,768]{1,0:T(8,128)(2,1)} %param.35, f32[1024,3072]{1,0:T(8,128)} %get-tuple-element.202, f32[3072]{0:T(1024)S(1)} %copy-done.45), kind=kOutput, calls=%fused_computation.47 | convolution fusion | flops 4885312512 | bytes 37773312 | tf_op jit(solution)/shard_map/dot_general | solution.py:42
  422.4 9.8 multiply_reduce_fusion.1
  438.5 190.6 %while.25 = (s32[]{:T(128)}, bf16[2,2,256,768]{2,3,1,0:T(8,128)(2,1)}, bf16[2,2,1024,1536]{2,3,1,0:T(8,128)(2,1)}, bf16[2,2,1024,1536]{2,3,1,0:T(8,128)(2,1)}, s...) while((s32[]{:T(128)}, ...), condition=%wide.region_12.13_spmd, body=%wide.region_10.12_spmd.sunk | while | flops 4137414656 | bytes 339427776 | solution.py:185
  438.9 3.5 dynamic-slice_bitcast_fusion.7
  444.9 10.1 fusion.126
  459.0 19.2 %multiply_reduce_fusion.8 = (f32[2,12,256]{2,1,0:T(8,128)}, f32[2,12,256,1024]{3,2,1,0:T(8,128)}) fusion(f32[2,12,256,1024]{3,2,1,0:T(8,128)} %fusion.126, f32[2,12,256]{2,1,0:T(8,128)} %dynamic-slice_bitcast_fusion.8, pred[2,1024]{1,0:T(4,128)(4,1)S(1)} %iota_compare_fusion.5, bf16[2,256,12,64]{1,3,2,0:T(8,128)(2,1)} %bitcast.172, ...), kind=kOutput, calls=%fused_computation.20.clone.1 | convolution fusion | flops 836757504 | bytes 54315008 | tf_op jit(solution)/shard_map/while/body/eval_jaxpr/fqhd,fkhd->fhqk/dot_general | solution.py:81
  478.2 21.7 %multiply_convert_fusion.5 = bf16[2,12,256,1024]{3,2,1,0:T(8,128)(2,1)} fusion(f32[2,12,256,1024]{3,2,1,0:T(8,128)} %get-tuple-element.307, f32[2,12,256,1024]{3,2,1,0:T(8,128)} %fusion.126, f32[2,12,256]{2,1,0:T(8,128)} %get-tuple-element.308, f32[2,12,256]{2,1,0:T(8,128)} %dynamic-slice_bitcast_fusion.8, pred[2,1024]{1,0:T(4,128)(4,1)S(1)} %iota_compare_fusion.5), kind=kLoop, calls=%fused_computation.19.clone.1 | loop fusion | flops 37748736 | bytes 62965760 | tf_op jit(solution)/shard_map/while/body/eval_jaxpr/convert_element_type | solution.py:85
  499.9 8.6 multiply_convert_fusion.6
  509.8 12.8 fusion.128
  522.6 5.1 broadcast_multiply_fusion.4
  527.7 6.2 fusion.129
  539.9 10.1 fusion.126
  554.0 19.2 %multiply_reduce_fusion.8 = (f32[2,12,256]{2,1,0:T(8,128)}, f32[2,12,256,1024]{3,2,1,0:T(8,128)}) fusion(f32[2,12,256,1024]{3,2,1,0:T(8,128)} %fusion.126, f32[2,12,256]{2,1,0:T(8,128)} %dynamic-slice_bitcast_fusion.8, pred[2,1024]{1,0:T(4,128)(4,1)S(1)} %iota_compare_fusion.5, bf16[2,256,12,64]{1,3,2,0:T(8,128)(2,1)} %bitcast.172, ...), kind=kOutput, calls=%fused_computation.20.clone.1 | convolution fusion | flops 836757504 | bytes 54315008 | tf_op jit(solution)/shard_map/while/body/eval_jaxpr/fqhd,fkhd->fhqk/dot_general | solution.py:81
  573.2 21.7 %multiply_convert_fusion.5 = bf16[2,12,256,1024]{3,2,1,0:T(8,128)(2,1)} fusion(f32[2,12,256,1024]{3,2,1,0:T(8,128)} %get-tuple-element.307, f32[2,12,256,1024]{3,2,1,0:T(8,128)} %fusion.126, f32[2,12,256]{2,1,0:T(8,128)} %get-tuple-element.308, f32[2,12,256]{2,1,0:T(8,128)} %dynamic-slice_bitcast_fusion.8, pred[2,1024]{1,0:T(4,128)(4,1)S(1)} %iota_compare_fusion.5), kind=kLoop, calls=%fused_computation.19.clone.1 | loop fusion | flops 37748736 | bytes 62965760 | tf_op jit(solution)/shard_map/while/body/eval_jaxpr/convert_element_type | solution.py:85
  594.9 8.6 multiply_convert_fusion.6
  604.8 12.8 fusion.128
  617.6 5.1 broadcast_multiply_fusion.4
  622.7 6.2 fusion.129
  629.1 16.7 %copy.43 = bf16[2,2,1024,1536]{3,2,1,0:T(8,128)(2,1)} copy(bf16[2,2,1024,1536]{2,3,1,0:T(8,128)(2,1)} %get-tuple-element.94) | data formatting | bytes 25165824 | tf_op jit(solution)/shard_map/convert_element_type | solution.py:191
  648.5 5.4 fusion.55
  654.0 10.9 fusion.44
  664.8 7.7 fusion.56
  672.6 183.4 %reduce-scatter.2.cloned.1.call-done = bf16[4,256,1536]{2,1,0:T(8,128)(2,1)} async-done(((bf16[4,1024,1536]{2,1,0:T(8,128)(2,1)}), bf16[4,256,1536]{2,1,0:T(8,128)(2,1)}) %reduce-scatter.2.cloned.1.call-update) | async-done | bytes 3145744 | tf_op jit(solution)/shard_map/reduce_scatter | solution.py:190
  856.0 9.7 fusion.34
  870.9 11.5 add_convert_fusion.2
  883.4 6.4 multiply_reduce_fusion.2
  889.8 44.4 %all-reduce = (f32[768]{0:T(1024)}, f32[768]{0:T(1024)}, f32[768]{0:T(1024)}, f32[768]{0:T(1024)}, f32[768]{0:T(1024)}, /*index=5*/f32[768]{0:T(1024)}, f32[768]{0:T(1024)}, f32[3072]{0:T(1024)}, f32[768]{0:T(1024)}) all-reduce(f32[768]{0:T(1024)} %get-tuple-element.125, ...), channel_id=1, replica_groups=mesh['fields'=8,'blk'=4] {'fields','blk'}, use_global_device_ids=true, to_apply=%region_17.18 | all-reduce | flops 9216 | bytes 73728 | tf_op jit(solution)/shard_map/psum | solution.py:204
  934.9 3.8 fusion.47
  941.3 358.8 %all-reduce.4.cloned.1.call-done = (f32[768,2304]{1,0:T(8,128)}, f32[768,768]{1,0:T(8,128)}, f32[768,3072]{1,0:T(8,128)}, f32[3072,768]{1,0:T(8,128)}) async-done(((f32[768,2304]{1,0:T(8,128)}, f32[768,768]{1,0:T(8,128)}, f32[768,3072]{1,0:T(8,128)}, f32[3072,768]{1,0:T(8,128)}), (f32[768,2304]{1,0:T(8,128)}, f32[768,768]{1,0:T(8,128)}, f32[768,3072]{1,0:T(8,128)}, ...) | async-done | bytes 28311568 | tf_op jit(solution)/shard_map/psum | solution.py:204
  1300.2 6.6 copy.81
  1308.1 9.3 copy.83
  1317.5 3.7 copy.84
  (244 shorter events, 71.1 us)
Async XLA Ops:
  7.2 13.0 copy-start
  7.2 241.9 %all-gather.2.cloned.1.call-start = ((), (), s32[]{:S(2)}) async-start(), calls=%async_computation.1 | async-start | bytes 15728640 | tf_op jit(solution)/shard_map/all_gather | solution.py:143
  7.2 9.8 copy-start.24
  9.6 9.0 copy-start.35
  28.0 828.0 %reduce-scatter.2.cloned.1.call-start = ((), (), s32[]{:S(2)}) async-start(), calls=%async_computation.2 | async-start | bytes 15728640 | tf_op jit(solution)/shard_map/reduce_scatter | solution.py:190
  29.4 9.3 copy-start.46
  29.4 9.9 copy-start.51
  29.4 10.5 copy-start.52
  40.5 225.3 %copy-start.57 = (s32[2,2]{1,0:T(2,128)S(1)}, s32[2,2]{1,0:T(2,128)}, u32[]{:S(2)}) copy-start(s32[2,2]{1,0:T(2,128)} %reshape.278) | copy-start | bytes 52
  265.8 88.4 %copy-start.47 = (f32[768]{0:T(1024)S(1)}, f32[768]{0:T(1024)}, u32[]{:S(2)}) copy-start(f32[768]{0:T(1024)} %convert_element_type.159) | copy-start | bytes 9220
  280.9 11.2 copy-start.15
  292.1 12.1 copy-start.19
  325.0 11.2 copy-start.15
  336.3 12.1 copy-start.19
  358.5 73.7 %copy-start.7 = (f32[1024,768]{1,0:T(8,128)}, f32[1024,768]{1,0:T(8,128)S(1)}, u32[]{:S(2)}) copy-start(f32[1024,768]{1,0:T(8,128)S(1)} %get-tuple-element.201) | copy-start | bytes 9437188
  358.5 73.7 %copy-start.27 = (f32[1024]{0:T(1024)}, f32[1024]{0:T(1024)S(1)}, u32[]{:S(2)}) copy-start(f32[1024]{0:T(1024)S(1)} %broadcast_multiply_fusion.1) | copy-start | bytes 12292
  359.1 73.1 %copy-start.29 = (f32[1024]{0:T(1024)}, f32[1024]{0:T(1024)S(1)}, u32[]{:S(2)}) copy-start(f32[1024]{0:T(1024)S(1)} %fusion.40) | copy-start | bytes 12292
  444.8 10.2 copy-start.1
  444.9 10.2 copy-start.26
  444.9 10.8 copy-start.14
  478.2 21.7 %copy-start.2 = (bf16[2,1024,768]{1,2,0:T(8,128)(2,1)S(1)}, bf16[2,1024,768]{1,2,0:T(8,128)(2,1)}, u32[]{:S(2)}) copy-start(bf16[2,1024,768]{1,2,0:T(8,128)(2,1)} %copy-done.1) | copy-start | bytes 9437188 | tf_op jit(solution)/shard_map/while
  499.9 8.6 copy-start.17
  499.9 9.9 copy-start.16
  508.5 14.1 %slice-start = ((s8[12582912]{0:T(1024)(128)(4,1)}), s8[4194304]{0:T(1024)(128)(4,1)S(1)}, s32[]{:S(2)}) async-start(s8[12582912]{0:T(1024)(128)(4,1)} %bitcast.161), calls=%async_computation.4 | async-start | bytes 8388608 | tf_op jit(solution)/shard_map/while
  509.8 12.8 slice-start.1
  509.8 12.8 slice-start.2
  539.8 10.2 copy-start.1
  539.8 10.2 copy-start.26
  539.8 10.8 copy-start.14
  573.2 21.7 %copy-start.2 = (bf16[2,1024,768]{1,2,0:T(8,128)(2,1)S(1)}, bf16[2,1024,768]{1,2,0:T(8,128)(2,1)}, u32[]{:S(2)}) copy-start(bf16[2,1024,768]{1,2,0:T(8,128)(2,1)} %copy-done.1) | copy-start | bytes 9437188 | tf_op jit(solution)/shard_map/while
  594.9 9.9 copy-start.16
  603.5 14.1 %slice-start = ((s8[12582912]{0:T(1024)(128)(4,1)}), s8[4194304]{0:T(1024)(128)(4,1)S(1)}, s32[]{:S(2)}) async-start(s8[12582912]{0:T(1024)(128)(4,1)} %bitcast.161), calls=%async_computation.4 | async-start | bytes 8388608 | tf_op jit(solution)/shard_map/while
  604.8 12.8 slice-start.1
  604.8 12.8 slice-start.2
  645.8 654.4 %all-reduce.4.cloned.1.call-start = ((), (), s32[]{:S(2)}) async-start(), calls=%async_computation.3 | async-start | bytes 56623104 | tf_op jit(solution)/shard_map/psum | solution.py:204
  648.5 16.3 %slice-start.6 = ((s8[6291456]{0:T(1024)(128)(4,1)}), s8[4194304]{0:T(1024)(128)(4,1)S(1)}, s32[]{:S(2)}) async-start(s8[6291456]{0:T(1024)(128)(4,1)} %bitcast.196), calls=%async_computation.10 | async-start | bytes 8388608
  653.9 10.9 copy-start.12
  653.9 10.9 slice-start.7
  870.9 11.6 copy-start.25
  870.9 12.4 copy-start.6
  870.9 12.4 copy-start.21
  870.9 12.4 copy-start.36
  870.9 12.5 copy-start.38
  870.9 12.4 copy-start.40
  883.4 50.8 %copy-start.44 = (f32[1,2,4,128]{3,1,2,0:T(2,128)S(1)}, f32[1,2,4,128]{3,1,2,0:T(2,128)}, u32[]{:S(2)}) copy-start(f32[1,2,4,128]{3,1,2,0:T(2,128)} %copy-done.43) | copy-start | bytes 12292
  1306.7 10.7 slice-start.3
  1308.1 9.3 slice-start.4
  1308.1 9.3 slice-start.5
  (36 other events, 137.2 us)
Sparse Core Ops, SparseCore 0:
  28.1 220.8 all-gather.1
  645.9 210.0 reduce-scatter.1
  865.8 434.2 all-reduce.3
where the time goes:
time: 1330 us
  waiting for transfers between devices  751 us (56%)
  matrix products  292 us (22%)
  other arithmetic  114 us (9%)
  local copies, waits for them, and re-layouts  111 us (8%)
  blocking collectives  44.4 us (3%)
  between operations  14.6 us (1%)
    psum x1, waiting for transfers between devices, per_device(): lax.psum((gain_one_grad, bias_one_grad, qkv_grad, query_bias_grad, value_...  359 us
    all_gather x1, waiting for transfers between devices, per_device(): kv_all = lax.all_gather(kv_local, 'blk', axis=1, tiled=True)  209 us
    reduce_scatter x1, waiting for transfers between devices, per_device(): lax.psum_scatter(key_terms.astype(jnp.bfloat16), 'blk', scatter_dimension...  183 us
    dot_general x1, matrix products, per_device(): jnp.dot(a_two, up_weight, preferred_element_type=jnp.float32)  44.6 us
    psum x1, blocking collectives, per_device(): lax.psum((gain_one_grad, bias_one_grad, qkv_grad, query_bias_grad, value_...  44.4 us
    convert_element_type x2, other arithmetic, attend_back(): grad_scores = (probs * (grad_probs - centre)).astype(jnp.bfloat16)  43.4 us
    dot_general x4, matrix products, pair_scores(): jnp.einsum('fqhd,fkhd->fhqk', query, keys, preferred_element_type=jnp.flo...  40.6 us
    dot_general x2, matrix products, attend_back(): jnp.einsum('fqhd,fkhd->fhqk', grad_heads, values, preferred_element_type=...  38.4 us
  transfers between devices with their start and end apart: 3, of which 3 were waited for; matrix products, arithmetic and copies ran while one was open for 5% of the time, Pallas kernels for 0%

commit v1 on v0

v1 whole, which is shorter than its diff:
```python
from functools import partial
import math
import jax
import jax.numpy as jnp
from jax import lax
from jax.experimental import pallas as pl
from jax.experimental.pallas import tpu as pltpu
from jax.sharding import PartitionSpec as P

HEAD_DIM = 64
GRID_W = 64
epsilon = 1e-06
negative = -1e30
VMEM_BYTES = 60 * 1024 * 1024
LOG2E = math.log2(math.e)
F32 = jnp.float32
BF16 = jnp.bfloat16


def mm(a, b, ca, cb):
    return lax.dot_general(a, b, (((ca,), (cb,)), ((), ())), preferred_element_type=F32)


def whole(shape):
    return pl.BlockSpec(shape, lambda *_: (0,) * len(shape), pipeline_mode=pl.Buffered(1))


def norm_parts(values):
    centre = jnp.mean(values, -1, keepdims=True)
    centred = values - centre
    spread = jnp.mean(centred * centred, -1, keepdims=True)
    scale = lax.rsqrt(spread + epsilon)
    return centred * scale, scale


def norm_back(grad, hat, scale, gain):
    scaled = grad * gain
    return scale * (
        scaled
        - jnp.mean(scaled, -1, keepdims=True)
        - hat * jnp.mean(scaled * hat, -1, keepdims=True)
    )


def thirds(row):
    high = row.astype(BF16)
    rest = row - high.astype(F32)
    mid = rest.astype(BF16)
    low = (rest - mid.astype(F32)).astype(BF16)
    return high, mid, low


def project_kernel(tok, keep, row_table, col_table, gain, bias, weight, qb, vb, x0, a1t, qt, k, kt, v, vt):
    width = tok.shape[1]
    rows = tok.shape[0]
    patch = keep[...]
    tall = row_table.shape[0]
    wide = col_table.shape[0]
    row_hot = (lax.broadcasted_iota(jnp.int32, (rows, tall), 1) == patch // GRID_W).astype(F32)
    col_hot = (lax.broadcasted_iota(jnp.int32, (rows, wide), 1) == patch % GRID_W).astype(F32)
    pos_row = jnp.dot(row_hot, row_table[...], precision=lax.Precision.HIGHEST, preferred_element_type=F32)
    pos_col = jnp.dot(col_hot, col_table[...], precision=lax.Precision.HIGHEST, preferred_element_type=F32)
    x = tok[...].astype(F32) + jnp.concatenate([pos_row, pos_col], -1)
    x0[...] = x
    hat, _ = norm_parts(x)
    a = (hat * gain[...].astype(F32) + bias[...].astype(F32)).astype(BF16)
    a1t[...] = a.T
    q = (jnp.dot(a, weight[:, :width], preferred_element_type=F32) + qb[...].astype(F32)).astype(BF16)
    qt[...] = q.T
    kk = jnp.dot(a, weight[:, width : 2 * width], preferred_element_type=F32).astype(BF16)
    k[...] = kk
    kt[...] = kk.T
    vv = (jnp.dot(a, weight[:, 2 * width :], preferred_element_type=F32) + vb[...].astype(F32)).astype(BF16)
    v[...] = vv
    vt[...] = vv.T


def project(tok, keep, tables, gain, bias, weight, qb, vb, block=256):
    slots, width = tok.shape
    nat = pl.BlockSpec((block, width), lambda i: (i, 0))
    tra = pl.BlockSpec((width, block), lambda i: (0, i))
    sn = jax.ShapeDtypeStruct((slots, width), BF16)
    st = jax.ShapeDtypeStruct((width, slots), BF16)
    return pl.pallas_call(
        project_kernel,
        grid=(slots // block,),
        in_specs=[
            nat,
            pl.BlockSpec((block, 1), lambda i: (i, 0)),
            whole(tables[0].shape),
            whole(tables[1].shape),
            whole((1, width)),
            whole((1, width)),
            whole(weight.shape),
            whole((1, width)),
            whole((1, width)),
        ],
        out_specs=[nat, tra, tra, nat, tra, nat, tra],
        out_shape=[jax.ShapeDtypeStruct((slots, width), F32), st, st, sn, st, sn, st],
        compiler_params=pltpu.CompilerParams(vmem_limit_bytes=VMEM_BYTES),
        cost_estimate=pl.CostEstimate(flops=2 * slots * width * 3 * width, bytes_accessed=20 * slots * width, transcendentals=0),
        name="project",
    )(tok, keep[:, None], *tables, gain[None], bias[None], weight, qb[None], vb[None])


def augment_cols(block, extra, second):
    lane = lax.broadcasted_iota(jnp.int32, block.shape, 1)
    return jnp.where((lane >= HEAD_DIM) if second else (lane < HEAD_DIM), block, extra)


def augment_rows(block, extra, second):
    if second:
        return jnp.concatenate([extra, block[HEAD_DIM:]], 0)
    return jnp.concatenate([block[:HEAD_DIM], extra], 0)


def key_bias(count, slots):
    return jnp.where(lax.broadcasted_iota(jnp.int32, (slots, 1), 0) < count, 0.0, negative)


def attend_kernel(block, count, qt, k, vt, o, ot, lse):
    slots = k.shape[0]
    c = HEAD_DIM**-0.5 * LOG2E
    lane = lax.broadcasted_iota(jnp.int32, (slots, 2 * HEAD_DIM), 1)
    kb = key_bias(count[0, 0], slots)
    extra_col = jnp.where(lane % HEAD_DIM == 0, kb, 0.0).astype(BF16)
    sub = lax.broadcasted_iota(jnp.int32, (HEAD_DIM, block), 0)
    extra_row = jnp.where(sub == 0, 1.0, 0.0).astype(BF16)
    subv = lax.broadcasted_iota(jnp.int32, (16, slots), 0)
    ones = jnp.where(subv == 0, 1.0, 0.0).astype(BF16)
    for head in range(2):
        ka = augment_cols(k[...], extra_col, head == 1)
        va = jnp.concatenate([vt[head * HEAD_DIM : (head + 1) * HEAD_DIM, :], ones], 0)
        for i in range(slots // block):
            cols = slice(i * block, (i + 1) * block)
            qa = augment_rows(qt[:, cols], extra_row, head == 1)
            s = mm(ka, qa, 1, 0)
            top = jnp.max(s, 0, keepdims=True)
            p = jnp.exp2((s - top) * c).astype(BF16)
            r = mm(va, p, 1, 0)
            total = r[HEAD_DIM : HEAD_DIM + 1]
            mixed = (r[:HEAD_DIM] / total).astype(BF16)
            ot[head * HEAD_DIM : (head + 1) * HEAD_DIM, cols] = mixed
            lse[0, head : head + 1, cols] = top * HEAD_DIM**-0.5 + jnp.log(total)
    o[...] = ot[...].T


def attend(count, qt, k, vt, block=256):
    slots, width = k.shape
    pairs = width // (2 * HEAD_DIM)
    tra = pl.BlockSpec((2 * HEAD_DIM, slots), lambda j: (j, 0))
    nat = pl.BlockSpec((slots, 2 * HEAD_DIM), lambda j: (0, j))
    return pl.pallas_call(
        partial(attend_kernel, block),
        grid=(pairs,),
        in_specs=[pl.BlockSpec(memory_space=pltpu.SMEM), tra, nat, tra],
        out_specs=[nat, tra, pl.BlockSpec((1, 2, slots), lambda j: (j, 0, 0))],
        out_shape=[
            jax.ShapeDtypeStruct((slots, width), BF16),
            jax.ShapeDtypeStruct((width, slots), BF16),
            jax.ShapeDtypeStruct((pairs, 2, slots), F32),
        ],
        compiler_params=pltpu.CompilerParams(vmem_limit_bytes=VMEM_BYTES),
        cost_estimate=pl.CostEstimate(flops=16 * slots * slots * width, bytes_accessed=12 * slots * width, transcendentals=slots * slots * 12),
        name="attend",
    )(count, qt, k, vt)


def middle_kernel(
    o, ot, x0, y, w_out, b_out, gain, bias, up, up_bias, down, down_bias,
    out, d_up, d_up_bias, d_down, d_out, dx1, dot_, vecs,
    x1, hat, scale, a2, a2t, acc, dacc,
):
    step = pl.program_id(0)
    last = pl.num_programs(0) - 1

    @pl.when(step == 0)
    def _():
        x = x0[...] + jnp.dot(o[...], w_out[...], preferred_element_type=F32) + b_out[...].astype(F32)
        x1[...] = x
        h, s = norm_parts(x)
        hat[...] = h
        scale[...] = s
        a = (h * gain[...].astype(F32) + bias[...].astype(F32)).astype(BF16)
        a2[...] = a
        a2t[...] = a.T
        acc[...] = jnp.zeros_like(acc)
        dacc[...] = jnp.zeros_like(dacc)

    h = jnp.dot(a2[...], up[...], preferred_element_type=F32) + up_bias[...].astype(F32)
    phi = 0.5 + 0.5 * lax.erf(h * (0.5**0.5))
    slope = phi + h * (jnp.exp2(h * h * (-0.5 * LOG2E)) * (2 * math.pi) ** -0.5)
    g = (h * phi).astype(BF16)
    dg = mm(y[...], down[...], 1, 1)
    dh = (dg * slope).astype(BF16)
    d_up_bias[...] = jnp.sum(dh.astype(F32), 0, keepdims=True)
    acc[...] += jnp.dot(g, down[...], preferred_element_type=F32)
    dacc[...] += mm(dh, up[...], 1, 1)
    d_up[...] = jnp.dot(a2t[...], dh, preferred_element_type=F32).astype(BF16)
    d_down[...] = jnp.dot(g.T, y[...], preferred_element_type=F32).astype(BF16)

    @pl.when(step == last)
    def _():
        out[...] = (x1[...] + acc[...] + down_bias[...].astype(F32)).astype(BF16)
        grad = dacc[...]
        yf = y[...].astype(F32)
        dx = yf + norm_back(grad, hat[...], scale[...], gain[...].astype(F32))
        dx1[...] = dx
        dz = dx.astype(BF16)
        vecs[0:1, :] = jnp.sum(grad * hat[...], 0, keepdims=True)
        vecs[1:2, :] = jnp.sum(grad, 0, keepdims=True)
        vecs[2:3, :] = jnp.sum(yf, 0, keepdims=True)
        vecs[3:4, :] = jnp.sum(dz.astype(F32), 0, keepdims=True)
        vecs[4:8, :] = jnp.zeros_like(vecs[4:8, :])
        d_out[...] = jnp.dot(ot[...], dz, preferred_element_type=F32).astype(BF16)
        dot_[...] = mm(dz, w_out[...], 1, 1).astype(BF16).T


def middle(o, ot, x0, y, w_out, b_out, gain, bias, up, up_bias, down, down_bias, block=256):
    slots, width = o.shape
    ff = up.shape[1]
    return pl.pallas_call(
        middle_kernel,
        grid=(ff // block,),
        in_specs=[
            whole((slots, width)),
            whole((width, slots)),
            whole((slots, width)),
            whole((slots, width)),
            whole((width, width)),
            whole((1, width)),
            whole((1, width)),
            whole((1, width)),
            pl.BlockSpec((width, block), lambda i: (0, i)),
            pl.BlockSpec((1, block), lambda i: (0, i)),
            pl.BlockSpec((block, width), lambda i: (i, 0)),
            whole((1, width)),
        ],
        out_specs=[
            whole((slots, width)),
            pl.BlockSpec((width, block), lambda i: (0, i)),
            pl.BlockSpec((1, block), lambda i: (0, i)),
            pl.BlockSpec((block, width), lambda i: (i, 0)),
            whole((width, width)),
            whole((slots, width)),
            whole((width, slots)),
            whole((8, width)),
        ],
        out_shape=[
            jax.ShapeDtypeStruct((slots, width), BF16),
            jax.ShapeDtypeStruct((width, ff), BF16),
            jax.ShapeDtypeStruct((1, ff), F32),
            jax.ShapeDtypeStruct((ff, width), BF16),
            jax.ShapeDtypeStruct((width, width), BF16),
            jax.ShapeDtypeStruct((slots, width), F32),
            jax.ShapeDtypeStruct((width, slots), BF16),
            jax.ShapeDtypeStruct((8, width), F32),
        ],
        scratch_shapes=[
            pltpu.VMEM((slots, width), F32),
            pltpu.VMEM((slots, width), F32),
            pltpu.VMEM((slots, 1), F32),
            pltpu.VMEM((slots, width), BF16),
            pltpu.VMEM((width, slots), BF16),
            pltpu.VMEM((slots, width), F32),
            pltpu.VMEM((slots, width), F32),
        ],
        compiler_params=pltpu.CompilerParams(vmem_limit_bytes=VMEM_BYTES),
        cost_estimate=pl.CostEstimate(flops=12 * slots * width * ff, bytes_accessed=20 * slots * width, transcendentals=2 * slots * ff),
        name="middle",
    )(o, ot, x0, y, w_out, b_out[None], gain[None], bias[None], up, up_bias[None], down, down_bias[None])


def back_kernel(
    block, count, qt, k, kt, v, dot_, ot, lse, a1t, wq, wk, wv, x0, dx1, gain,
    dwq, dwk, dwv, dqb, dvb, din, vecs,
    acc, dt,
):
    step = pl.program_id(0)
    last = pl.num_programs(0) - 1
    slots = k.shape[0]
    pair = 2 * HEAD_DIM
    c = HEAD_DIM**-0.5 * LOG2E
    scale = HEAD_DIM**-0.5
    lane = lax.broadcasted_iota(jnp.int32, (slots, pair), 1) % HEAD_DIM
    kb = key_bias(count[0, 0], slots)
    extra_k = jnp.where(lane == 0, kb, jnp.where(lane < 4, 1.0, 0.0)).astype(BF16)
    extra_v = jnp.where(lane < 3, 1.0, 0.0).astype(BF16)
    zeros = jnp.zeros((HEAD_DIM - 4, slots), F32)
    one = jnp.ones((1, slots), F32)
    for head in range(2):
        rows = slice(head * HEAD_DIM, (head + 1) * HEAD_DIM)
        ka = augment_cols(k[...], extra_k, head == 1)
        va = augment_cols(v[...], extra_v, head == 1)
        delta = jnp.sum(dot_[rows, :].astype(F32) * ot[rows, :].astype(F32), 0, keepdims=True)
        l3 = [t.astype(F32) for t in thirds(lse[0, head : head + 1, :] * -(HEAD_DIM**0.5))]
        d3 = [t.astype(F32) for t in thirds(-delta)]
        extra_q = jnp.concatenate([one, *l3, zeros], 0).astype(BF16)
        extra_d = jnp.concatenate([*d3, zeros, 0.0 * one], 0).astype(BF16)
        qa = augment_rows(qt[...], extra_q, head == 1)
        da = augment_rows(dot_[...], extra_d, head == 1)
        for i in range(slots // block):
            cols = slice(i * block, (i + 1) * block)
            s = mm(ka, qa[:, cols], 1, 0)
            dp = mm(va, da[:, cols], 1, 0)
            p = jnp.exp2(s * c)
            ds = (p * dp).astype(BF16)
            p = p.astype(BF16)
            dt[head * HEAD_DIM : (head + 1) * HEAD_DIM, cols] = (mm(kt[rows, :], ds, 1, 0) * scale).astype(BF16)
            dv = mm(dot_[rows, cols], p, 1, 1)
            dk = mm(qt[rows, cols], ds, 1, 1)
            if i == 0:
                dv_sum, dk_sum = dv, dk
            else:
                dv_sum, dk_sum = dv_sum + dv, dk_sum + dk
        dt[pair + head * HEAD_DIM : pair + (head + 1) * HEAD_DIM, :] = (dk_sum * scale).astype(BF16)
        dt[2 * pair + head * HEAD_DIM : 2 * pair + (head + 1) * HEAD_DIM, :] = dv_sum.astype(BF16)

    d = dt[...]
    grads = mm(a1t[...], d, 1, 1).astype(BF16)
    dwq[...] = grads[:, :pair]
    dwk[...] = grads[:, pair : 2 * pair]
    dwv[...] = grads[:, 2 * pair :]
    dqb[...] = jnp.broadcast_to(jnp.sum(d[:pair].astype(F32), 1, keepdims=True), dqb.shape)
    dvb[...] = jnp.broadcast_to(jnp.sum(d[2 * pair :].astype(F32), 1, keepdims=True), dvb.shape)
    w = jnp.concatenate([wq[...], wk[...], wv[...]], 1)
    part = mm(d.T, w, 1, 1)

    @pl.when(step == 0)
    def _():
        acc[...] = part

    @pl.when(step > 0)
    def _():
        acc[...] += part

    @pl.when(step == last)
    def _():
        grad = acc[...]
        hat, sc = norm_parts(x0[...])
        dn = norm_back(grad, hat, sc, gain[...].astype(F32))
        din[...] = (dx1[...] + dn).astype(BF16)
        vecs[0:1, :] = jnp.sum(grad * hat, 0, keepdims=True)
        vecs[1:2, :] = jnp.sum(grad, 0, keepdims=True)
        vecs[2:8, :] = jnp.zeros_like(vecs[2:8, :])


def back(count, qt, k, kt, v, dot_, ot, lse, a1t, weight, x0, dx1, gain, block=256):
    slots, width = k.shape
    pair = 2 * HEAD_DIM
    pairs = width // pair
    tra = pl.BlockSpec((pair, slots), lambda j: (j, 0))
    nat = pl.BlockSpec((slots, pair), lambda j: (0, j))

    def cols(part):
        return pl.BlockSpec((width, pair), lambda j: (0, part * pairs + j))

    sw = jax.ShapeDtypeStruct((width, width), BF16)
    sb = jax.ShapeDtypeStruct((width, 128), F32)
    return pl.pallas_call(
        partial(back_kernel, block),
        grid=(pairs,),
        in_specs=[
            pl.BlockSpec(memory_space=pltpu.SMEM),
            tra, nat, tra, nat, tra, tra,
            pl.BlockSpec((1, 2, slots), lambda j: (j, 0, 0)),
            whole((width, slots)),
            cols(0), cols(1), cols(2),
            whole((slots, width)),
            whole((slots, width)),
            whole((1, width)),
        ],
        out_specs=[cols(0), cols(0), cols(0), pl.BlockSpec((pair, 128), lambda j: (j, 0)), pl.BlockSpec((pair, 128), lambda j: (j, 0)),
            whole((slots, width)), whole((8, width))],
        out_shape=[sw, sw, sw, sb, sb, jax.ShapeDtypeStruct((slots, width), BF16), jax.ShapeDtypeStruct((8, width), F32)],
        scratch_shapes=[pltpu.VMEM((slots, width), F32), pltpu.VMEM((3 * pair, slots), BF16)],
        compiler_params=pltpu.CompilerParams(vmem_limit_bytes=VMEM_BYTES),
        cost_estimate=pl.CostEstimate(flops=40 * slots * slots * width, bytes_accessed=30 * slots * width, transcendentals=slots * slots * 12),
        name="back",
    )(count, qt, k, kt, v, dot_, ot, lse, a1t, weight, weight, weight, x0, dx1, gain[None])


def tables(width):
    quarter = width // 4
    omega = 1.0 / 10000.0 ** (jnp.arange(quarter).astype(F32) / quarter)

    def table(length):
        ang = jnp.arange(length).astype(F32)[:, None] * omega
        return jnp.concatenate([jnp.sin(ang), jnp.cos(ang)], -1)

    return table(2048 // GRID_W), table(GRID_W)


def to_field(part):
    return lax.all_to_all(part, "blk", 0, 1, tiled=True)[0]


def to_slots(whole_field):
    return lax.all_to_all(whole_field[None], "blk", 1, 0, tiled=True)


def per_device(
    tokens, keep_index, counts, norm1_gain, norm1_bias, qkv_weight, query_bias, value_bias, out_weight, out_bias,
    norm2_gain, norm2_bias, up_weight, up_bias, down_weight, down_bias, cotangent,
):
    width = tokens.shape[2]
    both = ("fields", "blk")
    count = lax.dynamic_slice(counts, (lax.axis_index("blk"),), (1,))[None]
    x0, a1t, qt, k, kt, v, vt = project(
        to_field(tokens), to_field(keep_index), tables(width), norm1_gain, norm1_bias, qkv_weight, query_bias, value_bias
    )
    y = to_field(cotangent)
    o, ot, lse = attend(count, qt, k, vt)
    out, d_up, d_up_bias, d_down, d_out, dx1, dot_, vecs_two = middle(
        o, ot, x0, y, out_weight, out_bias, norm2_gain, norm2_bias, up_weight, up_bias, down_weight, down_bias
    )
    d_up, d_down, d_out = lax.psum((d_up, d_down, d_out), both)
    output = to_slots(out)
    dwq, dwk, dwv, dqb, dvb, din, vecs_one = back(
        count, qt, k, kt, v, dot_, ot, lse, a1t, qkv_weight, x0, dx1, norm1_gain
    )
    dwq, dwk, dwv = lax.psum((dwq, dwk, dwv), both)
    input_grad = to_slots(din)
    vecs = jnp.concatenate(
        [vecs_one[:2], vecs_two[:4], dqb[:, 0][None], dvb[:, 0][None], d_up_bias.reshape(-1, width)], 0
    )
    vecs = lax.psum(vecs, both)
    return (
        output,
        input_grad,
        vecs[0],
        vecs[1],
        jnp.concatenate([dwq, dwk, dwv], 1).astype(F32),
        vecs[6],
        vecs[7],
        d_out.astype(F32),
        vecs[5],
        vecs[2],
        vecs[3],
        d_up.astype(F32),
        vecs[8:].reshape(-1),
        d_down.astype(F32),
        vecs[4],
    )


def solution(mesh):
    rows = P("fields", "blk", None)
    return jax.shard_map(
        per_device,
        mesh=mesh,
        in_specs=(rows, P("fields", "blk"), P("fields"), *[P()] * 13, rows),
        out_specs=(rows, rows, *[P()] * 13),
        check_vma=False,
    )
```

time: 1330 us -> 587 us (0.44)
  waiting for transfers between devices: 751 us -> 224 us
  matrix products: 292 us -> 0 us
  Pallas kernels: 0 us -> 160 us
  local copies, waits for them, and re-layouts: 111 us -> 38.7 us
  other arithmetic: 114 us -> 42.6 us
  blocking collectives: 44.4 us -> 83.8 us
  starting transfers between devices: 0.12 us -> 16.5 us
    dot_general x26 -> x0, matrix products: 292 us -> none  [the longest x1 44.6 us: per_device(): jnp.dot(a_two, up_weight, preferred_element_type=jnp.float32)]
    all_gather x1 -> x0, waiting for transfers between devices: 209 us -> none  [per_device(): kv_all = lax.all_gather(kv_local, 'blk', axis=1, tiled=True)]
    psum x1, waiting for transfers between devices: 359 us -> 154 us  [per_device(): dwq, dwk, dwv = lax.psum((dwq, dwk, dwv), both)]
    reduce_scatter x1 -> x0, waiting for transfers between devices: 183 us -> none  [per_device(): lax.psum_scatter(key_terms.astype(jnp.bfloat16), 'blk', scatter_dimension...]
    pallas_call x0 -> x4, Pallas kernels: none -> 160 us  [the longest x1 58.4 us: back(): pl.pallas_call(partial(back_kernel, block), grid=(pairs,), in_specs=[pl.B...]
    all_to_all x0 -> x4, waiting for transfers between devices: none -> 70.8 us  [the longest x2 35.6 us: to_field(): return lax.all_to_all(part, 'blk', 0, 1, tiled=True)[0]]
    reduce_sum x11 -> x0, other arithmetic: 36.3 us -> none  [the longest x2 22.4 us: attend_pair(): total = jnp.sum(expo, -1, keepdims=True)]
    convert_element_type x15 -> x6, other arithmetic: 52.3 us -> 16.8 us  [the longest x1 7.52 us: per_device(): d_up.astype(F32)]
  transfers between devices with their start and end apart: 3 -> 5, of which waited for: 3 -> 3; matrix products, arithmetic and copies ran while one was open for 5% -> 10% of each run, Pallas kernels for 0% -> 9%
where the time goes in v1:
time: 587 us; the launch traced here: 580 us
  waiting for transfers between devices  224 us (38%)
  Pallas kernels  160 us (27%)
  blocking collectives  83.8 us (14%)
  other arithmetic  42.6 us (7%)
  local copies, waits for them, and re-layouts  38.7 us (7%)
  starting transfers between devices  16.5 us (3%)
  between operations  14.8 us (3%)
    psum x1, waiting for transfers between devices, per_device(): dwq, dwk, dwv = lax.psum((dwq, dwk, dwv), both)  154 us
    psum x1, blocking collectives, per_device(): vecs = lax.psum(vecs, both)  72.1 us
    pallas_call x1, Pallas kernels, back(): pl.pallas_call(partial(back_kernel, block), grid=(pairs,), in_specs=[pl.B...  58.4 us
    pallas_call x1, Pallas kernels, middle(): pl.pallas_call(middle_kernel, grid=(ff // block,), in_specs=[whole((slots...  51.2 us
    pallas_call x1, Pallas kernels, attend(): pl.pallas_call(partial(attend_kernel, block), grid=(pairs,), in_specs=[pl...  37 us
    all_to_all x2, waiting for transfers between devices, to_field(): return lax.all_to_all(part, 'blk', 0, 1, tiled=True)[0]  35.6 us
    all_to_all x2, waiting for transfers between devices, to_slots(): return lax.all_to_all(whole_field[None], 'blk', 1, 0, tiled=True)  35.2 us
    unnamed x2, other arithmetic  23.2 us
  transfers between devices with their start and end apart: 5, of which 3 were waited for; matrix products, arithmetic and copies ran while one was open for 10% of the time, Pallas kernels for 9%

profile of v1, /device:TPU:0, one launch (start us, length us, event | category | flops | bytes accessed | tf_op | source)
XLA Modules:
  0.0 580.4 jit_solution(17937169084226415358)
XLA Ops:
  7.2 0.7 all_to_all.18
  7.9 11.7 %all_to_all.55 = s32[4,1,256]{2,1,0:T(1,128)S(1)} all-to-all(s32[4,1,256]{2,1,0:T(1,128)S(1)} %all_to_all.18), channel_id=1, replica_groups=mesh['fields'=8,'blk'=4] {'blk'}, dimensions={0} | all-to-all | bytes 8192 | tf_op jit(solution)/shard_map/all_to_all | solution.py:395
  19.6 3.6 all-to-all-start
  23.3 35.6 %all-to-all-done = bf16[4,256,768]{2,1,0:T(8,128)(2,1)S(1)} async-done(((bf16[4,256,768]{2,1,0:T(8,128)(2,1)}), bf16[4,256,768]{2,1,0:T(8,128)(2,1)S(1)}, u32[]{:S(2)}, u32[]{:S(2)}) %all-to-all-start) | async-done | bytes 1572896 | tf_op jit(solution)/shard_map/all_to_all | solution.py:395
  58.9 1.1 copy-done.2
  60.0 3.6 all-to-all-start.2
  63.7 0.6 broadcast_in_dim.42.gain
  64.3 0.6 broadcast_in_dim.43.bias
  64.9 0.6 broadcast_in_dim.44.qb
  65.4 0.6 broadcast_in_dim.45.vb
  66.0 0.6 broadcast_in_dim.49.up_bias
  66.6 0.6 broadcast_in_dim.46.b_out
  67.2 0.6 broadcast_in_dim.47.gain
  67.8 0.6 broadcast_in_dim.48.bias
  68.4 0.6 broadcast_in_dim.50.down_bias
  69.0 0.6 dynamic_slice.3
  69.8 0.7 pad_maximum_fusion.1.row_table
  70.8 0.7 pad_maximum_fusion.col_table
  71.6 1.0 copy.36.keep
  72.6 13.0 %project.1 = (f32[1024,768]{1,0:T(8,128)}, bf16[768,1024]{1,0:T(8,128)(2,1)}, bf16[768,1024]{1,0:T(8,128)(2,1)}, bf16[1024,768]{1,0:T(8,128)(2,1)}, bf16[768,102...) custom-call(bf16[1024,768]{1,0:T(8,128)(2,1)} %bitcast.21, s32[1024,1]{1,0:T(8,128)} %copy.36.keep, ...), custom_call_target="tpu_custom_call" | custom-call | flops 3623878656 | bytes 15728640 | tf_op jit(solution)/shard_map/project/pallas_call | solution.py:84
  85.6 37.0 %attend.1 = (bf16[1024,768]{1,0:T(8,128)(2,1)}, bf16[768,1024]{1,0:T(8,128)(2,1)}, f32[6,2,1024]{2,1,0:T(2,128)}) custom-call(s32[1,1]{1,0:T(1,128)} %bitcast.count, bf16[768,1024]{1,0:T(8,128)(2,1)} %get-tuple-element.40.qt, bf16[1024,768]{1,0:T(8,128)(2,1)} %get-tuple-element.41.k, bf16[768,1024]{1,0:T(8,128)(2,1)} %get-tuple-element.42.vt), custom_call_target="tpu_custom_call" | custom-call | flops 12884901888 | bytes 9437184 | tf_op jit(solution)/shard_map/attend/pallas_call | solution.py:153
  122.5 1.2 copy-done.1
  123.7 51.2 %middle.1 = (bf16[1024,768]{1,0:T(8,128)(2,1)}, bf16[768,3072]{1,0:T(8,128)(2,1)}, f32[1,3072]{1,0:T(1,128)}, bf16[3072,768]{1,0:T(8,128)(2,1)}, bf16[768,768]{1...) custom-call(bf16[1024,768]{1,0:T(8,128)(2,1)} %get-tuple-element.43.o, ...), custom_call_target="tpu_custom_call" | custom-call | flops 28991029248 | bytes 15728640 | tf_op jit(solution)/shard_map/middle/pallas_call | solution.py:222
  175.0 58.4 %back.1 = (bf16[768,768]{1,0:T(8,128)(2,1)}, bf16[768,768]{1,0:T(8,128)(2,1)}, bf16[768,768]{1,0:T(8,128)(2,1)}, f32[768,128]{1,0:T(8,128)}, f32[768,128]{1,0:T(...) custom-call(s32[1,1]{1,0:T(1,128)} %bitcast.count, bf16[768,1024]{1,0:T(8,128)(2,1)} %get-tuple-element.40.qt, ...), custom_call_target="tpu_custom_call" | custom-call | flops 32212254720 | bytes 23592960 | tf_op jit(solution)/shard_map/back/pallas_call | solution.py:360
  233.5 3.8 copy.43
  237.8 11.6 %reduce.25 = bf16[1024,768]{1,0:T(8,128)(2,1)} reduce(bf16[1024,1,768]{2,1,0:T(2,128)(2,1)S(1)} %bitcast.16, bf16[]{:T(256)} %broadcast.24), dimensions={1}, to_apply=%bitcast.14.reduce_sub_computation | reduce | bytes 3145730
  249.4 3.7 reshape.95
  253.1 5.0 all-to-all-start.4
  258.1 3.9 copy.44
  262.0 11.6 %reduce.24 = bf16[1024,768]{1,0:T(8,128)(2,1)} reduce(bf16[1024,1,768]{2,1,0:T(2,128)(2,1)S(1)} %bitcast.17, bf16[]{:T(256)} %broadcast.24), dimensions={1}, to_apply=%bitcast.15.reduce_sub_computation | reduce | bytes 3145730
  273.6 3.7 reshape.93
  277.4 35.2 %all-to-all-done.4 = bf16[4,2,98304]{2,1,0:T(2,128)(2,1)} async-done(((bf16[4,2,98304]{2,1,0:T(2,128)(2,1)}), bf16[4,2,98304]{2,1,0:T(2,128)(2,1)}, u32[]{:S(2)}, u32[]{:S(2)}) %all-to-all-start.4) | async-done | bytes 1572896 | tf_op jit(solution)/shard_map/all_to_all | solution.py:399
  312.5 4.3 all-to-all-start.3
  317.2 0.7 slice.39
  318.4 0.7 reduce.23
  319.2 72.1 %psum.49 = f32[12,768]{1,0:T(8,128)S(1)} all-reduce(f32[12,768]{1,0:T(8,128)S(1)} %concatenate.14), channel_id=1, replica_groups=mesh['fields'=8,'blk'=4] {'fields','blk'}, use_global_device_ids=true, to_apply=%region_0.0 | all-reduce | flops 9216 | bytes 73728 | tf_op jit(solution)/shard_map/psum | solution.py:427
  391.3 0.6 reshape.73
  391.9 0.7 slice_reduce_fusion.2
  392.6 3.1 reshape.96
  395.7 1.4 copy.40
  397.1 3.1 reshape.94
  400.2 1.4 copy.39
  401.6 153.5 %all-reduce.3.cloned.1.call-done = (bf16[768,768]{1,0:T(8,128)(2,1)}, bf16[768,768]{1,0:T(8,128)(2,1)}, bf16[768,768]{1,0:T(8,128)(2,1)}, bf16[768,768]{1,0:T(8,...) async-done(((bf16[768,768]{1,0:T(8,128)(2,1)}, bf16[768,768]{1,0:T(8,128)(2,1)}, bf16[768,768]{1,0:T(8,128)(2,1)}, bf16[768,768]{1,0:T(8,128)(2,1)}, ...) | async-done | bytes 14155792 | tf_op jit(solution)/shard_map/psum | solution.py:422
  555.1 7.5 %convert_element_type.48 = f32[768,3072]{1,0:T(8,128)} convert(bf16[768,3072]{1,0:T(8,128)(2,1)} %get-tuple-element.77) | non-fusion elementwise | flops 2359296 | bytes 14155776 | tf_op jit(solution)/shard_map/convert_element_type | solution.py:440
  562.6 4.5 convert_element_type.49
  567.1 1.6 convert_element_type.47
  568.7 0.8 copy-done.5
  569.9 3.2 maximum_convert_fusion
  (57 shorter events, 2.5 us)
Async XLA Ops:
  19.6 39.3 %all-to-all-start = ((bf16[4,256,768]{2,1,0:T(8,128)(2,1)}), bf16[4,256,768]{2,1,0:T(8,128)(2,1)S(1)}, u32[]{:S(2)}, u32[]{:S(2)}) async-start(bf16[4,256,768]{2,1,0:T(8,128)(2,1)} %param.17), calls=%async_computation | async-start | bytes 3145728 | tf_op jit(solution)/shard_map/all_to_all | solution.py:395
  23.1 40.5 %copy-start.12 = (bf16[768]{0:T(1024)(128)(2,1)S(1)}, bf16[768]{0:T(1024)(128)(2,1)}, u32[]{:S(2)}) copy-start(bf16[768]{0:T(1024)(128)(2,1)} %param.20) | copy-start | bytes 4612
  23.1 41.1 %copy-start.13 = (bf16[768]{0:T(1024)(128)(2,1)S(1)}, bf16[768]{0:T(1024)(128)(2,1)}, u32[]{:S(2)}) copy-start(bf16[768]{0:T(1024)(128)(2,1)} %param.21) | copy-start | bytes 4612
  23.2 41.7 %copy-start.14 = (bf16[768]{0:T(1024)(128)(2,1)S(1)}, bf16[768]{0:T(1024)(128)(2,1)}, u32[]{:S(2)}) copy-start(bf16[768]{0:T(1024)(128)(2,1)} %param.23) | copy-start | bytes 4612
  23.2 42.3 %copy-start.15 = (bf16[768]{0:T(1024)(128)(2,1)S(1)}, bf16[768]{0:T(1024)(128)(2,1)}, u32[]{:S(2)}) copy-start(bf16[768]{0:T(1024)(128)(2,1)} %param.24) | copy-start | bytes 4612
  23.2 42.8 %copy-start.11 = (bf16[3072]{0:T(1024)(128)(2,1)S(1)}, bf16[3072]{0:T(1024)(128)(2,1)}, u32[]{:S(2)}) copy-start(bf16[3072]{0:T(1024)(128)(2,1)} %param.30) | copy-start | bytes 18436
  23.2 43.4 %copy-start.16 = (bf16[768]{0:T(1024)(128)(2,1)S(1)}, bf16[768]{0:T(1024)(128)(2,1)}, u32[]{:S(2)}) copy-start(bf16[768]{0:T(1024)(128)(2,1)} %param.26) | copy-start | bytes 4612
  23.2 44.0 %copy-start.17 = (bf16[768]{0:T(1024)(128)(2,1)S(1)}, bf16[768]{0:T(1024)(128)(2,1)}, u32[]{:S(2)}) copy-start(bf16[768]{0:T(1024)(128)(2,1)} %param.27) | copy-start | bytes 4612
  23.2 44.6 %copy-start.18 = (bf16[768]{0:T(1024)(128)(2,1)S(1)}, bf16[768]{0:T(1024)(128)(2,1)}, u32[]{:S(2)}) copy-start(bf16[768]{0:T(1024)(128)(2,1)} %param.28) | copy-start | bytes 4612
  23.2 45.2 %copy-start.19 = (bf16[768]{0:T(1024)(128)(2,1)S(1)}, bf16[768]{0:T(1024)(128)(2,1)}, u32[]{:S(2)}) copy-start(bf16[768]{0:T(1024)(128)(2,1)} %param.32) | copy-start | bytes 4612
  23.2 45.7 %copy-start.20 = (s32[4]{0:T(128)S(1)}, s32[4]{0:T(128)}, u32[]{:S(2)}) copy-start(s32[4]{0:T(128)} %param.19) | copy-start | bytes 52
  58.9 1.1 copy-start.2
  60.0 62.5 %all-to-all-start.2 = ((bf16[4,256,768]{2,1,0:T(8,128)(2,1)}), bf16[4,256,768]{2,1,0:T(8,128)(2,1)S(1)}, u32[]{:S(2)}, u32[]{:S(2)}) async-start(bf16[4,256,768]{2,1,0:T(8,128)(2,1)} %param.33), calls=%async_computation.2 | async-start | bytes 3145728 | tf_op jit(solution)/shard_map/all_to_all | solution.py:395
  63.6 491.4 %all-reduce.3.cloned.1.call-start = ((), (), s32[]{:S(2)}) async-start(), calls=%async_computation.5 | async-start | bytes 28311552 | tf_op jit(solution)/shard_map/psum | solution.py:422
  122.5 1.2 copy-start.1
  253.1 59.4 %all-to-all-start.4 = ((bf16[4,2,98304]{2,1,0:T(2,128)(2,1)}), bf16[4,2,98304]{2,1,0:T(2,128)(2,1)}, u32[]{:S(2)}, u32[]{:S(2)}) async-start(bf16[4,2,98304]{2,1,0:T(2,128)(2,1)} %reshape.95), calls=%async_computation.4 | async-start | bytes 3145728 | tf_op jit(solution)/shard_map/all_to_all | solution.py:399
  277.3 39.5 %copy-start.7 = (f32[768,128]{1,0:T(8,128)S(1)}, f32[768,128]{1,0:T(8,128)}, u32[]{:S(2)}) copy-start(f32[768,128]{1,0:T(8,128)} %get-tuple-element.56) | copy-start | bytes 1179652
  277.3 39.5 %copy-start.8 = (f32[768,128]{1,0:T(8,128)S(1)}, f32[768,128]{1,0:T(8,128)}, u32[]{:S(2)}) copy-start(f32[768,128]{1,0:T(8,128)} %get-tuple-element.57) | copy-start | bytes 1179652
  277.3 41.1 %copy-start.9 = (f32[1,3072]{1,0:T(1,128)S(1)}, f32[1,3072]{1,0:T(1,128)}, u32[]{:S(2)}) copy-start(f32[1,3072]{1,0:T(1,128)} %get-tuple-element.58) | copy-start | bytes 36868
  277.4 41.8 %copy-start.10 = (f32[8,768]{1,0:T(8,128)S(1)}, f32[8,768]{1,0:T(8,128)}, u32[]{:S(2)}) copy-start(f32[8,768]{1,0:T(8,128)} %get-tuple-element.55) | copy-start | bytes 73732
  312.5 84.5 %all-to-all-start.3 = ((bf16[4,2,98304]{2,1,0:T(2,128)(2,1)}), bf16[4,2,98304]{2,1,0:T(2,128)(2,1)}, u32[]{:S(2)}, u32[]{:S(2)}) async-start(bf16[4,2,98304]{2,1,0:T(2,128)(2,1)} %reshape.93), calls=%async_computation.3 | async-start | bytes 3145728 | tf_op jit(solution)/shard_map/all_to_all | solution.py:399
  555.1 7.5 %copy-start = (bf16[3072,768]{1,0:T(8,128)(2,1)S(1)}, bf16[3072,768]{1,0:T(8,128)(2,1)}, u32[]{:S(2)}) copy-start(bf16[3072,768]{1,0:T(8,128)(2,1)} %get-tuple-element.78) | copy-start | bytes 14155780
  562.6 4.5 copy-start.3
  567.1 1.7 copy-start.4
  567.1 2.5 copy-start.5
  567.1 2.8 copy-start.6
Sparse Core Ops, SparseCore 0:
  233.6 321.4 all-reduce.2

commit v2 on v1

v2 whole, which is shorter than its diff:
```python
from functools import partial
import math
import jax
import jax.numpy as jnp
from jax import lax
from jax.experimental import pallas as pl
from jax.experimental.pallas import tpu as pltpu
from jax.sharding import PartitionSpec as P

HEAD_DIM = 64
GRID_W = 64
epsilon = 1e-06
negative = -1e30
VMEM_BYTES = 60 * 1024 * 1024
LOG2E = math.log2(math.e)
F32 = jnp.float32
BF16 = jnp.bfloat16


def mm(a, b, ca, cb):
    return lax.dot_general(a, b, (((ca,), (cb,)), ((), ())), preferred_element_type=F32)


def whole(shape):
    return pl.BlockSpec(shape, lambda *_: (0,) * len(shape), pipeline_mode=pl.Buffered(1))


def norm_parts(values):
    centre = jnp.mean(values, -1, keepdims=True)
    centred = values - centre
    spread = jnp.mean(centred * centred, -1, keepdims=True)
    scale = lax.rsqrt(spread + epsilon)
    return centred * scale, scale


def norm_back(grad, hat, scale, gain):
    scaled = grad * gain
    return scale * (
        scaled
        - jnp.mean(scaled, -1, keepdims=True)
        - hat * jnp.mean(scaled * hat, -1, keepdims=True)
    )


def thirds(row):
    high = row.astype(BF16)
    rest = row - high.astype(F32)
    mid = rest.astype(BF16)
    low = (rest - mid.astype(F32)).astype(BF16)
    return high, mid, low


def project_kernel(tok, keep, row_table, col_table, gain, bias, weight, qb, vb, x0, a1t, qt, k, kt, v, vt):
    width = tok.shape[1]
    rows = tok.shape[0]
    patch = keep[...]
    tall = row_table.shape[0]
    wide = col_table.shape[0]
    row_hot = (lax.broadcasted_iota(jnp.int32, (rows, tall), 1) == patch // GRID_W).astype(F32)
    col_hot = (lax.broadcasted_iota(jnp.int32, (rows, wide), 1) == patch % GRID_W).astype(F32)
    pos_row = jnp.dot(row_hot, row_table[...], precision=lax.Precision.HIGHEST, preferred_element_type=F32)
    pos_col = jnp.dot(col_hot, col_table[...], precision=lax.Precision.HIGHEST, preferred_element_type=F32)
    x = tok[...].astype(F32) + jnp.concatenate([pos_row, pos_col], -1)
    x0[...] = x
    hat, _ = norm_parts(x)
    a = (hat * gain[...].astype(F32) + bias[...].astype(F32)).astype(BF16)
    a1t[...] = a.T
    q = (jnp.dot(a, weight[:, :width], preferred_element_type=F32) + qb[...].astype(F32)).astype(BF16)
    qt[...] = q.T
    kk = jnp.dot(a, weight[:, width : 2 * width], preferred_element_type=F32).astype(BF16)
    k[...] = kk
    kt[...] = kk.T
    vv = (jnp.dot(a, weight[:, 2 * width :], preferred_element_type=F32) + vb[...].astype(F32)).astype(BF16)
    v[...] = vv
    vt[...] = vv.T


def project(tok, keep, tables, gain, bias, weight, qb, vb, block=256):
    slots, width = tok.shape
    nat = pl.BlockSpec((block, width), lambda i: (i, 0))
    tra = pl.BlockSpec((width, block), lambda i: (0, i))
    sn = jax.ShapeDtypeStruct((slots, width), BF16)
    st = jax.ShapeDtypeStruct((width, slots), BF16)
    return pl.pallas_call(
        project_kernel,
        grid=(slots // block,),
        in_specs=[
            nat,
            pl.BlockSpec((block, 1), lambda i: (i, 0)),
            whole(tables[0].shape),
            whole(tables[1].shape),
            whole((1, width)),
            whole((1, width)),
            whole(weight.shape),
            whole((1, width)),
            whole((1, width)),
        ],
        out_specs=[nat, tra, tra, nat, tra, nat, tra],
        out_shape=[jax.ShapeDtypeStruct((slots, width), F32), st, st, sn, st, sn, st],
        compiler_params=pltpu.CompilerParams(vmem_limit_bytes=VMEM_BYTES),
        cost_estimate=pl.CostEstimate(flops=2 * slots * width * 3 * width, bytes_accessed=20 * slots * width, transcendentals=0),
        name="project",
    )(tok, keep[:, None], *tables, gain[None], bias[None], weight, qb[None], vb[None])


def augment_cols(block, extra, second):
    lane = lax.broadcasted_iota(jnp.int32, block.shape, 1)
    return jnp.where((lane >= HEAD_DIM) if second else (lane < HEAD_DIM), block, extra)


def augment_rows(block, extra, second):
    if second:
        return jnp.concatenate([extra, block[HEAD_DIM:]], 0)
    return jnp.concatenate([block[:HEAD_DIM], extra], 0)


def key_bias(count, slots):
    return jnp.where(lax.broadcasted_iota(jnp.int32, (slots, 1), 0) < count, 0.0, negative)


def attend_kernel(block, count, qt, k, vt, o, ot, lse):
    slots = k.shape[0]
    c = HEAD_DIM**-0.5 * LOG2E
    lane = lax.broadcasted_iota(jnp.int32, (slots, 2 * HEAD_DIM), 1)
    kb = key_bias(count[0, 0], slots)
    extra_col = jnp.where(lane % HEAD_DIM == 0, kb, 0.0).astype(BF16)
    sub = lax.broadcasted_iota(jnp.int32, (HEAD_DIM, block), 0)
    extra_row = jnp.where(sub == 0, 1.0, 0.0).astype(BF16)
    subv = lax.broadcasted_iota(jnp.int32, (16, slots), 0)
    ones = jnp.where(subv == 0, 1.0, 0.0).astype(BF16)
    for head in range(2):
        ka = augment_cols(k[...], extra_col, head == 1)
        va = jnp.concatenate([vt[head * HEAD_DIM : (head + 1) * HEAD_DIM, :], ones], 0)
        for i in range(slots // block):
            cols = slice(i * block, (i + 1) * block)
            qa = augment_rows(qt[:, cols], extra_row, head == 1)
            s = mm(ka, qa, 1, 0)
            top = jnp.max(s, 0, keepdims=True)
            p = jnp.exp2((s - top) * c).astype(BF16)
            r = mm(va, p, 1, 0)
            total = r[HEAD_DIM : HEAD_DIM + 1]
            mixed = (r[:HEAD_DIM] / total).astype(BF16)
            ot[head * HEAD_DIM : (head + 1) * HEAD_DIM, cols] = mixed
            lse[0, head : head + 1, cols] = top * HEAD_DIM**-0.5 + jnp.log(total)
    o[...] = ot[...].T


def attend(count, qt, k, vt, block=256):
    slots, width = k.shape
    pairs = width // (2 * HEAD_DIM)
    tra = pl.BlockSpec((2 * HEAD_DIM, slots), lambda j: (j, 0))
    nat = pl.BlockSpec((slots, 2 * HEAD_DIM), lambda j: (0, j))
    return pl.pallas_call(
        partial(attend_kernel, block),
        grid=(pairs,),
        in_specs=[pl.BlockSpec(memory_space=pltpu.SMEM), tra, nat, tra],
        out_specs=[nat, tra, pl.BlockSpec((1, 2, slots), lambda j: (j, 0, 0))],
        out_shape=[
            jax.ShapeDtypeStruct((slots, width), BF16),
            jax.ShapeDtypeStruct((width, slots), BF16),
            jax.ShapeDtypeStruct((pairs, 2, slots), F32),
        ],
        compiler_params=pltpu.CompilerParams(vmem_limit_bytes=VMEM_BYTES),
        cost_estimate=pl.CostEstimate(flops=16 * slots * slots * width, bytes_accessed=12 * slots * width, transcendentals=slots * slots * 12),
        name="attend",
    )(count, qt, k, vt)


SLOTS_AHEAD = 4
LANES = 128


class Sums:
    def __init__(self, fields, blk, rows, count, grads, recv, recv_blk, sems, free, free_blk):
        self.fields, self.blk, self.rows, self.count = fields, blk, rows, count
        self.bits = fields.bit_length() - 1
        self.grads, self.recv, self.recv_blk = grads, recv, recv_blk
        self.free, self.free_blk = free, free_blk
        self.send_rs, self.recv_rs, self.send_ag, self.recv_ag, self.blk_sems = sems
        self.f, self.z = lax.axis_index("fields"), lax.axis_index("blk")
        self.actions = 2 * self.bits + 3

    def weight(self, block, stage):
        even = 1 << stage
        odd = 1 << (stage if stage == 0 else self.bits - stage)
        odd_block = block % 2
        bit_even, bit_odd = (self.f // even) % 2, (self.f // odd) % 2
        bit = bit_even + odd_block * (bit_odd - bit_even)
        width = even + odd_block * (odd - even)
        return bit, self.f + width * (1 - 2 * bit)

    def start(self, block, stage):
        off = 0
        for k in range(stage):
            bit, _ = self.weight(block, k)
            off = off + bit * (self.rows >> (k + 1))
        return off

    def area(self, block, off, size):
        return self.grads.at[block, pl.ds(pl.multiple_of(off, 16), size)]

    def scatter_copy(self, block, stage):
        bit, partner = self.weight(block, stage)
        size = self.rows >> (stage + 1)
        off = self.start(block, stage) + (1 - bit) * size
        slot = block % SLOTS_AHEAD
        return pltpu.make_async_remote_copy(
            src_ref=self.area(block, off, size),
            dst_ref=self.recv[stage].at[slot],
            send_sem=self.send_rs.at[stage, slot],
            recv_sem=self.recv_rs.at[stage, slot],
            device_id=(partner, self.z),
            device_id_type=pl.DeviceIdType.MESH,
        )

    def gather_copy(self, block, stage):
        _, partner = self.weight(block, stage)
        part = self.area(block, self.start(block, stage + 1), self.rows >> (stage + 1))
        slot = block % SLOTS_AHEAD
        return pltpu.make_async_remote_copy(
            src_ref=part,
            dst_ref=part,
            send_sem=self.send_ag.at[stage, slot],
            recv_sem=self.recv_ag.at[stage, slot],
            device_id=(partner, self.z),
            device_id_type=pl.DeviceIdType.MESH,
        )

    def gather_wait(self, block, stage):
        self.gather_copy(block, stage).wait_send()
        bit, partner = self.weight(block, stage)
        size = self.rows >> (stage + 1)
        part = self.area(block, self.start(block, stage) + (1 - bit) * size, size)
        slot = block % SLOTS_AHEAD
        pltpu.make_async_remote_copy(
            src_ref=part,
            dst_ref=part,
            send_sem=self.send_ag.at[stage, slot],
            recv_sem=self.recv_ag.at[stage, slot],
            device_id=(partner, self.z),
            device_id_type=pl.DeviceIdType.MESH,
        ).wait_recv()

    def blk_copy(self, block, step, kind):
        size = self.rows // (self.fields * self.blk)
        to = (self.z + step) % self.blk
        base = self.start(block, self.bits)
        slot = block % SLOTS_AHEAD
        if kind == 0:
            src = self.area(block, base + to * size, size)
            dst = self.recv_blk.at[slot, step - 1]
        else:
            src = self.area(block, base + self.z * size, size)
            dst = src
        return pltpu.make_async_remote_copy(
            src_ref=src,
            dst_ref=dst,
            send_sem=self.blk_sems.at[kind, 0, step - 1, slot],
            recv_sem=self.blk_sems.at[kind, 1, step - 1, slot],
            device_id=(self.f, to),
            device_id_type=pl.DeviceIdType.MESH,
        )

    def blk_gather_wait(self, block, step):
        self.blk_copy(block, step, 1).wait_send()
        size = self.rows // (self.fields * self.blk)
        came = (self.z + self.blk - step) % self.blk
        slot = block % SLOTS_AHEAD
        part = self.area(block, self.start(block, self.bits) + came * size, size)
        pltpu.make_async_remote_copy(
            src_ref=part,
            dst_ref=part,
            send_sem=self.blk_sems.at[1, 0, step - 1, slot],
            recv_sem=self.blk_sems.at[1, 1, step - 1, slot],
            device_id=(self.f, came),
            device_id_type=pl.DeviceIdType.MESH,
        ).wait_recv()

    def add(self, block, off, size, take):
        chunk = size
        while chunk > 256 or size % chunk:
            chunk -= 16

        @pl.loop(0, size // chunk)
        def _(i):
            at = pl.ds(pl.multiple_of(off + i * chunk, 16), chunk)
            self.grads[block, at, :] = take(self.grads[block, at, :], pl.ds(pl.multiple_of(i * chunk, 16), chunk))

    def act(self, kind, block):
        bits = self.bits
        slot = block % SLOTS_AHEAD
        if 1 <= kind <= bits:
            stage = kind - 1
            self.scatter_copy(block, stage).wait()
            _, partner = self.weight(block, stage)
            pl.semaphore_signal(
                self.free.at[stage, block], 1, device_id=(partner, self.z), device_id_type=pl.DeviceIdType.MESH
            )
            got = self.recv[stage]
            self.add(block, self.start(block, stage + 1), self.rows >> (stage + 1), lambda a, at: a + got[slot, at, :])
        if kind < bits:
            self.scatter_copy(block, kind).start()
        elif kind == bits:
            for step in range(1, self.blk):
                self.blk_copy(block, step, 0).start()
        elif kind == bits + 1:
            for step in range(1, self.blk):
                self.blk_copy(block, step, 0).wait()
                pl.semaphore_signal(
                    self.free_blk.at[self.blk - step - 1, block],
                    1,
                    device_id=(self.f, (self.z + step) % self.blk),
                    device_id_type=pl.DeviceIdType.MESH,
                )
            size = self.rows // (self.fields * self.blk)

            def take(a, at):
                total = a.astype(F32)
                for step in range(1, self.blk):
                    total = total + self.recv_blk[slot, step - 1, at, :].astype(F32)
                return total.astype(BF16)

            self.add(block, self.start(block, bits) + self.z * size, size, take)
            for step in range(1, self.blk):
                pl.semaphore_wait(self.free_blk.at[step - 1, block], 1)
                self.blk_copy(block, step, 1).start()
        else:
            if kind == bits + 2:
                for step in range(1, self.blk):
                    self.blk_gather_wait(block, step)
            else:
                self.gather_wait(block, 2 * bits + 2 - kind + 1 - 1)
            stage = 2 * bits + 1 - kind
            if stage >= 0:
                pl.semaphore_wait(self.free.at[stage, block], 1)
                self.gather_copy(block, stage).start()

    def tick(self, tick, done):
        for kind in range(self.actions):
            block = tick - kind

            @pl.when((block >= 0) & (block < self.count))
            def _():
                self.act(kind, block)
                if kind == self.actions - 1:
                    done(block)


def mega_kernel(
    fields, blk, rows, ff_steps, pairs, tail,
    count, ot, x0, y, w_out, b_out, gain_two, bias_two, up, up_bias, down, down_bias,
    qt, k, kt, v, lse, a1t, wq, wk, wv, gain_one,
    out, din, up_out, down_out, qkv_out, out_out, vec_out,
    x1, a2, a2t, acc, dacc, out_s, dot_s, dt, din_s, grads, vec, recv_blk, vec_recv, vec_recv_blk,
    send_rs, recv_rs, send_ag, recv_ag, blk_sems, vec_sems, vec_blk_sems, move_sems, flush_sems, free, free_blk, *recv,
):
    step = pl.program_id(0)
    slots, width = x0.shape
    pair = 2 * HEAD_DIM
    chunk = slots // blk
    cols_of = width // LANES
    f, z = lax.axis_index("fields"), lax.axis_index("blk")
    bits = fields.bit_length() - 1
    ff = up.shape[1]
    heads_from, heads_to = ff_steps, ff_steps + 2 * pairs
    sums = Sums(
        fields, blk, rows, ff_steps + pairs, grads, recv, recv_blk, (send_rs, recv_rs, send_ag, recv_ag, blk_sems),
        free, free_blk,
    )
    VEC_G1, VEC_B1, VEC_Q, VEC_V, VEC_OUT, VEC_G2, VEC_B2, VEC_DOWN, VEC_UP = range(9)

    def put_vec(index, value):
        for i in range(cols_of):
            vec[index * cols_of + i : index * cols_of + i + 1, :] = value[:, i * LANES : (i + 1) * LANES]

    def moves(src, dst, kind):
        got = []
        for s in range(1, blk):
            to = (z + s) % blk
            got.append(
                pltpu.make_async_remote_copy(
                    src_ref=src.at[pl.ds(pl.multiple_of(to * chunk, 16), chunk)],
                    dst_ref=dst.at[z],
                    send_sem=move_sems.at[kind, 0, s],
                    recv_sem=move_sems.at[kind, 1, s],
                    device_id=(f, to),
                    device_id_type=pl.DeviceIdType.MESH,
                )
            )
        got.append(
            pltpu.make_async_copy(
                src.at[pl.ds(pl.multiple_of(z * chunk, 16), chunk)], dst.at[z], move_sems.at[kind, 0, 0]
            )
        )
        return got

    def moves_wait(src, dst, kind):
        got = moves(src, dst, kind)
        for c in got[:-1]:
            c.wait_send()
        for s in range(1, blk):
            came = (z + blk - s) % blk
            pltpu.make_async_remote_copy(
                src_ref=src.at[pl.ds(0, chunk)],
                dst_ref=dst.at[came],
                send_sem=move_sems.at[kind, 0, s],
                recv_sem=move_sems.at[kind, 1, s],
                device_id=(f, came),
                device_id_type=pl.DeviceIdType.MESH,
            ).wait_recv()
        got[-1].wait()

    @pl.when(step == 0)
    def _():
        barrier = pltpu.get_barrier_semaphore()
        for b in range(bits):
            bit = (f // (1 << b)) % 2
            pl.semaphore_signal(
                barrier, 1, device_id=(f + (1 << b) * (1 - 2 * bit), z), device_id_type=pl.DeviceIdType.MESH
            )
        for s in range(1, blk):
            pl.semaphore_signal(barrier, 1, device_id=(f, (z + s) % blk), device_id_type=pl.DeviceIdType.MESH)
        pl.semaphore_wait(barrier, bits + blk - 1)

        for r in range(blk):
            at = slice(r * chunk, (r + 1) * chunk)
            x = x0[at, :] + jnp.dot(ot[:, at].T, w_out[...], preferred_element_type=F32) + b_out[...].astype(F32)
            x1[at, :] = x
            hat, _ = norm_parts(x)
            a = (hat * gain_two[...].astype(F32) + bias_two[...].astype(F32)).astype(BF16)
            a2[at, :] = a
            a2t[:, at] = a.T
        acc[...] = jnp.zeros_like(acc)
        dacc[...] = jnp.zeros_like(dacc)

    def feed_copies(block):
        base = ff // LANES * width
        got = []
        for i in range(ff // LANES):
            at = pl.ds(pl.multiple_of(block * ff + i * LANES, LANES), LANES)
            got.append((grads.at[block, pl.ds(i * width, width)], up_out.at[:, at]))
        at = pl.ds(pl.multiple_of(block * ff, ff), ff)
        for i in range(cols_of):
            got.append((grads.at[block, pl.ds(base + i * ff, ff)], down_out.at[at, pl.ds(i * LANES, LANES)]))
        return [pltpu.make_async_copy(a, b, flush_sems.at[block, i]) for i, (a, b) in enumerate(got)]

    def proj_copies(block):
        got = []
        for i in range(4):
            at = pl.ds(pl.multiple_of((block - ff_steps + (i % 3) * pairs) * pair, pair), pair)
            got.append((grads.at[block, pl.ds(i * width, width)], (qkv_out if i < 3 else out_out).at[:, at]))
        return [pltpu.make_async_copy(a, b, flush_sems.at[block, i]) for i, (a, b) in enumerate(got)]

    def done(block):
        @pl.when(block < ff_steps)
        def _():
            for c in feed_copies(block):
                c.start()

        @pl.when(block >= ff_steps)
        def _():
            for c in proj_copies(block):
                c.start()

    def tick_of(s):
        return jnp.where(s < heads_to, (2 * s - 2) // 3, (2 * heads_to - 2) // 3 + s - heads_to)

    @pl.when((step >= 1) & (tick_of(step) != tick_of(step - 1)))
    def _():
        sums.tick(tick_of(step), done)

    @pl.when(step < heads_from)
    def _():
        h = jnp.dot(a2[...], up[...], preferred_element_type=F32) + up_bias[...].astype(F32)
        phi = 0.5 + 0.5 * lax.erf(h * (0.5**0.5))
        slope = phi + h * (jnp.exp2(h * h * (-0.5 * LOG2E)) * (2 * math.pi) ** -0.5)
        g = (h * phi).astype(BF16)
        dg = mm(y[...], down[...], 1, 1)
        dh = (dg * slope).astype(BF16)
        sum_up = jnp.sum(dh.astype(F32), 0, keepdims=True)
        for i in range(ff // LANES):
            vec[pl.ds(VEC_UP * cols_of + step * (ff // LANES) + i, 1), :] = sum_up[:, i * LANES : (i + 1) * LANES]
        acc[...] += jnp.dot(g, down[...], preferred_element_type=F32)
        dacc[...] += mm(dh, up[...], 1, 1)
        d_up = jnp.dot(a2t[...], dh, preferred_element_type=F32).astype(BF16)
        for i in range(ff // LANES):
            grads[step, i * width : (i + 1) * width, :] = d_up[:, i * LANES : (i + 1) * LANES]
        d_down = jnp.dot(g.T, y[...], preferred_element_type=F32).astype(BF16)
        base = ff // LANES * width
        for i in range(cols_of):
            grads[step, base + i * ff : base + (i + 1) * ff, :] = d_down[:, i * LANES : (i + 1) * LANES]
        if 2 * base < rows:
            grads[step, 2 * base :, :] = jnp.zeros((rows - 2 * base, LANES), BF16)

    @pl.when(step == heads_from - 1)
    def _():
        totals = [jnp.zeros((1, width), F32) for _ in range(4)]
        for r in range(blk):
            at = slice(r * chunk, (r + 1) * chunk)
            grad = dacc[at, :]
            yf = y[at, :].astype(F32)
            xs = x1[at, :]
            out_s[at, :] = (xs + acc[at, :] + down_bias[...].astype(F32)).astype(BF16)
            hat, sc = norm_parts(xs)
            dx = yf + norm_back(grad, hat, sc, gain_two[...].astype(F32))
            x1[at, :] = dx
            dz = dx.astype(BF16)
            a2[at, :] = dz
            dot_s[:, at] = mm(dz, w_out[...], 1, 1).astype(BF16).T
            for i, value in enumerate((grad * hat, grad, yf, dz.astype(F32))):
                totals[i] = totals[i] + jnp.sum(value, 0, keepdims=True)
        for c in moves(out_s, out, 0):
            c.start()
        for index, value in zip((VEC_G2, VEC_B2, VEC_DOWN, VEC_OUT), totals):
            put_vec(index, value)
        d_out = jnp.dot(ot[...], a2[...], preferred_element_type=F32).astype(BF16)
        for j in range(pairs):
            grads[ff_steps + j, 3 * width : 4 * width, :] = d_out[:, j * pair : (j + 1) * pair]
            if 4 * width < rows:
                grads[ff_steps + j, 4 * width :, :] = jnp.zeros((rows - 4 * width, LANES), BF16)
        dacc[...] = jnp.zeros_like(dacc)

    @pl.when((step >= heads_from) & (step < heads_to))
    def _():
        index = step - heads_from
        j, head = index // 2, index % 2
        c = HEAD_DIM**-0.5 * LOG2E
        scale = HEAD_DIM**-0.5
        block = 256
        lane = lax.broadcasted_iota(jnp.int32, (slots, pair), 1)
        kb = key_bias(count[0, 0], slots)
        mine = lane // HEAD_DIM == head
        lane = lane % HEAD_DIM
        ka = jnp.where(mine, k[...], jnp.where(lane == 0, kb, jnp.where(lane < 4, 1.0, 0.0)).astype(BF16))
        va = jnp.where(mine, v[...], jnp.where(lane < 3, 1.0, 0.0).astype(BF16))
        rows_of = pl.ds(pl.multiple_of(head * HEAD_DIM, HEAD_DIM), HEAD_DIM)
        rows_all = pl.ds(pl.multiple_of(index * HEAD_DIM, HEAD_DIM), HEAD_DIM)
        do_h = dot_s[rows_all, :]
        q_h = qt[rows_of, :]
        k_h = kt[rows_of, :]
        delta = jnp.sum(do_h.astype(F32) * ot[rows_all, :].astype(F32), 0, keepdims=True)
        l3 = [t.astype(F32) for t in thirds(lse[0, pl.ds(head, 1), :] * -(HEAD_DIM**0.5))]
        d3 = [t.astype(F32) for t in thirds(-delta)]
        zeros = jnp.zeros((HEAD_DIM - 4, slots), F32)
        one = jnp.ones((1, slots), F32)
        extra_q = jnp.concatenate([one, *l3, zeros], 0).astype(BF16)
        extra_d = jnp.concatenate([*d3, zeros, 0.0 * one], 0).astype(BF16)
        first = lax.broadcasted_iota(jnp.int32, (pair, slots), 0) // HEAD_DIM == head
        qa = jnp.where(first, jnp.concatenate([q_h, q_h], 0), jnp.concatenate([extra_q, extra_q], 0))
        da = jnp.where(first, jnp.concatenate([do_h, do_h], 0), jnp.concatenate([extra_d, extra_d], 0))
        for i in range(slots // block):
            at = slice(i * block, (i + 1) * block)
            s = mm(ka, qa[:, at], 1, 0)
            dp = mm(va, da[:, at], 1, 0)
            p = jnp.exp2(s * c)
            ds = (p * dp).astype(BF16)
            p = p.astype(BF16)
            dt[rows_of, at] = (mm(k_h, ds, 1, 0) * scale).astype(BF16)
            dv = mm(do_h[:, at], p, 1, 1)
            dk = mm(q_h[:, at], ds, 1, 1)
            if i == 0:
                dv_sum, dk_sum = dv, dk
            else:
                dv_sum, dk_sum = dv_sum + dv, dk_sum + dk
        dt[pl.ds(pl.multiple_of(pair + head * HEAD_DIM, HEAD_DIM), HEAD_DIM), :] = (dk_sum * scale).astype(BF16)
        dt[pl.ds(pl.multiple_of(2 * pair + head * HEAD_DIM, HEAD_DIM), HEAD_DIM), :] = dv_sum.astype(BF16)

        @pl.when(head == 1)
        def _():
            d = dt[...]
            part = mm(a1t[...], d, 1, 1).astype(BF16)
            for i in range(3):
                grads[ff_steps + j, i * width : (i + 1) * width, :] = part[:, i * pair : (i + 1) * pair]
            total = mm(jnp.ones((8, slots), BF16), d, 1, 1)
            vec[pl.ds(VEC_Q * cols_of + j, 1), :] = total[:1, :pair]
            vec[pl.ds(VEC_V * cols_of + j, 1), :] = total[:1, 2 * pair :]
            w = jnp.concatenate([wq[...], wk[...], wv[...]], 1)
            dacc[...] += mm(d.T, w, 1, 1)

    @pl.when(step == heads_to - 1)
    def _():
        totals = [jnp.zeros((1, width), F32) for _ in range(2)]
        for r in range(blk):
            at = slice(r * chunk, (r + 1) * chunk)
            grad = dacc[at, :]
            hat, sc = norm_parts(x0[at, :])
            dn = norm_back(grad, hat, sc, gain_one[...].astype(F32))
            din_s[at, :] = (x1[at, :] + dn).astype(BF16)
            for i, value in enumerate((grad * hat, grad)):
                totals[i] = totals[i] + jnp.sum(value, 0, keepdims=True)
        moves_wait(out_s, out, 0)
        for c in moves(din_s, din, 1):
            c.start()
        put_vec(VEC_G1, totals[0])
        put_vec(VEC_B1, totals[1])

    def vec_copy(b):
        bit = (f // (1 << b)) % 2
        return pltpu.make_async_remote_copy(
            src_ref=vec,
            dst_ref=vec_recv.at[b],
            send_sem=vec_sems.at[0, b],
            recv_sem=vec_sems.at[1, b],
            device_id=(f + (1 << b) * (1 - 2 * bit), z),
            device_id_type=pl.DeviceIdType.MESH,
        )

    def vec_blk_copy(s):
        return pltpu.make_async_remote_copy(
            src_ref=vec,
            dst_ref=vec_recv_blk.at[s - 1],
            send_sem=vec_blk_sems.at[0, s - 1],
            recv_sem=vec_blk_sems.at[1, s - 1],
            device_id=(f, (z + s) % blk),
            device_id_type=pl.DeviceIdType.MESH,
        )

    for b in range(bits + 2):

        @pl.when(step == heads_to + b)
        def _():
            if 1 <= b <= bits:
                vec_copy(b - 1).wait()
                vec[...] += vec_recv[b - 1]
            if b < bits:
                vec_copy(b).start()
            elif b == bits:
                for s in range(1, blk):
                    vec_blk_copy(s).start()
            else:
                for s in range(1, blk):
                    vec_blk_copy(s).wait()
                total = vec[...]
                for s in range(1, blk):
                    total = total + vec_recv_blk[s - 1]
                vec_out[...] = total

    @pl.when(step == heads_to + tail - 1)
    def _():
        moves_wait(din_s, din, 1)

        @pl.loop(0, ff_steps)
        def _(block):
            for c in feed_copies(block):
                c.wait()

        @pl.loop(ff_steps, ff_steps + pairs)
        def _(block):
            for c in proj_copies(block):
                c.wait()


def mega(mesh_shape, count, ot, x0, y, w_out, b_out, gain_two, bias_two, up, up_bias, down, down_bias,
         qt, k, kt, v, lse, a1t, w_qkv, gain_one, ff_block=256):
    fields, blk = mesh_shape
    slots, width = x0.shape
    pair = 2 * HEAD_DIM
    pairs = width // pair
    ff_steps = up.shape[1] // ff_block
    bits = fields.bit_length() - 1
    n = fields * blk
    rows = 2 * ff_block // LANES * width
    rows = -(-rows // (16 * n)) * 16 * n
    blocks = ff_steps + pairs
    last_tick = blocks - 1 + 2 * bits + 2
    heads_to = ff_steps + 2 * pairs
    tail = max(last_tick - (2 * heads_to - 2) // 3 + 1, bits + 2)
    vec_rows = (8 + up.shape[1] // width) * (width // LANES)
    chunk = slots // blk
    cols_of = width // LANES

    def ff_at(i):
        return jnp.minimum(i, ff_steps - 1)

    def pair_at(i):
        return jnp.clip((i - ff_steps) // 2, 0, pairs - 1)

    tra = pl.BlockSpec((pair, slots), lambda i: (pair_at(i), 0))
    nat = pl.BlockSpec((slots, pair), lambda i: (0, pair_at(i)))

    def cols(part):
        return pl.BlockSpec((width, pair), lambda i: (0, part * pairs + pair_at(i)))

    hbm = pl.BlockSpec(memory_space=pl.ANY)
    one = (1, width)
    dma = pltpu.SemaphoreType.DMA
    ahead = SLOTS_AHEAD
    flops = 12 * slots * width * up.shape[1] + 10 * slots * slots * width + 12 * slots * width * width
    return pl.pallas_call(
        partial(mega_kernel, fields, blk, rows, ff_steps, pairs, tail),
        grid=(heads_to + tail,),
        in_specs=[
            pl.BlockSpec(memory_space=pltpu.SMEM),
            whole((width, slots)),
            whole((slots, width)),
            whole((slots, width)),
            whole((width, width)),
            whole(one),
            whole(one),
            whole(one),
            pl.BlockSpec((width, ff_block), lambda i: (0, ff_at(i))),
            pl.BlockSpec((1, ff_block), lambda i: (0, ff_at(i))),
            pl.BlockSpec((ff_block, width), lambda i: (ff_at(i), 0)),
            whole(one),
            tra, nat, tra, nat,
            pl.BlockSpec((1, 2, slots), lambda i: (pair_at(i), 0, 0)),
            whole((width, slots)),
            cols(0), cols(1), cols(2),
            whole(one),
        ],
        out_specs=[hbm, hbm, hbm, hbm, hbm, hbm, whole((vec_rows, LANES))],
        out_shape=[
            jax.ShapeDtypeStruct((blk, chunk, width), BF16),
            jax.ShapeDtypeStruct((blk, chunk, width), BF16),
            jax.ShapeDtypeStruct((width, up.shape[1]), BF16),
            jax.ShapeDtypeStruct((up.shape[1], width), BF16),
            jax.ShapeDtypeStruct((width, 3 * width), BF16),
            jax.ShapeDtypeStruct((width, width), BF16),
            jax.ShapeDtypeStruct((vec_rows, LANES), F32),
        ],
        scratch_shapes=[
            pltpu.VMEM((slots, width), F32),
            pltpu.VMEM((slots, width), BF16),
            pltpu.VMEM((width, slots), BF16),
            pltpu.VMEM((slots, width), F32),
            pltpu.VMEM((slots, width), F32),
            pltpu.VMEM((slots, width), BF16),
            pltpu.VMEM((width, slots), BF16),
            pltpu.VMEM((3 * pair, slots), BF16),
            pltpu.VMEM((slots, width), BF16),
            pltpu.VMEM((blocks, rows, LANES), BF16),
            pltpu.VMEM((vec_rows, LANES), F32),
            pltpu.VMEM((ahead, blk - 1, rows // n, LANES), BF16),
            pltpu.VMEM((bits, vec_rows, LANES), F32),
            pltpu.VMEM((blk - 1, vec_rows, LANES), F32),
            dma((bits, ahead)),
            dma((bits, ahead)),
            dma((bits, ahead)),
            dma((bits, ahead)),
            dma((2, 2, blk - 1, ahead)),
            dma((2, bits)),
            dma((2, blk - 1)),
            dma((2, 2, blk)),
            dma((blocks, 2 * cols_of)),
            pltpu.SemaphoreType.REGULAR((bits, blocks)),
            pltpu.SemaphoreType.REGULAR((blk - 1, blocks)),
            *[pltpu.VMEM((ahead, rows >> (s + 1), LANES), BF16) for s in range(bits)],
        ],
        compiler_params=pltpu.CompilerParams(
            vmem_limit_bytes=67_000_000, collective_id=0, has_side_effects=True
        ),
        cost_estimate=pl.CostEstimate(flops=flops, bytes_accessed=60 * slots * width, transcendentals=0),
        name="mega",
    )(
        count, ot, x0, y, w_out, b_out[None], gain_two[None], bias_two[None], up, up_bias[None], down, down_bias[None],
        qt, k, kt, v, lse, a1t, w_qkv, w_qkv, w_qkv, gain_one[None],
    )


def tables(width):
    quarter = width // 4
    omega = 1.0 / 10000.0 ** (jnp.arange(quarter).astype(F32) / quarter)

    def table(length):
        ang = jnp.arange(length).astype(F32)[:, None] * omega
        return jnp.concatenate([jnp.sin(ang), jnp.cos(ang)], -1)

    return table(2048 // GRID_W), table(GRID_W)


def to_field(part):
    return lax.all_to_all(part, "blk", 0, 1, tiled=True)[0]


def per_device(
    mesh_shape, tokens, keep_index, counts, norm1_gain, norm1_bias, qkv_weight, query_bias, value_bias, out_weight,
    out_bias, norm2_gain, norm2_bias, up_weight, up_bias, down_weight, down_bias, cotangent,
):
    width = tokens.shape[2]
    count = lax.dynamic_slice(counts, (lax.axis_index("blk"),), (1,))[None]
    x0, a1t, qt, k, kt, v, vt = project(
        to_field(tokens), to_field(keep_index), tables(width), norm1_gain, norm1_bias, qkv_weight, query_bias, value_bias
    )
    y = to_field(cotangent)
    _, ot, lse = attend(count, qt, k, vt)
    output, input_grad, d_up, d_down, d_qkv, d_out, vecs = mega(
        mesh_shape, count, ot, x0, y, out_weight, out_bias, norm2_gain, norm2_bias, up_weight, up_bias, down_weight,
        down_bias, qt, k, kt, v, lse, a1t, qkv_weight, norm1_gain,
    )
    vec = vecs.reshape(-1, width)
    return (
        output,
        input_grad,
        vec[0],
        vec[1],
        d_qkv.astype(F32),
        vec[2],
        vec[3],
        d_out.astype(F32),
        vec[4],
        vec[5],
        vec[6],
        d_up.astype(F32),
        vec[8:].reshape(-1),
        d_down.astype(F32),
        vec[7],
    )


def solution(mesh):
    rows = P("fields", "blk", None)
    return jax.shard_map(
        partial(per_device, (mesh.shape["fields"], mesh.shape["blk"])),
        mesh=mesh,
        in_specs=(rows, P("fields", "blk"), P("fields"), *[P()] * 13, rows),
        out_specs=(rows, rows, *[P()] * 13),
        check_vma=False,
    )
```

time: 587 us -> 402 us (0.68)
  waiting for transfers between devices: 224 us -> 35.6 us
  Pallas kernels: 160 us -> 311 us
  blocking collectives: 83.8 us -> 11.7 us
  other arithmetic: 42.6 us -> 19 us
  local copies, waits for them, and re-layouts: 38.7 us -> 15.2 us
  between operations: 14.8 us -> 0.81 us
  starting transfers between devices: 16.5 us -> 7.92 us
    psum x1 -> x0, waiting for transfers between devices: 154 us -> none  [per_device(): dwq, dwk, dwv = lax.psum((dwq, dwk, dwv), both)]
    pallas_call x2 -> x1, Pallas kernels: 110 us -> 261 us  [mega(): pl.pallas_call(partial(mega_kernel, fields, blk, rows, ff_steps, pairs, t...]
    psum x1 -> x0, blocking collectives: 72.1 us -> none  [per_device(): vecs = lax.psum(vecs, both)]
    all_to_all x2 -> x0, waiting for transfers between devices: 35.2 us -> none  [to_slots(): return lax.all_to_all(whole_field[None], 'blk', 1, 0, tiled=True)]
    unnamed x2 -> x0, other arithmetic: 23.2 us -> none
    unnamed x49 -> x34, local copies, waits for them, and re-layouts: 20.5 us -> 4.87 us
    all_to_all x2 -> x0, starting transfers between devices: 9.33 us -> none  [to_slots(): return lax.all_to_all(whole_field[None], 'blk', 1, 0, tiled=True)]
    broadcast_in_dim x7 -> x5, local copies, waits for them, and re-layouts: 10.6 us -> 2.93 us  [the longest x1 0.61 us: mega(): up_bias[None]]
  transfers between devices with their start and end apart: 5 -> 2, of which waited for: 3 -> 1; matrix products, arithmetic and copies ran while one was open for 10% -> 2% of each run, Pallas kernels for 9% -> 12%
where the time goes in v2:
time: 402 us; the launch traced here: 401 us
  Pallas kernels  311 us (77%)
  waiting for transfers between devices  35.6 us (9%)
  other arithmetic  19 us (5%)
  local copies, waits for them, and re-layouts  15.2 us (4%)
  blocking collectives  11.7 us (3%)
  starting transfers between devices  7.92 us (2%)
    pallas_call x1, Pallas kernels, mega(): pl.pallas_call(partial(mega_kernel, fields, blk, rows, ff_steps, pairs, t...  261 us
    pallas_call x1, Pallas kernels, attend(): pl.pallas_call(partial(attend_kernel, block), grid=(pairs,), in_specs=[pl...  36.9 us
    all_to_all x2, waiting for transfers between devices, to_field(): return lax.all_to_all(part, 'blk', 0, 1, tiled=True)[0]  35.6 us
    pallas_call x1, Pallas kernels, project(): pl.pallas_call(project_kernel, grid=(slots // block,), in_specs=[nat, pl....  13 us
    all_to_all x1, blocking collectives, to_field(): return lax.all_to_all(part, 'blk', 0, 1, tiled=True)[0]  11.7 us
  transfers between devices with their start and end apart: 2, of which 1 were waited for; matrix products, arithmetic and copies ran while one was open for 2% of the time, Pallas kernels for 12%

profile of v2, /device:TPU:0, one launch (start us, length us, event | category | flops | bytes accessed | tf_op | source)
XLA Modules:
  0.0 401.2 jit_solution(4927389072954098954)
XLA Ops:
  0.6 0.7 all_to_all.10
  1.3 11.7 %all_to_all.31 = s32[4,1,256]{2,1,0:T(1,128)S(1)} all-to-all(s32[4,1,256]{2,1,0:T(1,128)S(1)} %all_to_all.10), channel_id=1, replica_groups=mesh['fields'=8,'blk'=4] {'blk'}, dimensions={0} | all-to-all | bytes 8192 | tf_op jit(solution)/shard_map/all_to_all | solution.py:772
  13.0 3.6 all-to-all-start
  16.6 0.0 copy-start.7
  16.6 0.0 copy-start.8
  16.6 0.0 copy-start.9
  16.6 0.0 copy-start.10
  16.6 0.0 copy-start.6
  16.7 0.0 copy-start.11
  16.7 0.0 copy-start.12
  16.7 0.0 copy-start.13
  16.7 0.0 copy-start.14
  16.7 0.0 copy-start.15
  16.7 35.6 %all-to-all-done = bf16[4,256,768]{2,1,0:T(8,128)(2,1)S(1)} async-done(((bf16[4,256,768]{2,1,0:T(8,128)(2,1)}), bf16[4,256,768]{2,1,0:T(8,128)(2,1)S(1)}, u32[]{:S(2)}, u32[]{:S(2)}) %all-to-all-start) | async-done | bytes 1572896 | tf_op jit(solution)/shard_map/all_to_all | solution.py:772
  52.4 1.1 copy-done.2
  53.5 4.4 %all-to-all-start.2 = ((bf16[4,256,768]{2,1,0:T(8,128)(2,1)}), bf16[4,256,768]{2,1,0:T(8,128)(2,1)}, u32[]{:S(2)}, u32[]{:S(2)}) async-start(bf16[4,256,768]{2,1,0:T(8,128)(2,1)} %param.33), calls=%async_computation.2 | async-start | bytes 3145728 | tf_op jit(solution)/shard_map/all_to_all | solution.py:772
  57.9 0.0 copy-done.7
  57.9 0.6 broadcast_in_dim.36.gain.gain_one
  58.5 0.6 broadcast_in_dim.37.bias
  59.1 0.6 broadcast_in_dim.38.qb
  59.7 0.6 broadcast_in_dim.39.vb
  60.2 0.0 copy-done.6
  60.2 0.6 broadcast_in_dim.43.up_bias
  60.8 0.6 broadcast_in_dim.40.b_out
  61.4 0.6 broadcast_in_dim.41.gain_two
  62.0 0.0 copy-done.13
  62.0 0.6 broadcast_in_dim.42.bias_two
  62.6 0.6 broadcast_in_dim.44.down_bias
  63.2 0.6 dynamic_slice.3
  63.8 0.2 multiply_sine_fusion.1
  64.0 0.7 pad_maximum_fusion.1.row_table
  64.7 0.3 multiply_sine_fusion
  65.0 0.7 pad_maximum_fusion.col_table
  65.7 1.0 copy.33.keep
  66.8 13.0 %project.1 = (f32[1024,768]{1,0:T(8,128)}, bf16[768,1024]{1,0:T(8,128)(2,1)}, bf16[768,1024]{1,0:T(8,128)(2,1)}, bf16[1024,768]{1,0:T(8,128)(2,1)}, bf16[768,102...) custom-call(bf16[1024,768]{1,0:T(8,128)(2,1)} %bitcast.22, s32[1024,1]{1,0:T(8,128)} %copy.33.keep, ...), custom_call_target="tpu_custom_call" | custom-call | flops 3623878656 | bytes 15728640 | tf_op jit(solution)/shard_map/project/pallas_call | solution.py:84
  79.7 36.9 %attend.1 = (bf16[1024,768]{1,0:T(8,128)(2,1)}, bf16[768,1024]{1,0:T(8,128)(2,1)}, f32[6,2,1024]{2,1,0:T(2,128)}) custom-call(s32[1,1]{1,0:T(1,128)} %bitcast.count, bf16[768,1024]{1,0:T(8,128)(2,1)} %get-tuple-element.31.qt, bf16[1024,768]{1,0:T(8,128)(2,1)} %get-tuple-element.32.k, bf16[768,1024]{1,0:T(8,128)(2,1)} %get-tuple-element.33.vt), custom_call_target="tpu_custom_call" | custom-call | flops 12884901888 | bytes 9437184 | tf_op jit(solution)/shard_map/attend/pallas_call | solution.py:153
  116.6 0.0 all-to-all-done.2
  116.6 261.1 %mega.1 = (bf16[4,256,768]{2,1,0:T(8,128)(2,1)}, bf16[4,256,768]{2,1,0:T(8,128)(2,1)}, bf16[768,3072]{1,0:T(8,128)(2,1)}, bf16[3072,768]{1,0:T(8,128)(2,1)}, bf1...) custom-call(s32[1,1]{1,0:T(1,128)} %bitcast.count, bf16[768,1024]{1,0:T(8,128)(2,1)} %get-tuple-element.34.ot, ...), custom_call_target="tpu_custom_call" | custom-call | flops 44291850240 | bytes 47185920 | tf_op jit(solution)/shard_map/mega/pallas_call | solution.py:689
  377.8 1.4 slice_bitcast_fusion.1
  379.2 1.3 slice_bitcast_fusion
  380.5 7.5 %convert_element_type.48 = f32[768,3072]{1,0:T(8,128)} convert(bf16[768,3072]{1,0:T(8,128)(2,1)} %get-tuple-element.45) | non-fusion elementwise | flops 2359296 | bytes 14155776 | tf_op jit(solution)/shard_map/convert_element_type | solution.py:803
  388.0 4.5 %convert_element_type.49 = f32[3072,768]{1,0:T(8,128)} convert(bf16[3072,768]{1,0:T(8,128)(2,1)S(1)} %copy-done) | non-fusion elementwise | flops 2359296 | bytes 14155776 | tf_op jit(solution)/shard_map/convert_element_type | solution.py:805
  392.5 3.5 convert_element_type.46
  396.0 1.6 convert_element_type.47
  397.5 0.5 copy-done.4
  398.1 1.1 copy.36
  399.2 0.8 copy-done.3
  400.1 1.1 copy.37
  (19 shorter events, 0.0 us)
Async XLA Ops:
  13.0 39.3 %all-to-all-start = ((bf16[4,256,768]{2,1,0:T(8,128)(2,1)}), bf16[4,256,768]{2,1,0:T(8,128)(2,1)S(1)}, u32[]{:S(2)}, u32[]{:S(2)}) async-start(bf16[4,256,768]{2,1,0:T(8,128)(2,1)} %param.17), calls=%async_computation | async-start | bytes 3145728 | tf_op jit(solution)/shard_map/all_to_all | solution.py:772
  16.6 41.3 %copy-start.7 = (bf16[768]{0:T(1024)(128)(2,1)S(1)}, bf16[768]{0:T(1024)(128)(2,1)}, u32[]{:S(2)}) copy-start(bf16[768]{0:T(1024)(128)(2,1)} %param.20) | copy-start | bytes 4612
  16.6 41.9 %copy-start.8 = (bf16[768]{0:T(1024)(128)(2,1)S(1)}, bf16[768]{0:T(1024)(128)(2,1)}, u32[]{:S(2)}) copy-start(bf16[768]{0:T(1024)(128)(2,1)} %param.21) | copy-start | bytes 4612
  16.6 42.4 %copy-start.9 = (bf16[768]{0:T(1024)(128)(2,1)S(1)}, bf16[768]{0:T(1024)(128)(2,1)}, u32[]{:S(2)}) copy-start(bf16[768]{0:T(1024)(128)(2,1)} %param.23) | copy-start | bytes 4612
  16.6 43.0 %copy-start.10 = (bf16[768]{0:T(1024)(128)(2,1)S(1)}, bf16[768]{0:T(1024)(128)(2,1)}, u32[]{:S(2)}) copy-start(bf16[768]{0:T(1024)(128)(2,1)} %param.24) | copy-start | bytes 4612
  16.6 43.6 %copy-start.6 = (bf16[3072]{0:T(1024)(128)(2,1)S(1)}, bf16[3072]{0:T(1024)(128)(2,1)}, u32[]{:S(2)}) copy-start(bf16[3072]{0:T(1024)(128)(2,1)} %param.30) | copy-start | bytes 18436
  16.7 44.2 %copy-start.11 = (bf16[768]{0:T(1024)(128)(2,1)S(1)}, bf16[768]{0:T(1024)(128)(2,1)}, u32[]{:S(2)}) copy-start(bf16[768]{0:T(1024)(128)(2,1)} %param.26) | copy-start | bytes 4612
  16.7 44.8 %copy-start.12 = (bf16[768]{0:T(1024)(128)(2,1)S(1)}, bf16[768]{0:T(1024)(128)(2,1)}, u32[]{:S(2)}) copy-start(bf16[768]{0:T(1024)(128)(2,1)} %param.27) | copy-start | bytes 4612
  16.7 45.3 %copy-start.13 = (bf16[768]{0:T(1024)(128)(2,1)S(1)}, bf16[768]{0:T(1024)(128)(2,1)}, u32[]{:S(2)}) copy-start(bf16[768]{0:T(1024)(128)(2,1)} %param.28) | copy-start | bytes 4612
  16.7 45.9 %copy-start.14 = (bf16[768]{0:T(1024)(128)(2,1)S(1)}, bf16[768]{0:T(1024)(128)(2,1)}, u32[]{:S(2)}) copy-start(bf16[768]{0:T(1024)(128)(2,1)} %param.32) | copy-start | bytes 4612
  16.7 46.5 %copy-start.15 = (s32[4]{0:T(128)S(1)}, s32[4]{0:T(128)}, u32[]{:S(2)}) copy-start(s32[4]{0:T(128)} %param.19) | copy-start | bytes 52
  52.4 1.1 copy-start.2
  53.5 63.1 %all-to-all-start.2 = ((bf16[4,256,768]{2,1,0:T(8,128)(2,1)}), bf16[4,256,768]{2,1,0:T(8,128)(2,1)}, u32[]{:S(2)}, u32[]{:S(2)}) async-start(bf16[4,256,768]{2,1,0:T(8,128)(2,1)} %param.33), calls=%async_computation.2 | async-start | bytes 3145728 | tf_op jit(solution)/shard_map/all_to_all | solution.py:772
  380.5 7.5 %copy-start = (bf16[3072,768]{1,0:T(8,128)(2,1)S(1)}, bf16[3072,768]{1,0:T(8,128)(2,1)}, u32[]{:S(2)}) copy-start(bf16[3072,768]{1,0:T(8,128)(2,1)} %get-tuple-element.46) | copy-start | bytes 14155780
  388.0 4.5 %copy-start.1 = (bf16[768,2304]{1,0:T(8,128)(2,1)S(1)}, bf16[768,2304]{1,0:T(8,128)(2,1)}, u32[]{:S(2)}) copy-start(bf16[768,2304]{1,0:T(8,128)(2,1)} %get-tuple-element.43) | copy-start | bytes 10616836
  392.5 3.5 copy-start.5
  396.0 2.1 copy-start.4
  398.1 2.0 copy-start.3

commit v3 on v2

--- a/solution.py
+++ b/solution.py
@@ -166,182 +166,87 @@
     )(count, qt, k, vt)
 
 
-SLOTS_AHEAD = 4
+SLOTS_AHEAD = 8
+LAG = 2
 LANES = 128
 
 
 class Sums:
-    def __init__(self, fields, blk, rows, count, grads, recv, recv_blk, sems, free, free_blk):
-        self.fields, self.blk, self.rows, self.count = fields, blk, rows, count
-        self.bits = fields.bit_length() - 1
-        self.grads, self.recv, self.recv_blk = grads, recv, recv_blk
-        self.free, self.free_blk = free, free_blk
-        self.send_rs, self.recv_rs, self.send_ag, self.recv_ag, self.blk_sems = sems
+    def __init__(self, fields, blk, rows, count, grads, recv, sems):
+        self.rows, self.count = rows, count
+        self.near, self.far = fields.bit_length() - 1, blk.bit_length() - 1
+        self.bits = self.near + self.far
+        self.grads, self.recv = grads, recv
+        self.send_rs, self.recv_rs, self.send_ag, self.recv_ag = sems
         self.f, self.z = lax.axis_index("fields"), lax.axis_index("blk")
-        self.actions = 2 * self.bits + 3
-
-    def weight(self, block, stage):
-        even = 1 << stage
-        odd = 1 << (stage if stage == 0 else self.bits - stage)
-        odd_block = block % 2
-        bit_even, bit_odd = (self.f // even) % 2, (self.f // odd) % 2
-        bit = bit_even + odd_block * (bit_odd - bit_even)
-        width = even + odd_block * (odd - even)
-        return bit, self.f + width * (1 - 2 * bit)
-
-    def start(self, block, stage):
-        off = 0
-        for k in range(stage):
-            bit, _ = self.weight(block, k)
-            off = off + bit * (self.rows >> (k + 1))
-        return off
-
-    def area(self, block, off, size):
-        return self.grads.at[block, pl.ds(pl.multiple_of(off, 16), size)]
-
-    def scatter_copy(self, block, stage):
-        bit, partner = self.weight(block, stage)
-        size = self.rows >> (stage + 1)
-        off = self.start(block, stage) + (1 - bit) * size
-        slot = block % SLOTS_AHEAD
+        self.actions = 2 * self.bits + 1
+        self.own = [lax.rem(lax.div(self.f, 1 << k), 2) for k in range(self.near)]
+        self.own += [lax.rem(lax.div(self.z, 1 << k), 2) for k in range(self.far)]
+
+    def route(self, odd):
+        keep, route = 0, []
+        for stage in range(self.bits):
+            bit = self.own[stage]
+            if stage < self.near:
+                other = stage if stage == 0 else self.near - stage
+                bit = bit + odd * (self.own[other] - bit)
+                width = (1 << stage) + odd * ((1 << other) - (1 << stage))
+                partner = (self.f + width * (1 - 2 * bit), self.z)
+            else:
+                partner = (self.f, self.z + (1 << (stage - self.near)) * (1 - 2 * bit))
+            size = self.rows >> (stage + 1)
+            route.append((partner, keep + bit * size, keep + (1 - bit) * size))
+            keep = keep + bit * size
+        return route
+
+    def copy(self, gather, block, slot, route, stage):
+        partner, kept, sent = route[stage]
+        part = pl.ds(pl.multiple_of(kept if gather else sent, 16), self.rows >> (stage + 1))
+        send, recv = (self.send_ag, self.recv_ag) if gather else (self.send_rs, self.recv_rs)
         return pltpu.make_async_remote_copy(
-            src_ref=self.area(block, off, size),
-            dst_ref=self.recv[stage].at[slot],
-            send_sem=self.send_rs.at[stage, slot],
-            recv_sem=self.recv_rs.at[stage, slot],
-            device_id=(partner, self.z),
+            src_ref=self.grads.at[block, part],
+            dst_ref=self.recv[stage].at[gather, slot],
+            send_sem=send.at[stage, slot],
+            recv_sem=recv.at[stage, slot],
+            device_id=partner,
             device_id_type=pl.DeviceIdType.MESH,
         )
 
-    def gather_copy(self, block, stage):
-        _, partner = self.weight(block, stage)
-        part = self.area(block, self.start(block, stage + 1), self.rows >> (stage + 1))
-        slot = block % SLOTS_AHEAD
-        return pltpu.make_async_remote_copy(
-            src_ref=part,
-            dst_ref=part,
-            send_sem=self.send_ag.at[stage, slot],
-            recv_sem=self.recv_ag.at[stage, slot],
-            device_id=(partner, self.z),
-            device_id_type=pl.DeviceIdType.MESH,
-        )
-
-    def gather_wait(self, block, stage):
-        self.gather_copy(block, stage).wait_send()
-        bit, partner = self.weight(block, stage)
+    def take(self, gather, block, slot, route, stage):
         size = self.rows >> (stage + 1)
-        part = self.area(block, self.start(block, stage) + (1 - bit) * size, size)
-        slot = block % SLOTS_AHEAD
-        pltpu.make_async_remote_copy(
-            src_ref=part,
-            dst_ref=part,
-            send_sem=self.send_ag.at[stage, slot],
-            recv_sem=self.recv_ag.at[stage, slot],
-            device_id=(partner, self.z),
-            device_id_type=pl.DeviceIdType.MESH,
-        ).wait_recv()
-
-    def blk_copy(self, block, step, kind):
-        size = self.rows // (self.fields * self.blk)
-        to = (self.z + step) % self.blk
-        base = self.start(block, self.bits)
-        slot = block % SLOTS_AHEAD
-        if kind == 0:
-            src = self.area(block, base + to * size, size)
-            dst = self.recv_blk.at[slot, step - 1]
-        else:
-            src = self.area(block, base + self.z * size, size)
-            dst = src
-        return pltpu.make_async_remote_copy(
-            src_ref=src,
-            dst_ref=dst,
-            send_sem=self.blk_sems.at[kind, 0, step - 1, slot],
-            recv_sem=self.blk_sems.at[kind, 1, step - 1, slot],
-            device_id=(self.f, to),
-            device_id_type=pl.DeviceIdType.MESH,
-        )
-
-    def blk_gather_wait(self, block, step):
-        self.blk_copy(block, step, 1).wait_send()
-        size = self.rows // (self.fields * self.blk)
-        came = (self.z + self.blk - step) % self.blk
-        slot = block % SLOTS_AHEAD
-        part = self.area(block, self.start(block, self.bits) + came * size, size)
-        pltpu.make_async_remote_copy(
-            src_ref=part,
-            dst_ref=part,
-            send_sem=self.blk_sems.at[1, 0, step - 1, slot],
-            recv_sem=self.blk_sems.at[1, 1, step - 1, slot],
-            device_id=(self.f, came),
-            device_id_type=pl.DeviceIdType.MESH,
-        ).wait_recv()
-
-    def add(self, block, off, size, take):
+        off = route[stage][2 if gather else 1]
         chunk = size
-        while chunk > 256 or size % chunk:
+        while chunk > 384 or size % chunk:
             chunk -= 16
+        came = self.recv[stage]
 
         @pl.loop(0, size // chunk)
         def _(i):
             at = pl.ds(pl.multiple_of(off + i * chunk, 16), chunk)
-            self.grads[block, at, :] = take(self.grads[block, at, :], pl.ds(pl.multiple_of(i * chunk, 16), chunk))
-
-    def act(self, kind, block):
+            got = came[gather, slot, pl.ds(pl.multiple_of(i * chunk, 16), chunk), :]
+            self.grads[block, at, :] = got if gather else self.grads[block, at, :] + got
+
+    def act(self, kind, block, slot, route):
         bits = self.bits
-        slot = block % SLOTS_AHEAD
-        if 1 <= kind <= bits:
-            stage = kind - 1
-            self.scatter_copy(block, stage).wait()
-            _, partner = self.weight(block, stage)
-            pl.semaphore_signal(
-                self.free.at[stage, block], 1, device_id=(partner, self.z), device_id_type=pl.DeviceIdType.MESH
-            )
-            got = self.recv[stage]
-            self.add(block, self.start(block, stage + 1), self.rows >> (stage + 1), lambda a, at: a + got[slot, at, :])
-        if kind < bits:
-            self.scatter_copy(block, kind).start()
-        elif kind == bits:
-            for step in range(1, self.blk):
-                self.blk_copy(block, step, 0).start()
-        elif kind == bits + 1:
-            for step in range(1, self.blk):
-                self.blk_copy(block, step, 0).wait()
-                pl.semaphore_signal(
-                    self.free_blk.at[self.blk - step - 1, block],
-                    1,
-                    device_id=(self.f, (self.z + step) % self.blk),
-                    device_id_type=pl.DeviceIdType.MESH,
-                )
-            size = self.rows // (self.fields * self.blk)
-
-            def take(a, at):
-                total = a.astype(F32)
-                for step in range(1, self.blk):
-                    total = total + self.recv_blk[slot, step - 1, at, :].astype(F32)
-                return total.astype(BF16)
-
-            self.add(block, self.start(block, bits) + self.z * size, size, take)
-            for step in range(1, self.blk):
-                pl.semaphore_wait(self.free_blk.at[step - 1, block], 1)
-                self.blk_copy(block, step, 1).start()
-        else:
-            if kind == bits + 2:
-                for step in range(1, self.blk):
-                    self.blk_gather_wait(block, step)
-            else:
-                self.gather_wait(block, 2 * bits + 2 - kind + 1 - 1)
-            stage = 2 * bits + 1 - kind
-            if stage >= 0:
-                pl.semaphore_wait(self.free.at[stage, block], 1)
-                self.gather_copy(block, stage).start()
+        if kind > 0:
+            gather = int(kind > bits)
+            stage = 2 * bits - kind if gather else kind - 1
+            self.copy(gather, block, slot, route, stage).wait()
+            self.take(gather, block, slot, route, stage)
+        if kind < 2 * bits:
+            gather = int(kind >= bits)
+            self.copy(gather, block, slot, route, 2 * bits - 1 - kind if gather else kind).start()
 
     def tick(self, tick, done):
+        assert LAG == 2
+        odd = lax.rem(lax.div(tick, 2), 2)
+        routes = self.route(odd), self.route(1 - odd)
         for kind in range(self.actions):
-            block = tick - kind
+            block = tick - LAG * kind
 
             @pl.when((block >= 0) & (block < self.count))
             def _():
-                self.act(kind, block)
+                self.act(kind, block, lax.rem(block, SLOTS_AHEAD), routes[kind % 2])
                 if kind == self.actions - 1:
                     done(block)
 
@@ -351,8 +256,8 @@
     count, ot, x0, y, w_out, b_out, gain_two, bias_two, up, up_bias, down, down_bias,
     qt, k, kt, v, lse, a1t, wq, wk, wv, gain_one,
     out, din, up_out, down_out, qkv_out, out_out, vec_out,
-    x1, a2, a2t, acc, dacc, out_s, dot_s, dt, din_s, grads, vec, recv_blk, vec_recv, vec_recv_blk,
-    send_rs, recv_rs, send_ag, recv_ag, blk_sems, vec_sems, vec_blk_sems, move_sems, flush_sems, free, free_blk, *recv,
+    x1, a2, a2t, acc, dacc, out_s, dot_s, dt, din_s, grads, vec, vec_recv, vec_recv_blk,
+    send_rs, recv_rs, send_ag, recv_ag, vec_sems, vec_blk_sems, move_sems, piece_sems, flush_sems, *recv,
 ):
     step = pl.program_id(0)
     slots, width = x0.shape
@@ -364,8 +269,7 @@
     ff = up.shape[1]
     heads_from, heads_to = ff_steps, ff_steps + 2 * pairs
     sums = Sums(
-        fields, blk, rows, ff_steps + pairs, grads, recv, recv_blk, (send_rs, recv_rs, send_ag, recv_ag, blk_sems),
-        free, free_blk,
+        fields, blk, rows, 2 * (ff_steps + pairs), grads, recv, (send_rs, recv_rs, send_ag, recv_ag)
     )
     VEC_G1, VEC_B1, VEC_Q, VEC_V, VEC_OUT, VEC_G2, VEC_B2, VEC_DOWN, VEC_UP = range(9)
 
@@ -373,53 +277,50 @@
         for i in range(cols_of):
             vec[index * cols_of + i : index * cols_of + i + 1, :] = value[:, i * LANES : (i + 1) * LANES]
 
-    def moves(src, dst, kind):
-        got = []
-        for s in range(1, blk):
-            to = (z + s) % blk
-            got.append(
-                pltpu.make_async_remote_copy(
-                    src_ref=src.at[pl.ds(pl.multiple_of(to * chunk, 16), chunk)],
-                    dst_ref=dst.at[z],
-                    send_sem=move_sems.at[kind, 0, s],
-                    recv_sem=move_sems.at[kind, 1, s],
-                    device_id=(f, to),
-                    device_id_type=pl.DeviceIdType.MESH,
-                )
-            )
-        got.append(
-            pltpu.make_async_copy(
-                src.at[pl.ds(pl.multiple_of(z * chunk, 16), chunk)], dst.at[z], move_sems.at[kind, 0, 0]
-            )
+    def local_copy(src, dst, sem):
+        return pltpu.make_async_copy(src.at[pl.ds(pl.multiple_of(z * chunk, 16), chunk)], dst.at[z], sem)
+
+    def send_part(src, dst, s, part, size, sems):
+        to = lax.rem(z + s, blk)
+        return pltpu.make_async_remote_copy(
+            src_ref=src.at[pl.ds(pl.multiple_of(to * chunk + part * size, 16), size)],
+            dst_ref=dst.at[z, pl.ds(pl.multiple_of(part * size, 16), size)],
+            send_sem=sems[0],
+            recv_sem=sems[1],
+            device_id=(f, to),
+            device_id_type=pl.DeviceIdType.MESH,
         )
-        return got
-
-    def moves_wait(src, dst, kind):
-        got = moves(src, dst, kind)
-        for c in got[:-1]:
-            c.wait_send()
-        for s in range(1, blk):
-            came = (z + blk - s) % blk
-            pltpu.make_async_remote_copy(
-                src_ref=src.at[pl.ds(0, chunk)],
-                dst_ref=dst.at[came],
-                send_sem=move_sems.at[kind, 0, s],
-                recv_sem=move_sems.at[kind, 1, s],
-                device_id=(f, came),
-                device_id_type=pl.DeviceIdType.MESH,
-            ).wait_recv()
-        got[-1].wait()
+
+    def part_came(src, dst, s, part, size, sems):
+        came = lax.rem(z + blk - s, blk)
+        return pltpu.make_async_remote_copy(
+            src_ref=src.at[pl.ds(0, size)],
+            dst_ref=dst.at[came, pl.ds(pl.multiple_of(part * size, 16), size)],
+            send_sem=sems[0],
+            recv_sem=sems[1],
+            device_id=(f, came),
+            device_id_type=pl.DeviceIdType.MESH,
+        )
+
+    pieces = 2 * pairs // (blk - 1)
+
+    def piece(maker, i):
+        sems = piece_sems.at[0, i], piece_sems.at[1, i]
+        return maker(out_s, out, lax.rem(i, blk - 1) + 1, lax.div(i, blk - 1), chunk // pieces, sems)
+
+    def din_part(maker, s):
+        return maker(din_s, din, s, 0, chunk, (move_sems.at[0, s], move_sems.at[1, s]))
 
     @pl.when(step == 0)
     def _():
         barrier = pltpu.get_barrier_semaphore()
         for b in range(bits):
-            bit = (f // (1 << b)) % 2
+            bit = lax.rem(lax.div(f, 1 << b), 2)
             pl.semaphore_signal(
                 barrier, 1, device_id=(f + (1 << b) * (1 - 2 * bit), z), device_id_type=pl.DeviceIdType.MESH
             )
         for s in range(1, blk):
-            pl.semaphore_signal(barrier, 1, device_id=(f, (z + s) % blk), device_id_type=pl.DeviceIdType.MESH)
+            pl.semaphore_signal(barrier, 1, device_id=(f, lax.rem(z + s, blk)), device_id_type=pl.DeviceIdType.MESH)
         pl.semaphore_wait(barrier, bits + blk - 1)
 
         for r in range(blk):
@@ -433,41 +334,65 @@
         acc[...] = jnp.zeros_like(acc)
         dacc[...] = jnp.zeros_like(dacc)
 
-    def feed_copies(block):
-        base = ff // LANES * width
+    def flush_copies(block, proj):
+        half = lax.rem(block, 2)
         got = []
-        for i in range(ff // LANES):
-            at = pl.ds(pl.multiple_of(block * ff + i * LANES, LANES), LANES)
-            got.append((grads.at[block, pl.ds(i * width, width)], up_out.at[:, at]))
-        at = pl.ds(pl.multiple_of(block * ff, ff), ff)
-        for i in range(cols_of):
-            got.append((grads.at[block, pl.ds(base + i * ff, ff)], down_out.at[at, pl.ds(i * LANES, LANES)]))
-        return [pltpu.make_async_copy(a, b, flush_sems.at[block, i]) for i, (a, b) in enumerate(got)]
-
-    def proj_copies(block):
-        got = []
-        for i in range(4):
-            at = pl.ds(pl.multiple_of((block - ff_steps + (i % 3) * pairs) * pair, pair), pair)
-            got.append((grads.at[block, pl.ds(i * width, width)], (qkv_out if i < 3 else out_out).at[:, at]))
-        return [pltpu.make_async_copy(a, b, flush_sems.at[block, i]) for i, (a, b) in enumerate(got)]
+        if proj:
+            j = lax.div(block, 2) - ff_steps
+            for i in range(2):
+                at = pl.ds(pl.multiple_of((j + i * pairs) * pair, pair), pair)
+                got.append((grads.at[block, pl.ds(i * width, width)], qkv_out.at[:, at]))
+            at = pl.ds(pl.multiple_of((j + 2 * pairs) * pair, pair), pair)
+            more = [(grads.at[block, pl.ds(0, width)], qkv_out.at[:, at])]
+            at = pl.ds(pl.multiple_of(j * pair, pair), pair)
+            more.append((grads.at[block, pl.ds(width, width)], out_out.at[:, at]))
+        else:
+            step_of = lax.div(block, 2)
+            for i in range(ff // LANES):
+                at = pl.ds(pl.multiple_of(step_of * ff + i * LANES, LANES), LANES)
+                got.append((grads.at[block, pl.ds(i * width, width)], up_out.at[:, at]))
+            at = pl.ds(pl.multiple_of(step_of * ff, ff), ff)
+            more = []
+            for i in range(cols_of):
+                more.append((grads.at[block, pl.ds(i * ff, ff)], down_out.at[at, pl.ds(i * LANES, LANES)]))
+        pick = lambda some: [pltpu.make_async_copy(a, b, flush_sems.at[block, i]) for i, (a, b) in enumerate(some)]
+        return half, pick, got, more
+
+    def flush(block, act):
+        for proj in (False, True):
+
+            @pl.when((block >= 2 * ff_steps) if proj else (block < 2 * ff_steps))
+            def _():
+                half, pick, got, more = flush_copies(block, proj)
+
+                @pl.when(half == 0)
+                def _():
+                    for c in pick(got):
+                        act(c)
+
+                @pl.when(half == 1)
+                def _():
+                    for c in pick(more):
+                        act(c)
 
     def done(block):
-        @pl.when(block < ff_steps)
-        def _():
-            for c in feed_copies(block):
-                c.start()
-
-        @pl.when(block >= ff_steps)
-        def _():
-            for c in proj_copies(block):
-                c.start()
-
-    def tick_of(s):
-        return jnp.where(s < heads_to, (2 * s - 2) // 3, (2 * heads_to - 2) // 3 + s - heads_to)
-
-    @pl.when((step >= 1) & (tick_of(step) != tick_of(step - 1)))
+        flush(block, lambda c: c.start())
+
+    ff_ticks = ff_steps - 1 + ff_steps // 3
+    index_of = step - ff_steps
+    in_feed, in_heads = step < ff_steps, step < heads_to
+    first = jnp.where(
+        in_feed,
+        step - 1 + lax.div(step, 3),
+        jnp.where(in_heads, ff_ticks + index_of + lax.div(index_of, 2), ff_ticks + pairs + index_of),
+    )
+    twice = jnp.where(in_feed, lax.rem(step, 3) == 2, in_heads & (lax.rem(index_of, 2) == 1))
+
+    @pl.when(step >= 1)
     def _():
-        sums.tick(tick_of(step), done)
+        @pl.loop(0, jnp.where(twice, 2, 1))
+        def _(i):
+            sums.tick(first + i, done)
 
     @pl.when(step < heads_from)
     def _():
@@ -484,13 +409,13 @@
         dacc[...] += mm(dh, up[...], 1, 1)
         d_up = jnp.dot(a2t[...], dh, preferred_element_type=F32).astype(BF16)
         for i in range(ff // LANES):
-            grads[step, i * width : (i + 1) * width, :] = d_up[:, i * LANES : (i + 1) * LANES]
+            grads[2 * step, i * width : (i + 1) * width, :] = d_up[:, i * LANES : (i + 1) * LANES]
         d_down = jnp.dot(g.T, y[...], preferred_element_type=F32).astype(BF16)
-        base = ff // LANES * width
         for i in range(cols_of):
-            grads[step, base + i * ff : base + (i + 1) * ff, :] = d_down[:, i * LANES : (i + 1) * LANES]
-        if 2 * base < rows:
-            grads[step, 2 * base :, :] = jnp.zeros((rows - 2 * base, LANES), BF16)
+            grads[2 * step + 1, i * ff : (i + 1) * ff, :] = d_down[:, i * LANES : (i + 1) * LANES]
+        if 2 * width < rows:
+            for i in range(2):
+                grads[2 * step + i, 2 * width :, :] = jnp.zeros((rows - 2 * width, LANES), BF16)
 
     @pl.when(step == heads_from - 1)
     def _():
@@ -509,21 +434,26 @@
             dot_s[:, at] = mm(dz, w_out[...], 1, 1).astype(BF16).T
             for i, value in enumerate((grad * hat, grad, yf, dz.astype(F32))):
                 totals[i] = totals[i] + jnp.sum(value, 0, keepdims=True)
-        for c in moves(out_s, out, 0):
-            c.start()
+        local_copy(out_s, out, move_sems.at[0, 0]).start()
         for index, value in zip((VEC_G2, VEC_B2, VEC_DOWN, VEC_OUT), totals):
             put_vec(index, value)
         d_out = jnp.dot(ot[...], a2[...], preferred_element_type=F32).astype(BF16)
         for j in range(pairs):
-            grads[ff_steps + j, 3 * width : 4 * width, :] = d_out[:, j * pair : (j + 1) * pair]
-            if 4 * width < rows:
-                grads[ff_steps + j, 4 * width :, :] = jnp.zeros((rows - 4 * width, LANES), BF16)
+            grads[2 * (ff_steps + j) + 1, width : 2 * width, :] = d_out[:, j * pair : (j + 1) * pair]
+            if 2 * width < rows:
+                for i in range(2):
+                    grads[2 * (ff_steps + j) + i, 2 * width :, :] = jnp.zeros((rows - 2 * width, LANES), BF16)
         dacc[...] = jnp.zeros_like(dacc)
 
     @pl.when((step >= heads_from) & (step < heads_to))
     def _():
         index = step - heads_from
-        j, head = index // 2, index % 2
+        j, head = lax.div(index, 2), lax.rem(index, 2)
+
+        @pl.when(index < pieces * (blk - 1))
+        def _():
+            piece(send_part, index).start()
+
         c = HEAD_DIM**-0.5 * LOG2E
         scale = HEAD_DIM**-0.5
         block = 256
@@ -570,14 +500,15 @@
             d = dt[...]
             part = mm(a1t[...], d, 1, 1).astype(BF16)
             for i in range(3):
-                grads[ff_steps + j, i * width : (i + 1) * width, :] = part[:, i * pair : (i + 1) * pair]
+                at = slice(i % 2 * width, (i % 2 + 1) * width)
+                grads[2 * (ff_steps + j) + i // 2, at, :] = part[:, i * pair : (i + 1) * pair]
             total = mm(jnp.ones((8, slots), BF16), d, 1, 1)
             vec[pl.ds(VEC_Q * cols_of + j, 1), :] = total[:1, :pair]
             vec[pl.ds(VEC_V * cols_of + j, 1), :] = total[:1, 2 * pair :]
             w = jnp.concatenate([wq[...], wk[...], wv[...]], 1)
             dacc[...] += mm(d.T, w, 1, 1)
 
-    @pl.when(step == heads_to - 1)
+    @pl.when(step == heads_to)
     def _():
         totals = [jnp.zeros((1, width), F32) for _ in range(2)]
         for r in range(blk):
@@ -588,14 +519,14 @@
             din_s[at, :] = (x1[at, :] + dn).astype(BF16)
             for i, value in enumerate((grad * hat, grad)):
                 totals[i] = totals[i] + jnp.sum(value, 0, keepdims=True)
-        moves_wait(out_s, out, 0)
-        for c in moves(din_s, din, 1):
-            c.start()
+        for s in range(1, blk):
+            din_part(send_part, s).start()
+        local_copy(din_s, din, move_sems.at[1, 0]).start()
         put_vec(VEC_G1, totals[0])
         put_vec(VEC_B1, totals[1])
 
     def vec_copy(b):
-        bit = (f // (1 << b)) % 2
+        bit = lax.rem(lax.div(f, 1 << b), 2)
         return pltpu.make_async_remote_copy(
             src_ref=vec,
             dst_ref=vec_recv.at[b],
@@ -611,43 +542,50 @@
             dst_ref=vec_recv_blk.at[s - 1],
             send_sem=vec_blk_sems.at[0, s - 1],
             recv_sem=vec_blk_sems.at[1, s - 1],
-            device_id=(f, (z + s) % blk),
+            device_id=(f, lax.rem(z + s, blk)),
             device_id_type=pl.DeviceIdType.MESH,
         )
 
-    for b in range(bits + 2):
-
-        @pl.when(step == heads_to + b)
-        def _():
-            if 1 <= b <= bits:
-                vec_copy(b - 1).wait()
-                vec[...] += vec_recv[b - 1]
-            if b < bits:
-                vec_copy(b).start()
-            elif b == bits:
-                for s in range(1, blk):
-                    vec_blk_copy(s).start()
-            else:
-                for s in range(1, blk):
-                    vec_blk_copy(s).wait()
-                total = vec[...]
-                for s in range(1, blk):
-                    total = total + vec_recv_blk[s - 1]
-                vec_out[...] = total
-
-    @pl.when(step == heads_to + tail - 1)
+    @pl.when(step == heads_to)
     def _():
-        moves_wait(din_s, din, 1)
-
-        @pl.loop(0, ff_steps)
+        @pl.loop(1, tail)
+        def _(i):
+            sums.tick(first + i, done)
+
+            for b in range(bits + 2):
+
+                @pl.when(i == 1 + 2 * b)
+                def _():
+                    if 1 <= b <= bits:
+                        vec_copy(b - 1).wait()
+                        vec[...] += vec_recv[b - 1]
+                    if b < bits:
+                        vec_copy(b).start()
+                    elif b == bits:
+                        for s in range(1, blk):
+                            vec_blk_copy(s).start()
+                    else:
+                        for s in range(1, blk):
+                            vec_blk_copy(s).wait()
+                        total = vec[...]
+                        for s in range(1, blk):
+                            total = total + vec_recv_blk[s - 1]
+                        vec_out[...] = total
+
+        @pl.loop(0, pieces * (blk - 1))
+        def _(i):
+            piece(send_part, i).wait_send()
+            piece(part_came, i).wait_recv()
+
+        for s in range(1, blk):
+            din_part(send_part, s).wait_send()
+            din_part(part_came, s).wait_recv()
+        local_copy(out_s, out, move_sems.at[0, 0]).wait()
+        local_copy(din_s, din, move_sems.at[1, 0]).wait()
+
+        @pl.loop(0, sums.count)
         def _(block):
-            for c in feed_copies(block):
-                c.wait()
-
-        @pl.loop(ff_steps, ff_steps + pairs)
-        def _(block):
-            for c in proj_copies(block):
-                c.wait()
+            flush(block, lambda c: c.wait())
 
 
 def mega(mesh_shape, count, ot, x0, y, w_out, b_out, gain_two, bias_two, up, up_bias, down, down_bias,
@@ -659,12 +597,13 @@
     ff_steps = up.shape[1] // ff_block
     bits = fields.bit_length() - 1
     n = fields * blk
-    rows = 2 * ff_block // LANES * width
-    rows = -(-rows // (16 * n)) * 16 * n
-    blocks = ff_steps + pairs
-    last_tick = blocks - 1 + 2 * bits + 2
+    assert ff_block == 2 * LANES
+    rows = -(-2 * width // (16 * n)) * 16 * n
+    blocks = 2 * (ff_steps + pairs)
+    levels = n.bit_length() - 1
+    last_tick = blocks - 1 + LAG * 2 * levels
     heads_to = ff_steps + 2 * pairs
-    tail = max(last_tick - (2 * heads_to - 2) // 3 + 1, bits + 2)
+    tail = max(last_tick - (ff_steps - 1 + ff_steps // 3 + 3 * pairs) + 1, 2 * bits + 4)
     vec_rows = (8 + up.shape[1] // width) * (width // LANES)
     chunk = slots // blk
     cols_of = width // LANES
@@ -688,7 +627,7 @@
     flops = 12 * slots * width * up.shape[1] + 10 * slots * slots * width + 12 * slots * width * width
     return pl.pallas_call(
         partial(mega_kernel, fields, blk, rows, ff_steps, pairs, tail),
-        grid=(heads_to + tail,),
+        grid=(heads_to + 1,),
         in_specs=[
             pl.BlockSpec(memory_space=pltpu.SMEM),
             whole((width, slots)),
@@ -730,21 +669,18 @@
             pltpu.VMEM((slots, width), BF16),
             pltpu.VMEM((blocks, rows, LANES), BF16),
             pltpu.VMEM((vec_rows, LANES), F32),
-            pltpu.VMEM((ahead, blk - 1, rows // n, LANES), BF16),
             pltpu.VMEM((bits, vec_rows, LANES), F32),
             pltpu.VMEM((blk - 1, vec_rows, LANES), F32),
-            dma((bits, ahead)),
-            dma((bits, ahead)),
-            dma((bits, ahead)),
-            dma((bits, ahead)),
-            dma((2, 2, blk - 1, ahead)),
+            dma((levels, ahead)),
+            dma((levels, ahead)),
+            dma((levels, ahead)),
+            dma((levels, ahead)),
             dma((2, bits)),
             dma((2, blk - 1)),
-            dma((2, 2, blk)),
-            dma((blocks, 2 * cols_of)),
-            pltpu.SemaphoreType.REGULAR((bits, blocks)),
-            pltpu.SemaphoreType.REGULAR((blk - 1, blocks)),
-            *[pltpu.VMEM((ahead, rows >> (s + 1), LANES), BF16) for s in range(bits)],
+            dma((2, blk)),
+            dma((2, 2 * pairs)),
+            dma((blocks, cols_of)),
+            *[pltpu.VMEM((2, ahead, rows >> (s + 1), LANES), BF16) for s in range(levels)],
         ],
         compiler_params=pltpu.CompilerParams(
             vmem_limit_bytes=67_000_000, collective_id=0, has_side_effects=True

time: 402 us -> 346 us (0.86)
  Pallas kernels: 311 us -> 255 us
    pallas_call x1, Pallas kernels: 261 us -> 205 us  [mega(): pl.pallas_call(partial(mega_kernel, fields, blk, rows, ff_steps, pairs, t...]
  transfers between devices with their start and end apart: 2 -> 2, of which waited for: 1 -> 1; matrix products, arithmetic and copies ran while one was open for 2% -> 3% of each run, Pallas kernels for 12% -> 14%
where the time goes in v3:
time: 346 us
  Pallas kernels  255 us (74%)
  waiting for transfers between devices  35.6 us (10%)
  other arithmetic  19 us (5%)
  local copies, waits for them, and re-layouts  15.2 us (4%)
  blocking collectives  11.7 us (3%)
  starting transfers between devices  7.92 us (2%)
    pallas_call x1, Pallas kernels, mega(): pl.pallas_call(partial(mega_kernel, fields, blk, rows, ff_steps, pairs, t...  205 us
    pallas_call x1, Pallas kernels, attend(): pl.pallas_call(partial(attend_kernel, block), grid=(pairs,), in_specs=[pl...  36.9 us
    all_to_all x2, waiting for transfers between devices, to_field(): return lax.all_to_all(part, 'blk', 0, 1, tiled=True)[0]  35.6 us
    pallas_call x1, Pallas kernels, project(): pl.pallas_call(project_kernel, grid=(slots // block,), in_specs=[nat, pl....  13 us
    all_to_all x1, blocking collectives, to_field(): return lax.all_to_all(part, 'blk', 0, 1, tiled=True)[0]  11.7 us
    all_to_all x2, starting transfers between devices, to_field(): return lax.all_to_all(part, 'blk', 0, 1, tiled=True)[0]  7.92 us
    convert_element_type x1, other arithmetic, per_device(): d_up.astype(F32)  7.52 us
  transfers between devices with their start and end apart: 2, of which 1 were waited for; matrix products, arithmetic and copies ran while one was open for 3% of the time, Pallas kernels for 14%

profile of v3, /device:TPU:0, one launch (start us, length us, event | category | flops | bytes accessed | tf_op | source)
XLA Modules:
  0.0 345.6 jit_solution(8430989399497867572)
XLA Ops:
  0.6 0.7 all_to_all.10
  1.3 11.7 %all_to_all.31 = s32[4,1,256]{2,1,0:T(1,128)S(1)} all-to-all(s32[4,1,256]{2,1,0:T(1,128)S(1)} %all_to_all.10), channel_id=1, replica_groups=mesh['fields'=8,'blk'=4] {'blk'}, dimensions={0} | all-to-all | bytes 8192 | tf_op jit(solution)/shard_map/all_to_all | solution.py:708
  13.0 3.6 %all-to-all-start = ((bf16[4,256,768]{2,1,0:T(8,128)(2,1)}), bf16[4,256,768]{2,1,0:T(8,128)(2,1)S(1)}, u32[]{:S(2)}, u32[]{:S(2)}) async-start(bf16[4,256,768]{2,1,0:T(8,128)(2,1)} %param.17), calls=%async_computation | async-start | bytes 3145728 | tf_op jit(solution)/shard_map/all_to_all | solution.py:708
  16.6 0.0 copy-start.7
  16.6 0.0 copy-start.8
  16.6 0.0 copy-start.9
  16.6 0.0 copy-start.10
  16.6 0.0 copy-start.6
  16.7 0.0 copy-start.11
  16.7 0.0 copy-start.12
  16.7 0.0 copy-start.13
  16.7 0.0 copy-start.14
  16.7 0.0 copy-start.15
  16.7 35.6 %all-to-all-done = bf16[4,256,768]{2,1,0:T(8,128)(2,1)S(1)} async-done(((bf16[4,256,768]{2,1,0:T(8,128)(2,1)}), bf16[4,256,768]{2,1,0:T(8,128)(2,1)S(1)}, u32[]{:S(2)}, u32[]{:S(2)}) %all-to-all-start) | async-done | bytes 1572896 | tf_op jit(solution)/shard_map/all_to_all | solution.py:708
  52.4 1.1 copy-done.2
  53.5 4.4 %all-to-all-start.2 = ((bf16[4,256,768]{2,1,0:T(8,128)(2,1)}), bf16[4,256,768]{2,1,0:T(8,128)(2,1)}, u32[]{:S(2)}, u32[]{:S(2)}) async-start(bf16[4,256,768]{2,1,0:T(8,128)(2,1)} %param.33), calls=%async_computation.2 | async-start | bytes 3145728 | tf_op jit(solution)/shard_map/all_to_all | solution.py:708
  57.9 0.6 broadcast_in_dim.36.gain.gain_one
  58.5 0.6 broadcast_in_dim.37.bias
  59.1 0.6 broadcast_in_dim.38.qb
  59.7 0.0 copy-done.10
  59.7 0.6 broadcast_in_dim.39.vb
  60.2 0.6 broadcast_in_dim.43.up_bias
  60.8 0.6 broadcast_in_dim.40.b_out
  61.4 0.0 copy-done.12
  61.4 0.6 broadcast_in_dim.41.gain_two
  62.0 0.6 broadcast_in_dim.42.bias_two
  62.6 0.6 broadcast_in_dim.44.down_bias
  63.2 0.6 dynamic_slice.3
  63.8 0.2 multiply_sine_fusion.1
  64.0 0.7 pad_maximum_fusion.1.row_table
  64.7 0.3 multiply_sine_fusion
  65.0 0.7 pad_maximum_fusion.col_table
  65.7 1.0 copy.33.keep
  66.8 13.0 %project.1 = (f32[1024,768]{1,0:T(8,128)}, bf16[768,1024]{1,0:T(8,128)(2,1)}, bf16[768,1024]{1,0:T(8,128)(2,1)}, bf16[1024,768]{1,0:T(8,128)(2,1)}, bf16[768,102...) custom-call(bf16[1024,768]{1,0:T(8,128)(2,1)} %bitcast.22, s32[1024,1]{1,0:T(8,128)} %copy.33.keep, ...), custom_call_target="tpu_custom_call" | custom-call | flops 3623878656 | bytes 15728640 | tf_op jit(solution)/shard_map/project/pallas_call | solution.py:84
  79.7 36.9 %attend.1 = (bf16[1024,768]{1,0:T(8,128)(2,1)}, bf16[768,1024]{1,0:T(8,128)(2,1)}, f32[6,2,1024]{2,1,0:T(2,128)}) custom-call(s32[1,1]{1,0:T(1,128)} %bitcast.count, bf16[768,1024]{1,0:T(8,128)(2,1)} %get-tuple-element.31.qt, bf16[1024,768]{1,0:T(8,128)(2,1)} %get-tuple-element.32.k, bf16[768,1024]{1,0:T(8,128)(2,1)} %get-tuple-element.33.vt), custom_call_target="tpu_custom_call" | custom-call | flops 12884901888 | bytes 9437184 | tf_op jit(solution)/shard_map/attend/pallas_call | solution.py:153
  116.6 0.0 all-to-all-done.2
  116.6 205.5 %mega.1 = (bf16[4,256,768]{2,1,0:T(8,128)(2,1)}, bf16[4,256,768]{2,1,0:T(8,128)(2,1)}, bf16[768,3072]{1,0:T(8,128)(2,1)}, bf16[3072,768]{1,0:T(8,128)(2,1)}, bf1...) custom-call(s32[1,1]{1,0:T(1,128)} %bitcast.count, bf16[768,1024]{1,0:T(8,128)(2,1)} %get-tuple-element.34.ot, ...), custom_call_target="tpu_custom_call" | custom-call | flops 44291850240 | bytes 47185920 | tf_op jit(solution)/shard_map/mega/pallas_call | solution.py:628
  322.1 1.4 slice_bitcast_fusion.1
  323.5 1.3 slice_bitcast_fusion
  324.9 7.5 %convert_element_type.48 = f32[768,3072]{1,0:T(8,128)} convert(bf16[768,3072]{1,0:T(8,128)(2,1)} %get-tuple-element.45) | non-fusion elementwise | flops 2359296 | bytes 14155776 | tf_op jit(solution)/shard_map/convert_element_type | solution.py:739
  332.4 0.0 copy-done
  332.4 4.5 %convert_element_type.49 = f32[3072,768]{1,0:T(8,128)} convert(bf16[3072,768]{1,0:T(8,128)(2,1)S(1)} %copy-done) | non-fusion elementwise | flops 2359296 | bytes 14155776 | tf_op jit(solution)/shard_map/convert_element_type | solution.py:741
  336.9 3.5 %convert_element_type.46 = f32[768,2304]{1,0:T(8,128)} convert(bf16[768,2304]{1,0:T(8,128)(2,1)S(1)} %copy-done.1) | non-fusion elementwise | flops 1769472 | bytes 10616832 | tf_op jit(solution)/shard_map/convert_element_type | solution.py:732
  340.3 1.6 convert_element_type.47
  341.9 0.5 copy-done.4
  342.5 1.1 copy.36
  343.6 0.8 copy-done.3
  344.4 1.1 copy.37
  (19 shorter events, 0.0 us)
Async XLA Ops:
  13.0 39.3 %all-to-all-start = ((bf16[4,256,768]{2,1,0:T(8,128)(2,1)}), bf16[4,256,768]{2,1,0:T(8,128)(2,1)S(1)}, u32[]{:S(2)}, u32[]{:S(2)}) async-start(bf16[4,256,768]{2,1,0:T(8,128)(2,1)} %param.17), calls=%async_computation | async-start | bytes 3145728 | tf_op jit(solution)/shard_map/all_to_all | solution.py:708
  16.6 41.3 %copy-start.7 = (bf16[768]{0:T(1024)(128)(2,1)S(1)}, bf16[768]{0:T(1024)(128)(2,1)}, u32[]{:S(2)}) copy-start(bf16[768]{0:T(1024)(128)(2,1)} %param.20) | copy-start | bytes 4612
  16.6 41.9 %copy-start.8 = (bf16[768]{0:T(1024)(128)(2,1)S(1)}, bf16[768]{0:T(1024)(128)(2,1)}, u32[]{:S(2)}) copy-start(bf16[768]{0:T(1024)(128)(2,1)} %param.21) | copy-start | bytes 4612
  16.6 42.4 %copy-start.9 = (bf16[768]{0:T(1024)(128)(2,1)S(1)}, bf16[768]{0:T(1024)(128)(2,1)}, u32[]{:S(2)}) copy-start(bf16[768]{0:T(1024)(128)(2,1)} %param.23) | copy-start | bytes 4612
  16.6 43.0 %copy-start.10 = (bf16[768]{0:T(1024)(128)(2,1)S(1)}, bf16[768]{0:T(1024)(128)(2,1)}, u32[]{:S(2)}) copy-start(bf16[768]{0:T(1024)(128)(2,1)} %param.24) | copy-start | bytes 4612
  16.6 43.6 %copy-start.6 = (bf16[3072]{0:T(1024)(128)(2,1)S(1)}, bf16[3072]{0:T(1024)(128)(2,1)}, u32[]{:S(2)}) copy-start(bf16[3072]{0:T(1024)(128)(2,1)} %param.30) | copy-start | bytes 18436
  16.7 44.2 %copy-start.11 = (bf16[768]{0:T(1024)(128)(2,1)S(1)}, bf16[768]{0:T(1024)(128)(2,1)}, u32[]{:S(2)}) copy-start(bf16[768]{0:T(1024)(128)(2,1)} %param.26) | copy-start | bytes 4612
  16.7 44.8 %copy-start.12 = (bf16[768]{0:T(1024)(128)(2,1)S(1)}, bf16[768]{0:T(1024)(128)(2,1)}, u32[]{:S(2)}) copy-start(bf16[768]{0:T(1024)(128)(2,1)} %param.27) | copy-start | bytes 4612
  16.7 45.3 %copy-start.13 = (bf16[768]{0:T(1024)(128)(2,1)S(1)}, bf16[768]{0:T(1024)(128)(2,1)}, u32[]{:S(2)}) copy-start(bf16[768]{0:T(1024)(128)(2,1)} %param.28) | copy-start | bytes 4612
  16.7 45.9 %copy-start.14 = (bf16[768]{0:T(1024)(128)(2,1)S(1)}, bf16[768]{0:T(1024)(128)(2,1)}, u32[]{:S(2)}) copy-start(bf16[768]{0:T(1024)(128)(2,1)} %param.32) | copy-start | bytes 4612
  16.7 46.5 %copy-start.15 = (s32[4]{0:T(128)S(1)}, s32[4]{0:T(128)}, u32[]{:S(2)}) copy-start(s32[4]{0:T(128)} %param.19) | copy-start | bytes 52
  52.4 1.1 copy-start.2
  53.5 63.1 %all-to-all-start.2 = ((bf16[4,256,768]{2,1,0:T(8,128)(2,1)}), bf16[4,256,768]{2,1,0:T(8,128)(2,1)}, u32[]{:S(2)}, u32[]{:S(2)}) async-start(bf16[4,256,768]{2,1,0:T(8,128)(2,1)} %param.33), calls=%async_computation.2 | async-start | bytes 3145728 | tf_op jit(solution)/shard_map/all_to_all | solution.py:708
  324.9 7.5 %copy-start = (bf16[3072,768]{1,0:T(8,128)(2,1)S(1)}, bf16[3072,768]{1,0:T(8,128)(2,1)}, u32[]{:S(2)}) copy-start(bf16[3072,768]{1,0:T(8,128)(2,1)} %get-tuple-element.46) | copy-start | bytes 14155780
  332.4 4.5 %copy-start.1 = (bf16[768,2304]{1,0:T(8,128)(2,1)S(1)}, bf16[768,2304]{1,0:T(8,128)(2,1)}, u32[]{:S(2)}) copy-start(bf16[768,2304]{1,0:T(8,128)(2,1)} %get-tuple-element.43) | copy-start | bytes 10616836
  336.9 3.5 %copy-start.5 = (bf16[768,768]{1,0:T(8,128)(2,1)S(1)}, bf16[768,768]{1,0:T(8,128)(2,1)}, u32[]{:S(2)}) copy-start(bf16[768,768]{1,0:T(8,128)(2,1)} %get-tuple-element.44) | copy-start | bytes 3538948
  340.3 2.1 copy-start.4
  342.5 2.0 copy-start.3

commit v4 on v3

--- a/solution.py
+++ b/solution.py
@@ -2,6 +2,7 @@
 import math
 import jax
 import jax.numpy as jnp
+import numpy as np
 from jax import lax
 from jax.experimental import pallas as pl
 from jax.experimental.pallas import tpu as pltpu
@@ -9,6 +10,7 @@
 
 HEAD_DIM = 64
 GRID_W = 64
+PATCHES = 2048
 epsilon = 1e-06
 negative = -1e30
 VMEM_BYTES = 60 * 1024 * 1024
@@ -19,6 +21,10 @@
 
 def mm(a, b, ca, cb):
     return lax.dot_general(a, b, (((ca,), (cb,)), ((), ())), preferred_element_type=F32)
+
+
+def row(ref):
+    return ref[...].astype(F32)[None]
 
 
 def whole(shape):
@@ -50,57 +56,73 @@
     return high, mid, low
 
 
-def project_kernel(tok, keep, row_table, col_table, gain, bias, weight, qb, vb, x0, a1t, qt, k, kt, v, vt):
-    width = tok.shape[1]
-    rows = tok.shape[0]
-    patch = keep[...]
-    tall = row_table.shape[0]
-    wide = col_table.shape[0]
-    row_hot = (lax.broadcasted_iota(jnp.int32, (rows, tall), 1) == patch // GRID_W).astype(F32)
-    col_hot = (lax.broadcasted_iota(jnp.int32, (rows, wide), 1) == patch % GRID_W).astype(F32)
-    pos_row = jnp.dot(row_hot, row_table[...], precision=lax.Precision.HIGHEST, preferred_element_type=F32)
-    pos_col = jnp.dot(col_hot, col_table[...], precision=lax.Precision.HIGHEST, preferred_element_type=F32)
-    x = tok[...].astype(F32) + jnp.concatenate([pos_row, pos_col], -1)
-    x0[...] = x
-    hat, _ = norm_parts(x)
-    a = (hat * gain[...].astype(F32) + bias[...].astype(F32)).astype(BF16)
+def tables(width):
+    quarter = width // 4
+    omega = 1.0 / 10000.0 ** (np.arange(quarter) / quarter)
+
+    def table(length):
+        ang = np.arange(length)[:, None] * omega
+        return jnp.asarray(np.concatenate([np.sin(ang), np.cos(ang)], -1), F32)
+
+    return table(PATCHES // GRID_W), table(GRID_W)
+
+
+def place_kernel(tok, keep, row_table, col_table, x0):
+    slots = tok.shape[1]
+    patch = keep[pl.ds(pl.program_id(0), 1), :]
+    parts = []
+    for table, of in ((row_table, lax.div(patch, GRID_W)), (col_table, lax.rem(patch, GRID_W))):
+        hot = (lax.broadcasted_iota(jnp.int32, (table.shape[0], slots), 0) == of).astype(F32)
+        parts.append(jnp.dot(hot.T, table[...], precision=lax.Precision.HIGHEST, preferred_element_type=F32))
+    x0[0] = (tok[0].astype(F32) + jnp.concatenate(parts, -1)).astype(BF16)
+
+
+def place(tokens, keep):
+    fields, slots, width = tokens.shape
+    row_table, col_table = tables(width)
+    block = pl.BlockSpec((1, slots, width), lambda i: (i, 0, 0))
+    return pl.pallas_call(
+        place_kernel,
+        grid=(fields,),
+        in_specs=[block, whole((fields, slots)), whole(row_table.shape), whole(col_table.shape)],
+        out_specs=block,
+        out_shape=jax.ShapeDtypeStruct(tokens.shape, BF16),
+        name="place",
+    )(tokens, keep, row_table, col_table)
+
+
+def project_kernel(x0, gain, bias, weight, qb, vb, a1t, qt, k, kt, v, vt):
+    width = x0.shape[1]
+    hat, _ = norm_parts(x0[...].astype(F32))
+    a = (hat * row(gain) + row(bias)).astype(BF16)
     a1t[...] = a.T
-    q = (jnp.dot(a, weight[:, :width], preferred_element_type=F32) + qb[...].astype(F32)).astype(BF16)
+    q = (jnp.dot(a, weight[:, :width], preferred_element_type=F32) + row(qb)).astype(BF16)
     qt[...] = q.T
     kk = jnp.dot(a, weight[:, width : 2 * width], preferred_element_type=F32).astype(BF16)
     k[...] = kk
     kt[...] = kk.T
-    vv = (jnp.dot(a, weight[:, 2 * width :], preferred_element_type=F32) + vb[...].astype(F32)).astype(BF16)
+    vv = (jnp.dot(a, weight[:, 2 * width :], preferred_element_type=F32) + row(vb)).astype(BF16)
     v[...] = vv
     vt[...] = vv.T
 
 
-def project(tok, keep, tables, gain, bias, weight, qb, vb, block=256):
-    slots, width = tok.shape
+def project(x0, gain, bias, weight, qb, vb, block=256):
+    slots, width = x0.shape
     nat = pl.BlockSpec((block, width), lambda i: (i, 0))
     tra = pl.BlockSpec((width, block), lambda i: (0, i))
     sn = jax.ShapeDtypeStruct((slots, width), BF16)
     st = jax.ShapeDtypeStruct((width, slots), BF16)
+    one = whole((width,))
     return pl.pallas_call(
         project_kernel,
         grid=(slots // block,),
-        in_specs=[
-            nat,
-            pl.BlockSpec((block, 1), lambda i: (i, 0)),
-            whole(tables[0].shape),
-            whole(tables[1].shape),
-            whole((1, width)),
-            whole((1, width)),
-            whole(weight.shape),
-            whole((1, width)),
-            whole((1, width)),
-        ],
-        out_specs=[nat, tra, tra, nat, tra, nat, tra],
-        out_shape=[jax.ShapeDtypeStruct((slots, width), F32), st, st, sn, st, sn, st],
+        in_specs=[nat, one, one, whole(weight.shape), one, one],
+        out_specs=[tra, tra, nat, tra, nat, tra],
+        out_shape=[st, st, sn, st, sn, st],
         compiler_params=pltpu.CompilerParams(vmem_limit_bytes=VMEM_BYTES),
         cost_estimate=pl.CostEstimate(flops=2 * slots * width * 3 * width, bytes_accessed=20 * slots * width, transcendentals=0),
         name="project",
-    )(tok, keep[:, None], *tables, gain[None], bias[None], weight, qb[None], vb[None])
+    )(x0, gain, bias, weight, qb, vb)
 
 
 def augment_cols(block, extra, second):
@@ -122,7 +144,7 @@
     slots = k.shape[0]
     c = HEAD_DIM**-0.5 * LOG2E
     lane = lax.broadcasted_iota(jnp.int32, (slots, 2 * HEAD_DIM), 1)
-    kb = key_bias(count[0, 0], slots)
+    kb = key_bias(count[lax.axis_index("blk")], slots)
     extra_col = jnp.where(lane % HEAD_DIM == 0, kb, 0.0).astype(BF16)
     sub = lax.broadcasted_iota(jnp.int32, (HEAD_DIM, block), 0)
     extra_row = jnp.where(sub == 0, 1.0, 0.0).astype(BF16)
@@ -167,13 +189,22 @@
 
 
 SLOTS_AHEAD = 8
-LAG = 2
 LANES = 128
+LAG_CORE, LAG_XY, LAG_Z = 2, 3, 3
+DIN_EVERY = 2
+
+
+def offsets(near, far):
+    lags = [LAG_CORE] + [LAG_XY] * (near - 1) + [LAG_Z] * far
+    ticks = [0]
+    for lag in lags + lags[::-1]:
+        ticks.append(ticks[-1] + lag)
+    return ticks
 
 
 class Sums:
-    def __init__(self, fields, blk, rows, count, grads, recv, sems):
-        self.rows, self.count = rows, count
+    def __init__(self, fields, blk, rows, early, count, grads, recv, sems):
+        self.rows, self.early, self.count = rows, early, count
         self.near, self.far = fields.bit_length() - 1, blk.bit_length() - 1
         self.bits = self.near + self.far
         self.grads, self.recv = grads, recv
@@ -238,15 +269,20 @@
             self.copy(gather, block, slot, route, 2 * bits - 1 - kind if gather else kind).start()
 
     def tick(self, tick, done):
-        assert LAG == 2
-        odd = lax.rem(lax.div(tick, 2), 2)
-        routes = self.route(odd), self.route(1 - odd)
-        for kind in range(self.actions):
-            block = tick - LAG * kind
-
-            @pl.when((block >= 0) & (block < self.count))
+        routes = {}
+        for odd_offset in (0, 1):
+            turn = lax.rem(lax.div(tick + odd_offset, 2), 2)
+            routes[odd_offset] = self.route(turn), self.route(1 - turn)
+        for kind, offset in enumerate(offsets(self.near, self.far)):
+            entry = tick - offset
+            late = entry - self.early - 2
+            block = jnp.where(late >= 0, self.early + lax.div(late, 2), entry)
+            runs = jnp.where(late >= 0, (lax.rem(late, 2) == 0) & (block < self.count), (entry >= 0) & (entry < self.early))
+            route = routes[offset % 2][(offset + 1) // 2 % 2]
+
+            @pl.when(runs)
             def _():
-                self.act(kind, block, lax.rem(block, SLOTS_AHEAD), routes[kind % 2])
+                self.act(kind, block, lax.rem(block, SLOTS_AHEAD), route)
                 if kind == self.actions - 1:
                     done(block)
 
@@ -256,7 +292,7 @@
     count, ot, x0, y, w_out, b_out, gain_two, bias_two, up, up_bias, down, down_bias,
     qt, k, kt, v, lse, a1t, wq, wk, wv, gain_one,
     out, din, up_out, down_out, qkv_out, out_out, vec_out,
-    x1, a2, a2t, acc, dacc, out_s, dot_s, dt, din_s, grads, vec, vec_recv, vec_recv_blk,
+    x1, a2, a2t, acc, dacc, out_s, dot_s, dt, din_s, dvk, grads, vec, vec_recv, vec_recv_blk,
     send_rs, recv_rs, send_ag, recv_ag, vec_sems, vec_blk_sems, move_sems, piece_sems, flush_sems, *recv,
 ):
     step = pl.program_id(0)
@@ -269,7 +305,7 @@
     ff = up.shape[1]
     heads_from, heads_to = ff_steps, ff_steps + 2 * pairs
     sums = Sums(
-        fields, blk, rows, 2 * (ff_steps + pairs), grads, recv, (send_rs, recv_rs, send_ag, recv_ag)
+        fields, blk, rows, 2 * ff_steps, 2 * (ff_steps + pairs), grads, recv, (send_rs, recv_rs, send_ag, recv_ag)
     )
     VEC_G1, VEC_B1, VEC_Q, VEC_V, VEC_OUT, VEC_G2, VEC_B2, VEC_DOWN, VEC_UP = range(9)
 
@@ -304,12 +340,10 @@
 
     pieces = 2 * pairs // (blk - 1)
 
-    def piece(maker, i):
-        sems = piece_sems.at[0, i], piece_sems.at[1, i]
-        return maker(out_s, out, lax.rem(i, blk - 1) + 1, lax.div(i, blk - 1), chunk // pieces, sems)
-
-    def din_part(maker, s):
-        return maker(din_s, din, s, 0, chunk, (move_sems.at[0, s], move_sems.at[1, s]))
+    def piece(maker, i, kind):
+        sems = piece_sems.at[kind, 0, i], piece_sems.at[kind, 1, i]
+        src, dst = ((out_s, out), (din_s, din))[kind]
+        return maker(src, dst, blk - 1 - lax.rem(i, blk - 1), lax.div(i, blk - 1), chunk // pieces, sems)
 
     @pl.when(step == 0)
     def _():
@@ -325,10 +359,10 @@
 
         for r in range(blk):
             at = slice(r * chunk, (r + 1) * chunk)
-            x = x0[at, :] + jnp.dot(ot[:, at].T, w_out[...], preferred_element_type=F32) + b_out[...].astype(F32)
+            x = x0[at, :].astype(F32) + jnp.dot(ot[:, at].T, w_out[...], preferred_element_type=F32) + row(b_out)
             x1[at, :] = x
             hat, _ = norm_parts(x)
-            a = (hat * gain_two[...].astype(F32) + bias_two[...].astype(F32)).astype(BF16)
+            a = (hat * row(gain_two) + row(bias_two)).astype(BF16)
             a2[at, :] = a
             a2t[:, at] = a.T
         acc[...] = jnp.zeros_like(acc)
@@ -378,25 +412,17 @@
     def done(block):
         flush(block, lambda c: c.start())
 
-    ff_ticks = ff_steps - 1 + ff_steps // 3
-    index_of = step - ff_steps
-    in_feed, in_heads = step < ff_steps, step < heads_to
-    first = jnp.where(
-        in_feed,
-        step - 1 + lax.div(step, 3),
-        jnp.where(in_heads, ff_ticks + index_of + lax.div(index_of, 2), ff_ticks + pairs + index_of),
-    )
-    twice = jnp.where(in_feed, lax.rem(step, 3) == 2, in_heads & (lax.rem(index_of, 2) == 1))
+    first = 2 * step - 2
 
     @pl.when(step >= 1)
     def _():
-        @pl.loop(0, jnp.where(twice, 2, 1))
+        @pl.loop(0, 2)
         def _(i):
             sums.tick(first + i, done)
 
     @pl.when(step < heads_from)
     def _():
-        h = jnp.dot(a2[...], up[...], preferred_element_type=F32) + up_bias[...].astype(F32)
+        h = jnp.dot(a2[...], up[...], preferred_element_type=F32) + row(up_bias)
         phi = 0.5 + 0.5 * lax.erf(h * (0.5**0.5))
         slope = phi + h * (jnp.exp2(h * h * (-0.5 * LOG2E)) * (2 * math.pi) ** -0.5)
         g = (h * phi).astype(BF16)
@@ -425,16 +451,16 @@
             grad = dacc[at, :]
             yf = y[at, :].astype(F32)
             xs = x1[at, :]
-            out_s[at, :] = (xs + acc[at, :] + down_bias[...].astype(F32)).astype(BF16)
+            out_s[at, :] = (xs + acc[at, :] + row(down_bias)).astype(BF16)
             hat, sc = norm_parts(xs)
-            dx = yf + norm_back(grad, hat, sc, gain_two[...].astype(F32))
+            dx = yf + norm_back(grad, hat, sc, row(gain_two))
             x1[at, :] = dx
             dz = dx.astype(BF16)
             a2[at, :] = dz
             dot_s[:, at] = mm(dz, w_out[...], 1, 1).astype(BF16).T
             for i, value in enumerate((grad * hat, grad, yf, dz.astype(F32))):
                 totals[i] = totals[i] + jnp.sum(value, 0, keepdims=True)
-        local_copy(out_s, out, move_sems.at[0, 0]).start()
+        local_copy(out_s, out, move_sems.at[0]).start()
         for index, value in zip((VEC_G2, VEC_B2, VEC_DOWN, VEC_OUT), totals):
             put_vec(index, value)
         d_out = jnp.dot(ot[...], a2[...], preferred_element_type=F32).astype(BF16)
@@ -452,13 +478,13 @@
 
         @pl.when(index < pieces * (blk - 1))
         def _():
-            piece(send_part, index).start()
+            piece(send_part, index, 0).start()
 
         c = HEAD_DIM**-0.5 * LOG2E
         scale = HEAD_DIM**-0.5
         block = 256
         lane = lax.broadcasted_iota(jnp.int32, (slots, pair), 1)
-        kb = key_bias(count[0, 0], slots)
+        kb = key_bias(count[z], slots)
         mine = lane // HEAD_DIM == head
         lane = lane % HEAD_DIM
         ka = jnp.where(mine, k[...], jnp.where(lane == 0, kb, jnp.where(lane < 4, 1.0, 0.0)).astype(BF16))
@@ -475,9 +501,9 @@
         one = jnp.ones((1, slots), F32)
         extra_q = jnp.concatenate([one, *l3, zeros], 0).astype(BF16)
         extra_d = jnp.concatenate([*d3, zeros, 0.0 * one], 0).astype(BF16)
-        first = lax.broadcasted_iota(jnp.int32, (pair, slots), 0) // HEAD_DIM == head
-        qa = jnp.where(first, jnp.concatenate([q_h, q_h], 0), jnp.concatenate([extra_q, extra_q], 0))
-        da = jnp.where(first, jnp.concatenate([do_h, do_h], 0), jnp.concatenate([extra_d, extra_d], 0))
+        upper = lax.broadcasted_iota(jnp.int32, (pair, slots), 0) // HEAD_DIM == head
+        qa = jnp.where(upper, jnp.concatenate([q_h, q_h], 0), jnp.concatenate([extra_q, extra_q], 0))
+        da = jnp.where(upper, jnp.concatenate([do_h, do_h], 0), jnp.concatenate([extra_d, extra_d], 0))
         for i in range(slots // block):
             at = slice(i * block, (i + 1) * block)
             s = mm(ka, qa[:, at], 1, 0)
@@ -489,11 +515,13 @@
             dv = mm(do_h[:, at], p, 1, 1)
             dk = mm(q_h[:, at], ds, 1, 1)
             if i == 0:
-                dv_sum, dk_sum = dv, dk
+                dvk[0] = dv
+                dvk[1] = dk
             else:
-                dv_sum, dk_sum = dv_sum + dv, dk_sum + dk
-        dt[pl.ds(pl.multiple_of(pair + head * HEAD_DIM, HEAD_DIM), HEAD_DIM), :] = (dk_sum * scale).astype(BF16)
-        dt[pl.ds(pl.multiple_of(2 * pair + head * HEAD_DIM, HEAD_DIM), HEAD_DIM), :] = dv_sum.astype(BF16)
+                dvk[0] += dv
+                dvk[1] += dk
+        dt[pl.ds(pl.multiple_of(pair + head * HEAD_DIM, HEAD_DIM), HEAD_DIM), :] = (dvk[1] * scale).astype(BF16)
+        dt[pl.ds(pl.multiple_of(2 * pair + head * HEAD_DIM, HEAD_DIM), HEAD_DIM), :] = dvk[0].astype(BF16)
 
         @pl.when(head == 1)
         def _():
@@ -514,14 +542,12 @@
         for r in range(blk):
             at = slice(r * chunk, (r + 1) * chunk)
             grad = dacc[at, :]
-            hat, sc = norm_parts(x0[at, :])
-            dn = norm_back(grad, hat, sc, gain_one[...].astype(F32))
+            hat, sc = norm_parts(x0[at, :].astype(F32))
+            dn = norm_back(grad, hat, sc, row(gain_one))
             din_s[at, :] = (x1[at, :] + dn).astype(BF16)
             for i, value in enumerate((grad * hat, grad)):
                 totals[i] = totals[i] + jnp.sum(value, 0, keepdims=True)
-        for s in range(1, blk):
-            din_part(send_part, s).start()
-        local_copy(din_s, din, move_sems.at[1, 0]).start()
+        local_copy(din_s, din, move_sems.at[1]).start()
         put_vec(VEC_G1, totals[0])
         put_vec(VEC_B1, totals[1])
 
@@ -548,13 +574,18 @@
 
     @pl.when(step == heads_to)
     def _():
-        @pl.loop(1, tail)
+        @pl.loop(2, tail)
         def _(i):
             sums.tick(first + i, done)
+            turn = lax.div(i - 2, DIN_EVERY)
+
+            @pl.when((lax.rem(i - 2, DIN_EVERY) == 0) & (turn < pieces * (blk - 1)))
+            def _():
+                piece(send_part, turn, 1).start()
 
             for b in range(bits + 2):
 
-                @pl.when(i == 1 + 2 * b)
+                @pl.when(i == 2 + 2 * b)
                 def _():
                     if 1 <= b <= bits:
                         vec_copy(b - 1).wait()
@@ -574,14 +605,12 @@
 
         @pl.loop(0, pieces * (blk - 1))
         def _(i):
-            piece(send_part, i).wait_send()
-            piece(part_came, i).wait_recv()
-
-        for s in range(1, blk):
-            din_part(send_part, s).wait_send()
-            din_part(part_came, s).wait_recv()
-        local_copy(out_s, out, move_sems.at[0, 0]).wait()
-        local_copy(din_s, din, move_sems.at[1, 0]).wait()
+            for kind in range(2):
+                piece(send_part, i, kind).wait_send()
+                piece(part_came, i, kind).wait_recv()
+
+        local_copy(out_s, out, move_sems.at[0]).wait()
+        local_copy(din_s, din, move_sems.at[1]).wait()
 
         @pl.loop(0, sums.count)
         def _(block):
@@ -601,9 +630,9 @@
     rows = -(-2 * width // (16 * n)) * 16 * n
     blocks = 2 * (ff_steps + pairs)
     levels = n.bit_length() - 1
-    last_tick = blocks - 1 + LAG * 2 * levels
     heads_to = ff_steps + 2 * pairs
-    tail = max(last_tick - (ff_steps - 1 + ff_steps // 3 + 3 * pairs) + 1, 2 * bits + 4)
+    last_tick = 2 * ff_steps + 2 + 2 * (2 * pairs - 1) + offsets(bits, levels - bits)[-1]
+    tail = last_tick + 1 - (2 * heads_to - 2)
     vec_rows = (8 + up.shape[1] // width) * (width // LANES)
     chunk = slots // blk
     cols_of = width // LANES
@@ -621,7 +650,7 @@
         return pl.BlockSpec((width, pair), lambda i: (0, part * pairs + pair_at(i)))
 
     hbm = pl.BlockSpec(memory_space=pl.ANY)
-    one = (1, width)
+    one = (width,)
     dma = pltpu.SemaphoreType.DMA
     ahead = SLOTS_AHEAD
     flops = 12 * slots * width * up.shape[1] + 10 * slots * slots * width + 12 * slots * width * width
@@ -638,7 +667,7 @@
             whole(one),
             whole(one),
             pl.BlockSpec((width, ff_block), lambda i: (0, ff_at(i))),
-            pl.BlockSpec((1, ff_block), lambda i: (0, ff_at(i))),
+            pl.BlockSpec((ff_block,), lambda i: (ff_at(i),)),
             pl.BlockSpec((ff_block, width), lambda i: (ff_at(i), 0)),
             whole(one),
             tra, nat, tra, nat,
@@ -667,6 +696,7 @@
             pltpu.VMEM((width, slots), BF16),
             pltpu.VMEM((3 * pair, slots), BF16),
             pltpu.VMEM((slots, width), BF16),
+            pltpu.VMEM((2, HEAD_DIM, slots), F32),
             pltpu.VMEM((blocks, rows, LANES), BF16),
             pltpu.VMEM((vec_rows, LANES), F32),
             pltpu.VMEM((bits, vec_rows, LANES), F32),
@@ -677,8 +707,8 @@
             dma((levels, ahead)),
             dma((2, bits)),
             dma((2, blk - 1)),
-            dma((2, blk)),
-            dma((2, 2 * pairs)),
+            dma((2,)),
+            dma((2, 2, 2 * pairs)),
             dma((blocks, cols_of)),
             *[pltpu.VMEM((2, ahead, rows >> (s + 1), LANES), BF16) for s in range(levels)],
         ],
@@ -688,20 +718,26 @@
         cost_estimate=pl.CostEstimate(flops=flops, bytes_accessed=60 * slots * width, transcendentals=0),
         name="mega",
     )(
-        count, ot, x0, y, w_out, b_out[None], gain_two[None], bias_two[None], up, up_bias[None], down, down_bias[None],
-        qt, k, kt, v, lse, a1t, w_qkv, w_qkv, w_qkv, gain_one[None],
+        count, ot, x0, y, w_out, b_out, gain_two, bias_two, up, up_bias, down, down_bias,
+        qt, k, kt, v, lse, a1t, w_qkv, w_qkv, w_qkv, gain_one,
     )
 
 
-def tables(width):
-    quarter = width // 4
-    omega = 1.0 / 10000.0 ** (jnp.arange(quarter).astype(F32) / quarter)
-
-    def table(length):
-        ang = jnp.arange(length).astype(F32)[:, None] * omega
-        return jnp.concatenate([jnp.sin(ang), jnp.cos(ang)], -1)
-
-    return table(2048 // GRID_W), table(GRID_W)
+def widen(arrays, steps):
+    def kernel(*refs):
+        for src, dst in zip(refs[: len(arrays)], refs[len(arrays) :]):
+            dst[...] = src[...].astype(F32)
+
+    specs = [pl.BlockSpec((a.shape[0] // steps, a.shape[1]), lambda i: (i, 0)) for a in arrays]
+    return pl.pallas_call(
+        kernel,
+        grid=(steps,),
+        in_specs=specs,
+        out_specs=specs,
+        out_shape=[jax.ShapeDtypeStruct(a.shape, F32) for a in arrays],
+        compiler_params=pltpu.CompilerParams(vmem_limit_bytes=VMEM_BYTES),
+        name="widen",
+    )(*arrays)
 
 
 def to_field(part):
@@ -713,32 +749,31 @@
     out_bias, norm2_gain, norm2_bias, up_weight, up_bias, down_weight, down_bias, cotangent,
 ):
     width = tokens.shape[2]
-    count = lax.dynamic_slice(counts, (lax.axis_index("blk"),), (1,))[None]
-    x0, a1t, qt, k, kt, v, vt = project(
-        to_field(tokens), to_field(keep_index), tables(width), norm1_gain, norm1_bias, qkv_weight, query_bias, value_bias
-    )
+    x0 = to_field(place(tokens, keep_index))
+    a1t, qt, k, kt, v, vt = project(x0, norm1_gain, norm1_bias, qkv_weight, query_bias, value_bias)
     y = to_field(cotangent)
-    _, ot, lse = attend(count, qt, k, vt)
+    _, ot, lse = attend(counts, qt, k, vt)
     output, input_grad, d_up, d_down, d_qkv, d_out, vecs = mega(
-        mesh_shape, count, ot, x0, y, out_weight, out_bias, norm2_gain, norm2_bias, up_weight, up_bias, down_weight,
+        mesh_shape, counts, ot, x0, y, out_weight, out_bias, norm2_gain, norm2_bias, up_weight, up_bias, down_weight,
         down_bias, qt, k, kt, v, lse, a1t, qkv_weight, norm1_gain,
     )
+    d_up, d_down, d_qkv, d_out = widen((d_up, d_down, d_qkv, d_out), 12)
     vec = vecs.reshape(-1, width)
     return (
         output,
         input_grad,
         vec[0],
         vec[1],
-        d_qkv.astype(F32),
+        d_qkv,
         vec[2],
         vec[3],
-        d_out.astype(F32),
+        d_out,
         vec[4],
         vec[5],
         vec[6],
-        d_up.astype(F32),
+        d_up,
         vec[8:].reshape(-1),
-        d_down.astype(F32),
+        d_down,
         vec[7],
     )
 

time: 346 us -> 304 us (0.88)
  waiting for transfers between devices: 35.6 us -> 0.01 us
  blocking collectives: 11.7 us -> 43.4 us
  other arithmetic: 19 us -> 0 us
  local copies, waits for them, and re-layouts: 15.2 us -> 5.83 us
  Pallas kernels: 255 us -> 249 us
  starting transfers between devices: 7.92 us -> 4.38 us
    all_to_all x2 -> x1, waiting for transfers between devices: 35.6 us -> 0.01 us  [to_field(): return lax.all_to_all(part, 'blk', 0, 1, tiled=True)[0]]
    all_to_all x1, blocking collectives: 11.7 us -> 43.4 us  [to_field(): return lax.all_to_all(part, 'blk', 0, 1, tiled=True)[0]]
    pallas_call x1, Pallas kernels: 205 us -> 183 us  [mega(): pl.pallas_call(partial(mega_kernel, fields, blk, rows, ff_steps, pairs, t...]
    pallas_call x1 -> x3, Pallas kernels: 13 us -> 30.1 us  [the longest x1 15.7 us: widen(): pl.pallas_call(kernel, grid=(steps,), in_specs=specs, out_specs=specs, ou...]
    convert_element_type x6 -> x0, other arithmetic: 17.1 us -> none  [the longest x1 7.52 us: per_device(): d_up.astype(F32)]
    broadcast_in_dim x9 -> x0, local copies, waits for them, and re-layouts: 5.26 us -> none  [the longest x1 0.61 us: mega(): up_bias[None]]
    all_to_all x2 -> x1, starting transfers between devices: 7.92 us -> 4.38 us  [to_field(): return lax.all_to_all(part, 'blk', 0, 1, tiled=True)[0]]
  transfers between devices with their start and end apart: 2 -> 1, of which waited for: 1 -> 0; matrix products, arithmetic and copies ran while one was open for 3% -> 0% of each run, Pallas kernels for 14% -> 15%
where the time goes in v4:
time: 304 us; the launch traced here: 303 us
  Pallas kernels  249 us (82%)
  blocking collectives  43.4 us (14%)
  local copies, waits for them, and re-layouts  5.83 us (2%)
  starting transfers between devices  4.38 us (1%)
    pallas_call x1, Pallas kernels, mega(): pl.pallas_call(partial(mega_kernel, fields, blk, rows, ff_steps, pairs, t...  183 us
    all_to_all x1, blocking collectives, to_field(): return lax.all_to_all(part, 'blk', 0, 1, tiled=True)[0]  43.4 us
    pallas_call x1, Pallas kernels, attend(): pl.pallas_call(partial(attend_kernel, block), grid=(pairs,), in_specs=[pl...  36.6 us
    pallas_call x1, Pallas kernels, widen(): pl.pallas_call(kernel, grid=(steps,), in_specs=specs, out_specs=specs, ou...  15.7 us
    pallas_call x1, Pallas kernels, project(): pl.pallas_call(project_kernel, grid=(slots // block,), in_specs=[nat, one...  8.9 us
  transfers between devices with their start and end apart: 1, of which 0 were waited for; matrix products, arithmetic and copies ran while one was open for 0% of the time, Pallas kernels for 15%

profile of v4, /device:TPU:0, one launch (start us, length us, event | category | flops | bytes accessed | tf_op | source)
XLA Modules:
  0.0 303.5 jit_solution(3205230030100311450)
XLA Ops:
  0.6 5.5 %place.1 = bf16[4,256,768]{2,1,0:T(8,128)(2,1)} custom-call(bf16[4,256,768]{2,1,0:T(8,128)(2,1)} %tok.1, s32[4,256]{1,0:T(4,128)} %keep.1, f32[32,384]{1,0:T(8,128)} %constant.4.clone.row_table, f32[64,384]{1,0:T(8,128)} %constant.5.clone.col_table), custom_call_target="tpu_custom_call" | custom-call | tf_op jit(solution)/shard_map/place/pallas_call | solution.py:84
  6.2 43.4 %all_to_all.8 = bf16[4,256,768]{2,1,0:T(8,128)(2,1)} all-to-all(bf16[4,256,768]{2,1,0:T(8,128)(2,1)} %place.1), channel_id=1, replica_groups=mesh['fields'=8,'blk'=4] {'blk'}, dimensions={0} | all-to-all | bytes 3145728 | tf_op jit(solution)/shard_map/all_to_all | solution.py:744
  49.5 4.4 %all-to-all-start.1 = ((bf16[4,256,768]{2,1,0:T(8,128)(2,1)}), bf16[4,256,768]{2,1,0:T(8,128)(2,1)}, u32[]{:S(2)}, u32[]{:S(2)}) async-start(bf16[4,256,768]{2,1,0:T(8,128)(2,1)} %param.35), calls=%async_computation.1 | async-start | bytes 3145728 | tf_op jit(solution)/shard_map/all_to_all | solution.py:744
  53.9 8.9 %project.1 = (bf16[768,1024]{1,0:T(8,128)(2,1)}, bf16[768,1024]{1,0:T(8,128)(2,1)}, bf16[1024,768]{1,0:T(8,128)(2,1)}, bf16[768,1024]{1,0:T(8,128)(2,1)}, bf16[1...) custom-call(bf16[1024,768]{1,0:T(8,128)(2,1)} %bitcast.20, bf16[768]{0:T(1024)(128)(2,1)} %gain_one.1, ...), custom_call_target="tpu_custom_call" | custom-call | flops 3623878656 | bytes 15728640 | tf_op jit(solution)/shard_map/project/pallas_call | solution.py:116
  62.8 36.6 %attend.1 = (bf16[1024,768]{1,0:T(8,128)(2,1)}, bf16[768,1024]{1,0:T(8,128)(2,1)}, f32[6,2,1024]{2,1,0:T(2,128)}) custom-call(s32[4]{0:T(128)} %count.3, bf16[768,1024]{1,0:T(8,128)(2,1)} %get-tuple-element.34.qt, bf16[1024,768]{1,0:T(8,128)(2,1)} %get-tuple-element.35.k, bf16[768,1024]{1,0:T(8,128)(2,1)} %get-tuple-element.36.vt), custom_call_target="tpu_custom_call" | custom-call | flops 12884901888 | bytes 9437184 | tf_op jit(solution)/shard_map/attend/pallas_call | solution.py:175
  99.4 0.0 all-to-all-done.1
  99.4 182.5 %mega.1 = (bf16[4,256,768]{2,1,0:T(8,128)(2,1)}, bf16[4,256,768]{2,1,0:T(8,128)(2,1)}, bf16[768,3072]{1,0:T(8,128)(2,1)}, bf16[3072,768]{1,0:T(8,128)(2,1)}, bf1...) custom-call(s32[4]{0:T(128)} %count.3, bf16[768,1024]{1,0:T(8,128)(2,1)} %get-tuple-element.37.ot, ...), custom_call_target="tpu_custom_call" | custom-call | flops 44291850240 | bytes 47185920 | tf_op jit(solution)/shard_map/mega/pallas_call | solution.py:657
  281.9 1.4 slice_bitcast_fusion.1
  283.3 1.3 slice_bitcast_fusion
  284.6 0.0 copy-start.1
  284.6 15.7 %widen.1 = (f32[768,3072]{1,0:T(8,128)}, f32[3072,768]{1,0:T(8,128)}, f32[768,2304]{1,0:T(8,128)}, f32[768,768]{1,0:T(8,128)}) custom-call(bf16[768,3072]{1,0:T(8,128)(2,1)} %get-tuple-element.45.refs_0_, bf16[3072,768]{1,0:T(8,128)(2,1)} %get-tuple-element.46.refs_1_, bf16[768,2304]{1,0:T(8,128)(2,1)} %get-tuple-element.47.refs_2_, ...), custom_call_target="tpu_custom_call" | custom-call | tf_op jit(solution)/shard_map/widen/pallas_call | solution.py:732
  300.4 0.0 copy-done.1
  300.4 0.0 copy-start
  300.4 1.1 copy.36
  301.5 0.8 copy-done
  302.3 1.1 copy.37
Async XLA Ops:
  49.5 49.8 %all-to-all-start.1 = ((bf16[4,256,768]{2,1,0:T(8,128)(2,1)}), bf16[4,256,768]{2,1,0:T(8,128)(2,1)}, u32[]{:S(2)}, u32[]{:S(2)}) async-start(bf16[4,256,768]{2,1,0:T(8,128)(2,1)} %param.35), calls=%async_computation.1 | async-start | bytes 3145728 | tf_op jit(solution)/shard_map/all_to_all | solution.py:744
  284.6 15.7 %copy-start.1 = (bf16[4,256,768]{2,1,0:T(8,128)(2,1)S(1)}, bf16[4,256,768]{2,1,0:T(8,128)(2,1)}, u32[]{:S(2)}) copy-start(bf16[4,256,768]{2,1,0:T(8,128)(2,1)} %get-tuple-element.76) | copy-start | bytes 4718596
  300.4 2.0 copy-start

commit v5 on v4

--- a/solution.py
+++ b/solution.py
@@ -150,24 +150,32 @@
     extra_row = jnp.where(sub == 0, 1.0, 0.0).astype(BF16)
     subv = lax.broadcasted_iota(jnp.int32, (16, slots), 0)
     ones = jnp.where(subv == 0, 1.0, 0.0).astype(BF16)
+    work = []
     for head in range(2):
         ka = augment_cols(k[...], extra_col, head == 1)
         va = jnp.concatenate([vt[head * HEAD_DIM : (head + 1) * HEAD_DIM, :], ones], 0)
         for i in range(slots // block):
-            cols = slice(i * block, (i + 1) * block)
-            qa = augment_rows(qt[:, cols], extra_row, head == 1)
-            s = mm(ka, qa, 1, 0)
-            top = jnp.max(s, 0, keepdims=True)
-            p = jnp.exp2((s - top) * c).astype(BF16)
-            r = mm(va, p, 1, 0)
-            total = r[HEAD_DIM : HEAD_DIM + 1]
-            mixed = (r[:HEAD_DIM] / total).astype(BF16)
-            ot[head * HEAD_DIM : (head + 1) * HEAD_DIM, cols] = mixed
-            lse[0, head : head + 1, cols] = top * HEAD_DIM**-0.5 + jnp.log(total)
+            work.append((head, ka, va, slice(i * block, (i + 1) * block)))
+
+    def scores(item):
+        head, ka, _, cols = item
+        return mm(ka, augment_rows(qt[:, cols], extra_row, head == 1), 1, 0)
+
+    s = scores(work[0])
+    for n, (head, _, va, cols) in enumerate(work):
+        later = scores(work[n + 1]) if n + 1 < len(work) else None
+        top = jnp.max(s, 0, keepdims=True)
+        p = jnp.exp2((s - top) * c).astype(BF16)
+        r = mm(va, p, 1, 0)
+        total = r[HEAD_DIM : HEAD_DIM + 1]
+        mixed = (r[:HEAD_DIM] / total).astype(BF16)
+        ot[head * HEAD_DIM : (head + 1) * HEAD_DIM, cols] = mixed
+        lse[0, head : head + 1, cols] = top * HEAD_DIM**-0.5 + jnp.log(total)
+        s = later
     o[...] = ot[...].T
 
 
-def attend(count, qt, k, vt, block=256):
+def attend(count, qt, k, vt, block=512):
     slots, width = k.shape
     pairs = width // (2 * HEAD_DIM)
     tra = pl.BlockSpec((2 * HEAD_DIM, slots), lambda j: (j, 0))
@@ -422,21 +430,28 @@
 
     @pl.when(step < heads_from)
     def _():
-        h = jnp.dot(a2[...], up[...], preferred_element_type=F32) + row(up_bias)
-        phi = 0.5 + 0.5 * lax.erf(h * (0.5**0.5))
-        slope = phi + h * (jnp.exp2(h * h * (-0.5 * LOG2E)) * (2 * math.pi) ** -0.5)
-        g = (h * phi).astype(BF16)
-        dg = mm(y[...], down[...], 1, 1)
-        dh = (dg * slope).astype(BF16)
-        sum_up = jnp.sum(dh.astype(F32), 0, keepdims=True)
+        half = slots // 2
+        parts = [slice(0, half), slice(half, slots)]
+        ahead = []
+        for at in parts:
+            h = jnp.dot(a2[at, :], up[...], preferred_element_type=F32) + row(up_bias)
+            ahead.append((h, mm(y[at, :], down[...], 1, 1)))
+        sum_up = d_up = d_down = 0.0
+        for at, (h, dg) in zip(parts, ahead):
+            phi = 0.5 + 0.5 * lax.erf(h * (0.5**0.5))
+            slope = phi + h * (jnp.exp2(h * h * (-0.5 * LOG2E)) * (2 * math.pi) ** -0.5)
+            g = (h * phi).astype(BF16)
+            dh = (dg * slope).astype(BF16)
+            acc[at, :] += jnp.dot(g, down[...], preferred_element_type=F32)
+            dacc[at, :] += mm(dh, up[...], 1, 1)
+            sum_up = sum_up + jnp.sum(dh.astype(F32), 0, keepdims=True)
+            d_up = d_up + jnp.dot(a2t[:, at], dh, preferred_element_type=F32)
+            d_down = d_down + jnp.dot(g.T, y[at, :], preferred_element_type=F32)
+        d_up, d_down = d_up.astype(BF16), d_down.astype(BF16)
         for i in range(ff // LANES):
             vec[pl.ds(VEC_UP * cols_of + step * (ff // LANES) + i, 1), :] = sum_up[:, i * LANES : (i + 1) * LANES]
-        acc[...] += jnp.dot(g, down[...], preferred_element_type=F32)
-        dacc[...] += mm(dh, up[...], 1, 1)
-        d_up = jnp.dot(a2t[...], dh, preferred_element_type=F32).astype(BF16)
         for i in range(ff // LANES):
             grads[2 * step, i * width : (i + 1) * width, :] = d_up[:, i * LANES : (i + 1) * LANES]
-        d_down = jnp.dot(g.T, y[...], preferred_element_type=F32).astype(BF16)
         for i in range(cols_of):
             grads[2 * step + 1, i * ff : (i + 1) * ff, :] = d_down[:, i * LANES : (i + 1) * LANES]
         if 2 * width < rows:
@@ -504,10 +519,16 @@
         upper = lax.broadcasted_iota(jnp.int32, (pair, slots), 0) // HEAD_DIM == head
         qa = jnp.where(upper, jnp.concatenate([q_h, q_h], 0), jnp.concatenate([extra_q, extra_q], 0))
         da = jnp.where(upper, jnp.concatenate([do_h, do_h], 0), jnp.concatenate([extra_d, extra_d], 0))
+        def scores(i):
+            at = slice(i * block, (i + 1) * block)
+            return mm(ka, qa[:, at], 1, 0), mm(va, da[:, at], 1, 0)
+
+        ready = scores(0)
         for i in range(slots // block):
             at = slice(i * block, (i + 1) * block)
-            s = mm(ka, qa[:, at], 1, 0)
-            dp = mm(va, da[:, at], 1, 0)
+            s, dp = ready
+            if i + 1 < slots // block:
+                ready = scores(i + 1)
             p = jnp.exp2(s * c)
             ds = (p * dp).astype(BF16)
             p = p.astype(BF16)

time: 304 us -> 292 us (0.961)
  Pallas kernels: 249 us -> 230 us
  waiting for transfers between devices: 0.01 us -> 6.6 us
    pallas_call x1, Pallas kernels: 36.6 us -> 20.7 us  [attend(): pl.pallas_call(partial(attend_kernel, block), grid=(pairs,), in_specs=[pl...]
    all_to_all x1, waiting for transfers between devices: 0.01 us -> 6.6 us  [to_field(): return lax.all_to_all(part, 'blk', 0, 1, tiled=True)[0]]
    pallas_call x1, Pallas kernels: 183 us -> 179 us  [mega(): pl.pallas_call(partial(mega_kernel, fields, blk, rows, ff_steps, pairs, t...]
  transfers between devices with their start and end apart: 1 -> 1, of which waited for: 0 -> 1; matrix products, arithmetic and copies ran while one was open for 0% -> 0% of each run, Pallas kernels for 15% -> 10%
where the time goes in v5:
time: 292 us; the launch traced here: 291 us
  Pallas kernels  230 us (79%)
  blocking collectives  43.4 us (15%)
  waiting for transfers between devices  6.6 us (2%)
  local copies, waits for them, and re-layouts  5.83 us (2%)
  starting transfers between devices  4.38 us (2%)
    pallas_call x1, Pallas kernels, mega(): pl.pallas_call(partial(mega_kernel, fields, blk, rows, ff_steps, pairs, t...  179 us
    all_to_all x1, blocking collectives, to_field(): return lax.all_to_all(part, 'blk', 0, 1, tiled=True)[0]  43.4 us
    pallas_call x1, Pallas kernels, attend(): pl.pallas_call(partial(attend_kernel, block), grid=(pairs,), in_specs=[pl...  20.7 us
    pallas_call x1, Pallas kernels, widen(): pl.pallas_call(kernel, grid=(steps,), in_specs=specs, out_specs=specs, ou...  15.7 us
    pallas_call x1, Pallas kernels, project(): pl.pallas_call(project_kernel, grid=(slots // block,), in_specs=[nat, one...  8.9 us
    all_to_all x1, waiting for transfers between devices, to_field(): return lax.all_to_all(part, 'blk', 0, 1, tiled=True)[0]  6.6 us
  transfers between devices with their start and end apart: 1, of which 1 were waited for; matrix products, arithmetic and copies ran while one was open for 0% of the time, Pallas kernels for 10%

profile of v5, /device:TPU:0, one launch (start us, length us, event | category | flops | bytes accessed | tf_op | source)
XLA Modules:
  0.0 290.9 jit_solution(9788226216681369831)
XLA Ops:
  0.6 5.5 %place.1 = bf16[4,256,768]{2,1,0:T(8,128)(2,1)} custom-call(bf16[4,256,768]{2,1,0:T(8,128)(2,1)} %tok.1, s32[4,256]{1,0:T(4,128)} %keep.1, f32[32,384]{1,0:T(8,128)} %constant.4.clone.row_table, f32[64,384]{1,0:T(8,128)} %constant.5.clone.col_table), custom_call_target="tpu_custom_call" | custom-call | tf_op jit(solution)/shard_map/place/pallas_call | solution.py:84
  6.2 43.4 %all_to_all.8 = bf16[4,256,768]{2,1,0:T(8,128)(2,1)} all-to-all(bf16[4,256,768]{2,1,0:T(8,128)(2,1)} %place.1), channel_id=1, replica_groups=mesh['fields'=8,'blk'=4] {'blk'}, dimensions={0} | all-to-all | bytes 3145728 | tf_op jit(solution)/shard_map/all_to_all | solution.py:765
  49.5 4.4 %all-to-all-start.1 = ((bf16[4,256,768]{2,1,0:T(8,128)(2,1)}), bf16[4,256,768]{2,1,0:T(8,128)(2,1)}, u32[]{:S(2)}, u32[]{:S(2)}) async-start(bf16[4,256,768]{2,1,0:T(8,128)(2,1)} %param.35), calls=%async_computation.1 | async-start | bytes 3145728 | tf_op jit(solution)/shard_map/all_to_all | solution.py:765
  53.9 8.9 %project.1 = (bf16[768,1024]{1,0:T(8,128)(2,1)}, bf16[768,1024]{1,0:T(8,128)(2,1)}, bf16[1024,768]{1,0:T(8,128)(2,1)}, bf16[768,1024]{1,0:T(8,128)(2,1)}, bf16[1...) custom-call(bf16[1024,768]{1,0:T(8,128)(2,1)} %bitcast.20, bf16[768]{0:T(1024)(128)(2,1)} %gain_one.1, ...), custom_call_target="tpu_custom_call" | custom-call | flops 3623878656 | bytes 15728640 | tf_op jit(solution)/shard_map/project/pallas_call | solution.py:116
  62.8 20.7 %attend.1 = (bf16[1024,768]{1,0:T(8,128)(2,1)}, bf16[768,1024]{1,0:T(8,128)(2,1)}, f32[6,2,1024]{2,1,0:T(2,128)}) custom-call(s32[4]{0:T(128)} %count.3, bf16[768,1024]{1,0:T(8,128)(2,1)} %get-tuple-element.34.qt, bf16[1024,768]{1,0:T(8,128)(2,1)} %get-tuple-element.35.k, bf16[768,1024]{1,0:T(8,128)(2,1)} %get-tuple-element.36.vt), custom_call_target="tpu_custom_call" | custom-call | flops 12884901888 | bytes 9437184 | tf_op jit(solution)/shard_map/attend/pallas_call | solution.py:183
  83.5 6.6 %all-to-all-done.1 = bf16[4,256,768]{2,1,0:T(8,128)(2,1)} async-done(((bf16[4,256,768]{2,1,0:T(8,128)(2,1)}), bf16[4,256,768]{2,1,0:T(8,128)(2,1)}, u32[]{:S(2)}, u32[]{:S(2)}) %all-to-all-start.1) | async-done | bytes 1572896 | tf_op jit(solution)/shard_map/all_to_all | solution.py:765
  90.1 179.2 %mega.1 = (bf16[4,256,768]{2,1,0:T(8,128)(2,1)}, bf16[4,256,768]{2,1,0:T(8,128)(2,1)}, bf16[768,3072]{1,0:T(8,128)(2,1)}, bf16[3072,768]{1,0:T(8,128)(2,1)}, bf1...) custom-call(s32[4]{0:T(128)} %count.3, bf16[768,1024]{1,0:T(8,128)(2,1)} %get-tuple-element.37.ot, ...), custom_call_target="tpu_custom_call" | custom-call | flops 44291850240 | bytes 47185920 | tf_op jit(solution)/shard_map/mega/pallas_call | solution.py:678
  269.3 1.4 slice_bitcast_fusion.1
  270.7 1.3 slice_bitcast_fusion
  272.0 0.0 copy-start.1
  272.0 15.7 %widen.1 = (f32[768,3072]{1,0:T(8,128)}, f32[3072,768]{1,0:T(8,128)}, f32[768,2304]{1,0:T(8,128)}, f32[768,768]{1,0:T(8,128)}) custom-call(bf16[768,3072]{1,0:T(8,128)(2,1)} %get-tuple-element.45.refs_0_, bf16[3072,768]{1,0:T(8,128)(2,1)} %get-tuple-element.46.refs_1_, bf16[768,2304]{1,0:T(8,128)(2,1)} %get-tuple-element.47.refs_2_, ...), custom_call_target="tpu_custom_call" | custom-call | tf_op jit(solution)/shard_map/widen/pallas_call | solution.py:753
  287.7 0.0 copy-done.1
  287.7 0.0 copy-start
  287.8 1.1 copy.36
  288.9 0.8 copy-done
  289.7 1.1 copy.37
Async XLA Ops:
  49.5 40.5 %all-to-all-start.1 = ((bf16[4,256,768]{2,1,0:T(8,128)(2,1)}), bf16[4,256,768]{2,1,0:T(8,128)(2,1)}, u32[]{:S(2)}, u32[]{:S(2)}) async-start(bf16[4,256,768]{2,1,0:T(8,128)(2,1)} %param.35), calls=%async_computation.1 | async-start | bytes 3145728 | tf_op jit(solution)/shard_map/all_to_all | solution.py:765
  272.0 15.7 %copy-start.1 = (bf16[4,256,768]{2,1,0:T(8,128)(2,1)S(1)}, bf16[4,256,768]{2,1,0:T(8,128)(2,1)}, u32[]{:S(2)}) copy-start(bf16[4,256,768]{2,1,0:T(8,128)(2,1)} %get-tuple-element.76) | copy-start | bytes 4718596
  287.7 2.0 copy-start

commit v6 on v5

--- a/solution.py
+++ b/solution.py
@@ -2,6 +2,7 @@
 import math
 import jax
 import jax.numpy as jnp
+import ml_dtypes
 import numpy as np
 from jax import lax
 from jax.experimental import pallas as pl
@@ -62,33 +63,80 @@
 
     def table(length):
         ang = np.arange(length)[:, None] * omega
-        return jnp.asarray(np.concatenate([np.sin(ang), np.cos(ang)], -1), F32)
+        rest = np.concatenate([np.sin(ang), np.cos(ang)], -1).astype(np.float32)
+        parts = []
+        for _ in range(3):
+            parts.append(rest.astype(ml_dtypes.bfloat16))
+            rest = rest - parts[-1].astype(np.float32)
+        return jnp.asarray(np.concatenate(parts, 0))
 
     return table(PATCHES // GRID_W), table(GRID_W)
 
 
-def place_kernel(tok, keep, row_table, col_table, x0):
+def place_kernel(blk, tok, keep, row_table, col_table, x0, placed, sems):
     slots = tok.shape[1]
-    patch = keep[pl.ds(pl.program_id(0), 1), :]
-    parts = []
-    for table, of in ((row_table, lax.div(patch, GRID_W)), (col_table, lax.rem(patch, GRID_W))):
-        hot = (lax.broadcasted_iota(jnp.int32, (table.shape[0], slots), 0) == of).astype(F32)
-        parts.append(jnp.dot(hot.T, table[...], precision=lax.Precision.HIGHEST, preferred_element_type=F32))
-    x0[0] = (tok[0].astype(F32) + jnp.concatenate(parts, -1)).astype(BF16)
-
-
-def place(tokens, keep):
+    f, z = lax.axis_index("fields"), lax.axis_index("blk")
+    barrier = pltpu.get_barrier_semaphore()
+    for s in range(1, blk):
+        pl.semaphore_signal(barrier, 1, device_id=(f, lax.rem(z + s, blk)), device_id_type=pl.DeviceIdType.MESH)
+    pl.semaphore_wait(barrier, blk - 1)
+
+    def copy(s):
+        to = lax.rem(z + s, blk)
+        return pltpu.make_async_remote_copy(
+            src_ref=placed.at[to],
+            dst_ref=x0.at[z],
+            send_sem=sems.at[0, s],
+            recv_sem=sems.at[1, s],
+            device_id=(f, to),
+            device_id_type=pl.DeviceIdType.MESH,
+        )
+
+    def came(s):
+        source = lax.rem(z + blk - s, blk)
+        return pltpu.make_async_remote_copy(
+            src_ref=placed.at[source],
+            dst_ref=x0.at[source],
+            send_sem=sems.at[0, s],
+            recv_sem=sems.at[1, s],
+            device_id=(f, source),
+            device_id_type=pl.DeviceIdType.MESH,
+        )
+
+    for s in range(blk - 1, -1, -1):
+        to = lax.rem(z + s, blk)
+        patch = keep[pl.ds(to, 1), :]
+        parts = []
+        for table, of in ((row_table, lax.div(patch, GRID_W)), (col_table, lax.rem(patch, GRID_W))):
+            size = table.shape[0] // 3
+            index = lax.broadcasted_iota(jnp.int32, (size, slots), 0)
+            hot = jnp.where(index == of, 1.0, 0.0).astype(BF16)
+            hot = jnp.concatenate([hot, hot, hot], 0).T
+            parts.append(jnp.dot(hot, table[...], preferred_element_type=F32))
+        here = (tok[to].astype(F32) + jnp.concatenate(parts, -1)).astype(BF16)
+        if s > 0:
+            placed[to] = here
+            copy(s).start()
+        else:
+            x0[z] = here
+    for s in range(blk - 1, 0, -1):
+        copy(s).wait_send()
+        came(s).wait_recv()
+
+
+def place(blk, tokens, keep):
     fields, slots, width = tokens.shape
     row_table, col_table = tables(width)
-    block = pl.BlockSpec((1, slots, width), lambda i: (i, 0, 0))
+    vmem = pl.BlockSpec(memory_space=pltpu.VMEM)
     return pl.pallas_call(
-        place_kernel,
-        grid=(fields,),
-        in_specs=[block, whole((fields, slots)), whole(row_table.shape), whole(col_table.shape)],
-        out_specs=block,
+        partial(place_kernel, blk),
+        in_specs=[vmem] * 4,
+        out_specs=vmem,
         out_shape=jax.ShapeDtypeStruct(tokens.shape, BF16),
+        scratch_shapes=[pltpu.VMEM(tokens.shape, BF16), pltpu.SemaphoreType.DMA((2, blk))],
+        compiler_params=pltpu.CompilerParams(collective_id=1, has_side_effects=True),
         name="place",
-    )(tokens, keep, row_table, col_table)
+    )(tokens, keep, row_table, col_table).reshape(fields * slots, width)
 
 
 def project_kernel(x0, gain, bias, weight, qb, vb, a1t, qt, k, kt, v, vt):
@@ -744,21 +792,34 @@
     )
 
 
-def widen(arrays, steps):
+def widen(arrays, vecs, lengths, steps):
+    count = len(arrays)
+
     def kernel(*refs):
-        for src, dst in zip(refs[: len(arrays)], refs[len(arrays) :]):
+        for src, dst in zip(refs[:count], refs[count + 1 : 2 * count + 1]):
             dst[...] = src[...].astype(F32)
+
+        @pl.when(pl.program_id(0) == 0)
+        def _():
+            at = 0
+            for dst, length in zip(refs[2 * count + 1 :], lengths):
+                for i in range(length // LANES):
+                    dst[i * LANES : (i + 1) * LANES] = refs[count][at + i, :]
+                at += length // LANES
 
     specs = [pl.BlockSpec((a.shape[0] // steps, a.shape[1]), lambda i: (i, 0)) for a in arrays]
     return pl.pallas_call(
         kernel,
         grid=(steps,),
-        in_specs=specs,
-        out_specs=specs,
-        out_shape=[jax.ShapeDtypeStruct(a.shape, F32) for a in arrays],
+        in_specs=[*specs, whole(vecs.shape)],
+        out_specs=[*specs, *[whole((n,)) for n in lengths]],
+        out_shape=[
+            *[jax.ShapeDtypeStruct(a.shape, F32) for a in arrays],
+            *[jax.ShapeDtypeStruct((n,), F32) for n in lengths],
+        ],
         compiler_params=pltpu.CompilerParams(vmem_limit_bytes=VMEM_BYTES),
         name="widen",
-    )(*arrays)
+    )(*arrays, vecs)
 
 
 def to_field(part):
@@ -770,16 +831,17 @@
     out_bias, norm2_gain, norm2_bias, up_weight, up_bias, down_weight, down_bias, cotangent,
 ):
     width = tokens.shape[2]
-    x0 = to_field(place(tokens, keep_index))
+    x0 = place(mesh_shape[1], tokens, keep_index)
     a1t, qt, k, kt, v, vt = project(x0, norm1_gain, norm1_bias, qkv_weight, query_bias, value_bias)
-    y = to_field(cotangent)
+    _, later = lax.optimization_barrier((x0, cotangent))
+    y = to_field(later)
     _, ot, lse = attend(counts, qt, k, vt)
     output, input_grad, d_up, d_down, d_qkv, d_out, vecs = mega(
         mesh_shape, counts, ot, x0, y, out_weight, out_bias, norm2_gain, norm2_bias, up_weight, up_bias, down_weight,
         down_bias, qt, k, kt, v, lse, a1t, qkv_weight, norm1_gain,
     )
-    d_up, d_down, d_qkv, d_out = widen((d_up, d_down, d_qkv, d_out), 12)
-    vec = vecs.reshape(-1, width)
+    lengths = [width] * 8 + [up_weight.shape[1]]
+    d_up, d_down, d_qkv, d_out, *vec = widen((d_up, d_down, d_qkv, d_out), vecs, lengths, 6)
     return (
         output,
         input_grad,
@@ -793,7 +855,7 @@
         vec[5],
         vec[6],
         d_up,
-        vec[8:].reshape(-1),
+        vec[8],
         d_down,
         vec[7],
     )

time: 292 us -> 282 us (0.966)
  blocking collectives: 43.4 us -> 0 us
  Pallas kernels: 230 us -> 266 us
    all_to_all x1 -> x0, blocking collectives: 43.4 us -> none  [to_field(): return lax.all_to_all(part, 'blk', 0, 1, tiled=True)[0]]
    pallas_call x2, Pallas kernels: 21.2 us -> 58.3 us  [the longest x1 42.8 us: place(): pl.pallas_call(partial(place_kernel, blk), in_specs=[vmem] * 4, out_specs...]
where the time goes in v6:
time: 282 us
  Pallas kernels  266 us (94%)
  waiting for transfers between devices  6.98 us (2%)
  starting transfers between devices  4.4 us (2%)
  local copies, waits for them, and re-layouts  3.11 us (1%)
    pallas_call x1, Pallas kernels, mega(): pl.pallas_call(partial(mega_kernel, fields, blk, rows, ff_steps, pairs, t...  179 us
    pallas_call x1, Pallas kernels, place(): pl.pallas_call(partial(place_kernel, blk), in_specs=[vmem] * 4, out_specs...  42.8 us
    pallas_call x1, Pallas kernels, attend(): pl.pallas_call(partial(attend_kernel, block), grid=(pairs,), in_specs=[pl...  20.5 us
    pallas_call x1, Pallas kernels, widen(): pl.pallas_call(kernel, grid=(steps,), in_specs=[*specs, whole(vecs.shape)...  15.6 us
    pallas_call x1, Pallas kernels, project(): pl.pallas_call(project_kernel, grid=(slots // block,), in_specs=[nat, one...  8.89 us
    all_to_all x1, waiting for transfers between devices, to_field(): return lax.all_to_all(part, 'blk', 0, 1, tiled=True)[0]  6.98 us
  transfers between devices with their start and end apart: 1, of which 1 were waited for; matrix products, arithmetic and copies ran while one was open for 0% of the time, Pallas kernels for 10%

profile of v6, /device:TPU:0, one launch (start us, length us, event | category | flops | bytes accessed | tf_op | source)
XLA Modules:
  0.0 281.7 jit_solution(9396743856295859385)
XLA Ops:
  0.6 42.8 %place.1 = bf16[4,256,768]{2,1,0:T(8,128)(2,1)} custom-call(bf16[4,256,768]{2,1,0:T(8,128)(2,1)} %tok.1, s32[4,256]{1,0:T(4,128)} %keep.1, bf16[96,384]{1,0:T(8,128)(2,1)} %constant.4.clone.row_table, bf16[192,384]{1,0:T(8,128)(2,1)} %constant.5.clone.col_table), custom_call_target="tpu_custom_call" | custom-call | tf_op jit(solution)/shard_map/place/pallas_call | solution.py:131
  43.4 4.4 %all-to-all-start = ((bf16[4,256,768]{2,1,0:T(8,128)(2,1)}), bf16[4,256,768]{2,1,0:T(8,128)(2,1)}, u32[]{:S(2)}, u32[]{:S(2)}) async-start(bf16[4,256,768]{2,1,0:T(8,128)(2,1)} %param.35), calls=%async_computation | async-start | bytes 3145728 | tf_op jit(solution)/shard_map/all_to_all | solution.py:826
  47.8 8.9 %project.1 = (bf16[768,1024]{1,0:T(8,128)(2,1)}, bf16[768,1024]{1,0:T(8,128)(2,1)}, bf16[1024,768]{1,0:T(8,128)(2,1)}, bf16[768,1024]{1,0:T(8,128)(2,1)}, bf16[1...) custom-call(bf16[1024,768]{1,0:T(8,128)(2,1)} %bitcast.2, bf16[768]{0:T(1024)(128)(2,1)} %gain_one.1, bf16[768]{0:T(1024)(128)(2,1)} %bias.1, ...), custom_call_target="tpu_custom_call" | custom-call | flops 3623878656 | bytes 15728640 | tf_op jit(solution)/shard_map/project/pallas_call | solution.py:164
  56.7 20.5 %attend.1 = (bf16[1024,768]{1,0:T(8,128)(2,1)}, bf16[768,1024]{1,0:T(8,128)(2,1)}, f32[6,2,1024]{2,1,0:T(2,128)}) custom-call(s32[4]{0:T(128)} %count.3, bf16[768,1024]{1,0:T(8,128)(2,1)} %get-tuple-element.44.qt, bf16[1024,768]{1,0:T(8,128)(2,1)} %get-tuple-element.45.k, bf16[768,1024]{1,0:T(8,128)(2,1)} %get-tuple-element.46.vt), custom_call_target="tpu_custom_call" | custom-call | flops 12884901888 | bytes 9437184 | tf_op jit(solution)/shard_map/attend/pallas_call | solution.py:231
  77.3 7.0 %all-to-all-done = bf16[4,256,768]{2,1,0:T(8,128)(2,1)} async-done(((bf16[4,256,768]{2,1,0:T(8,128)(2,1)}), bf16[4,256,768]{2,1,0:T(8,128)(2,1)}, u32[]{:S(2)}, u32[]{:S(2)}) %all-to-all-start) | async-done | bytes 1572896 | tf_op jit(solution)/shard_map/all_to_all | solution.py:826
  84.2 178.7 %mega.1 = (bf16[4,256,768]{2,1,0:T(8,128)(2,1)}, bf16[4,256,768]{2,1,0:T(8,128)(2,1)}, bf16[768,3072]{1,0:T(8,128)(2,1)}, bf16[3072,768]{1,0:T(8,128)(2,1)}, bf1...) custom-call(s32[4]{0:T(128)} %count.3, bf16[768,1024]{1,0:T(8,128)(2,1)} %get-tuple-element.47.ot, ...), custom_call_target="tpu_custom_call" | custom-call | flops 44291850240 | bytes 47185920 | tf_op jit(solution)/shard_map/mega/pallas_call | solution.py:726
  263.0 0.0 copy-start.1
  263.0 15.6 %widen.1 = (f32[768,3072]{1,0:T(8,128)}, f32[3072,768]{1,0:T(8,128)}, f32[768,2304]{1,0:T(8,128)}, f32[768,768]{1,0:T(8,128)}, f32[768]{0:T(1024)}, /*index=5*/f...) custom-call(bf16[768,3072]{1,0:T(8,128)(2,1)} %get-tuple-element.55., ...), custom_call_target="tpu_custom_call" | custom-call | tf_op jit(solution)/shard_map/widen/pallas_call | solution.py:811
  278.5 0.0 copy-done.1
  278.5 0.0 copy-start
  278.6 1.1 copy.36
  279.7 0.8 copy-done
  280.5 1.1 copy.37
Async XLA Ops:
  43.4 40.8 %all-to-all-start = ((bf16[4,256,768]{2,1,0:T(8,128)(2,1)}), bf16[4,256,768]{2,1,0:T(8,128)(2,1)}, u32[]{:S(2)}, u32[]{:S(2)}) async-start(bf16[4,256,768]{2,1,0:T(8,128)(2,1)} %param.35), calls=%async_computation | async-start | bytes 3145728 | tf_op jit(solution)/shard_map/all_to_all | solution.py:826
  263.0 15.6 %copy-start.1 = (bf16[4,256,768]{2,1,0:T(8,128)(2,1)S(1)}, bf16[4,256,768]{2,1,0:T(8,128)(2,1)}, u32[]{:S(2)}) copy-start(bf16[4,256,768]{2,1,0:T(8,128)(2,1)} %get-tuple-element.88) | copy-start | bytes 4718596
  278.5 2.0 copy-start

commit v7 on v6

--- a/solution.py
+++ b/solution.py
@@ -244,9 +244,9 @@
     )(count, qt, k, vt)
 
 
-SLOTS_AHEAD = 8
+SLOTS_AHEAD = 10
 LANES = 128
-LAG_CORE, LAG_XY, LAG_Z = 2, 3, 3
+LAG_CORE, LAG_XY, LAG_Z = 2, 4, 4
 DIN_EVERY = 2
 
 

time: 282 us -> 282 us (level)
  no operation moved by 1% of the time
where the time goes in v7:
time: 282 us; the launch traced here: 281 us
  Pallas kernels  266 us (94%)
  waiting for transfers between devices  6.98 us (2%)
  starting transfers between devices  4.4 us (2%)
  local copies, waits for them, and re-layouts  3.11 us (1%)
    pallas_call x1, Pallas kernels, mega(): pl.pallas_call(partial(mega_kernel, fields, blk, rows, ff_steps, pairs, t...  178 us
    pallas_call x1, Pallas kernels, place(): pl.pallas_call(partial(place_kernel, blk), in_specs=[vmem] * 4, out_specs...  42.8 us
    pallas_call x1, Pallas kernels, attend(): pl.pallas_call(partial(attend_kernel, block), grid=(pairs,), in_specs=[pl...  20.5 us
    pallas_call x1, Pallas kernels, widen(): pl.pallas_call(kernel, grid=(steps,), in_specs=[*specs, whole(vecs.shape)...  15.6 us
    pallas_call x1, Pallas kernels, project(): pl.pallas_call(project_kernel, grid=(slots // block,), in_specs=[nat, one...  8.89 us
    all_to_all x1, waiting for transfers between devices, to_field(): return lax.all_to_all(part, 'blk', 0, 1, tiled=True)[0]  6.98 us
  transfers between devices with their start and end apart: 1, of which 1 were waited for; matrix products, arithmetic and copies ran while one was open for 0% of the time, Pallas kernels for 10%

profile of v7, /device:TPU:0, one launch (start us, length us, event | category | flops | bytes accessed | tf_op | source)
XLA Modules:
  0.0 281.0 jit_solution(118643107502027048)
XLA Ops:
  0.6 42.8 %place.1 = bf16[4,256,768]{2,1,0:T(8,128)(2,1)} custom-call(bf16[4,256,768]{2,1,0:T(8,128)(2,1)} %tok.1, s32[4,256]{1,0:T(4,128)} %keep.1, bf16[96,384]{1,0:T(8,128)(2,1)} %constant.4.clone.row_table, bf16[192,384]{1,0:T(8,128)(2,1)} %constant.5.clone.col_table), custom_call_target="tpu_custom_call" | custom-call | tf_op jit(solution)/shard_map/place/pallas_call | solution.py:131
  43.4 4.4 %all-to-all-start = ((bf16[4,256,768]{2,1,0:T(8,128)(2,1)}), bf16[4,256,768]{2,1,0:T(8,128)(2,1)}, u32[]{:S(2)}, u32[]{:S(2)}) async-start(bf16[4,256,768]{2,1,0:T(8,128)(2,1)} %param.35), calls=%async_computation | async-start | bytes 3145728 | tf_op jit(solution)/shard_map/all_to_all | solution.py:826
  47.8 8.9 %project.1 = (bf16[768,1024]{1,0:T(8,128)(2,1)}, bf16[768,1024]{1,0:T(8,128)(2,1)}, bf16[1024,768]{1,0:T(8,128)(2,1)}, bf16[768,1024]{1,0:T(8,128)(2,1)}, bf16[1...) custom-call(bf16[1024,768]{1,0:T(8,128)(2,1)} %bitcast.2, bf16[768]{0:T(1024)(128)(2,1)} %gain_one.1, bf16[768]{0:T(1024)(128)(2,1)} %bias.1, ...), custom_call_target="tpu_custom_call" | custom-call | flops 3623878656 | bytes 15728640 | tf_op jit(solution)/shard_map/project/pallas_call | solution.py:164
  56.7 20.5 %attend.1 = (bf16[1024,768]{1,0:T(8,128)(2,1)}, bf16[768,1024]{1,0:T(8,128)(2,1)}, f32[6,2,1024]{2,1,0:T(2,128)}) custom-call(s32[4]{0:T(128)} %count.3, bf16[768,1024]{1,0:T(8,128)(2,1)} %get-tuple-element.44.qt, bf16[1024,768]{1,0:T(8,128)(2,1)} %get-tuple-element.45.k, bf16[768,1024]{1,0:T(8,128)(2,1)} %get-tuple-element.46.vt), custom_call_target="tpu_custom_call" | custom-call | flops 12884901888 | bytes 9437184 | tf_op jit(solution)/shard_map/attend/pallas_call | solution.py:231
  77.3 7.0 %all-to-all-done = bf16[4,256,768]{2,1,0:T(8,128)(2,1)} async-done(((bf16[4,256,768]{2,1,0:T(8,128)(2,1)}), bf16[4,256,768]{2,1,0:T(8,128)(2,1)}, u32[]{:S(2)}, u32[]{:S(2)}) %all-to-all-start) | async-done | bytes 1572896 | tf_op jit(solution)/shard_map/all_to_all | solution.py:826
  84.2 178.0 %mega.1 = (bf16[4,256,768]{2,1,0:T(8,128)(2,1)}, bf16[4,256,768]{2,1,0:T(8,128)(2,1)}, bf16[768,3072]{1,0:T(8,128)(2,1)}, bf16[3072,768]{1,0:T(8,128)(2,1)}, bf1...) custom-call(s32[4]{0:T(128)} %count.3, bf16[768,1024]{1,0:T(8,128)(2,1)} %get-tuple-element.47.ot, ...), custom_call_target="tpu_custom_call" | custom-call | flops 44291850240 | bytes 47185920 | tf_op jit(solution)/shard_map/mega/pallas_call | solution.py:726
  262.3 0.0 copy-start.1
  262.3 15.6 %widen.1 = (f32[768,3072]{1,0:T(8,128)}, f32[3072,768]{1,0:T(8,128)}, f32[768,2304]{1,0:T(8,128)}, f32[768,768]{1,0:T(8,128)}, f32[768]{0:T(1024)}, /*index=5*/f...) custom-call(bf16[768,3072]{1,0:T(8,128)(2,1)} %get-tuple-element.55., ...), custom_call_target="tpu_custom_call" | custom-call | tf_op jit(solution)/shard_map/widen/pallas_call | solution.py:811
  277.9 0.0 copy-done.1
  277.9 0.0 copy-start
  277.9 1.1 copy.36
  279.0 0.8 copy-done
  279.9 1.1 copy.37
Async XLA Ops:
  43.4 40.8 %all-to-all-start = ((bf16[4,256,768]{2,1,0:T(8,128)(2,1)}), bf16[4,256,768]{2,1,0:T(8,128)(2,1)}, u32[]{:S(2)}, u32[]{:S(2)}) async-start(bf16[4,256,768]{2,1,0:T(8,128)(2,1)} %param.35), calls=%async_computation | async-start | bytes 3145728 | tf_op jit(solution)/shard_map/all_to_all | solution.py:826
  262.3 15.6 %copy-start.1 = (bf16[4,256,768]{2,1,0:T(8,128)(2,1)S(1)}, bf16[4,256,768]{2,1,0:T(8,128)(2,1)}, u32[]{:S(2)}) copy-start(bf16[4,256,768]{2,1,0:T(8,128)(2,1)} %get-tuple-element.88) | copy-start | bytes 4718596
  277.9 2.0 copy-start
